TPU v7x, 128 devices: a whole 4x4x4 slice. The times are simulated.
128 devices in a mesh: seq: 16 (over x, z), exp: 8 (over y, core).
Axes of the slice: x: 4, y: 4, z: 4, core: 2. Of those that a mesh axis runs over, the one named last changes fastest.
Arguments:
- tokens: bfloat16 [16384, 1536], P(('seq', 'exp')), may hold values from -6 to 6
- in_gain: float32 [1536], replicated, may hold values from 0.5 to 1.5
- in_z: bfloat16 [1536, 3072], P(None, 'exp'), may hold values from -0.15625 to 0.15625
- in_x: bfloat16 [1536, 3072], P(None, 'exp'), may hold values from -0.15625 to 0.15625
- in_bc: bfloat16 [1536, 256], replicated, may hold values from -0.15625 to 0.15625
- in_dt: bfloat16 [1536, 48], P(None, 'exp'), may hold values from -0.0390625 to 0.0390625
- conv_x: float32 [4, 3072], P(None, 'exp'), may hold values from -3 to 3
- conv_bc: float32 [4, 256], replicated, may hold values from -3 to 3
- dt_bias: float32 [48], P('exp'), may hold values from -7 to -2
- a_log: float32 [48], P('exp'), may hold values from -1 to 2.5
- d_skip: float32 [48], P('exp'), may hold values from 0.5 to 1.5
- norm_gain: float32 [3072], P('exp'), may hold values from 0.5 to 1.5
- out_w: bfloat16 [3072, 1536], P('exp'), may hold values from -0.109375 to 0.109375
- post_gain: float32 [1536], replicated, may hold values from 0.5 to 1.5
- sh_gate: bfloat16 [1536, 1024], P(None, 'exp'), may hold values from -0.15625 to 0.15625
- sh_up: bfloat16 [1536, 1024], P(None, 'exp'), may hold values from -0.15625 to 0.15625
- sh_down: bfloat16 [1024, 1536], P('exp'), may hold values from -0.1875 to 0.1875
- ex_gate: bfloat16 [64, 1536, 512], P('seq'), may hold values from -0.15625 to 0.15625
- ex_up: bfloat16 [64, 1536, 512], P('seq'), may hold values from -0.15625 to 0.15625
- ex_down: bfloat16 [64, 512, 1536], P('seq'), may hold values from -0.25 to 0.25
- routes: int32 [16384, 6], P(('seq', 'exp')), may hold values from 0 to 63, all different within a row; in each aligned block of 128 rows (0 to 127, 128 to 255, ...) at most 16 rows name the same one
- gates: float32 [16384, 6], P(('seq', 'exp')), may hold values from 0.1 to 1
- lengths: int32 [16], replicated, may hold values from 1 to 4096, 16384 in all
- cache_slot: int32 [16], replicated, may hold values from 0 to 15, each once
Outputs:
- layer_out: bfloat16 [16384, 1536], P(('seq', 'exp'))
- state_cache: float32 [16, 48, 64, 128], P('seq', 'exp')
Inputs may be any that keep to these rules, and one draw needn't show every extreme that they name: `routes`: in the rows of one device (aligned blocks of 128 rows) no expert is named by more than 16 rows, a bound that some block reaches; each row names 6 different experts. The lengths sum to 16384; the largest is exactly 4096. `cache_slot`: every slot is named once.
All inputs are finite; a program needn't handle non-finite values.
Results may differ from a plain program's by a relative error of at most 0.019.
Values may be sent and summed in bfloat16 or wider, within the bound.
No kernel may reach another device: no remote copies, remote signals or barrier semaphores. Data moves between devices by JAX's collectives and lax.ppermute only.
A program may use at most 128 MiB of HBM per device.

v0:
```python
import jax
import jax.numpy as jnp
from jax import lax
from jax.sharding import PartitionSpec as P

BLOCK = 512
DI = 3072


epsilon = 1e-05
highest = lax.Precision.HIGHEST


def from_behind(block, axis, distance):
    devices = range(lax.axis_size(axis))
    route = [(i - distance, i) for i in devices if i - distance in devices]
    return lax.ppermute(block, axis, route)


def rms_rows(values, gain):
    meansq = jnp.mean(values * values, axis=-1, keepdims=True)
    return values * lax.rsqrt(meansq + epsilon) * gain


def segment_of(positions, req_ends):
    return jnp.sum((positions[:, None] >= req_ends[None, :]).astype(jnp.int32), axis=1)


def causal_conv(extended, weight, ext_segment, segment, row_count):
    summed = jnp.zeros((row_count, extended.shape[1]), jnp.float32)
    for tap in range(weight.shape[0]):
        window = extended[tap : tap + row_count].astype(jnp.float32)
        kept = (ext_segment[tap : tap + row_count] == segment)[:, None]
        summed = summed + jnp.where(kept, weight[tap] * window, 0.0)
    return jax.nn.silu(summed).astype(jnp.bfloat16)


def body(
    tokens,
    in_gain,
    in_z,
    in_x,
    in_bc,
    in_dt,
    conv_x,
    conv_bc,
    dt_bias,
    a_log,
    d_skip,
    norm_gain,
    out_w,
    post_gain,
    sh_gate,
    sh_up,
    sh_down,
    ex_gate,
    ex_up,
    ex_down,
    routes,
    gates,
    lengths,
    cache_slot,
):
    seq_count = lax.axis_size("seq")
    own_rows = tokens.shape[0]
    width = tokens.shape[1]
    state_size = in_bc.shape[1] // 2
    local_heads = a_log.shape[0]
    head_width = conv_x.shape[1] // local_heads
    taps = conv_x.shape[0]
    stream = lax.all_gather(tokens, "exp", axis=0, tiled=True)
    row_count = stream.shape[0]
    normed_in = rms_rows(stream.astype(jnp.float32), in_gain).astype(jnp.bfloat16)
    gate_raw = jnp.dot(normed_in, in_z, preferred_element_type=jnp.float32).astype(jnp.bfloat16)
    conv_in_x = jnp.dot(normed_in, in_x, preferred_element_type=jnp.float32).astype(jnp.bfloat16)
    conv_in_bc = jnp.dot(normed_in, in_bc, preferred_element_type=jnp.float32).astype(jnp.bfloat16)
    dt_raw = jnp.dot(normed_in, in_dt, preferred_element_type=jnp.float32).astype(jnp.bfloat16)
    req_ends = jnp.cumsum(lengths)
    req_count = lengths.shape[0]
    req_ids = jnp.arange(req_count, dtype=jnp.int32)
    end_pos = req_ends - 1
    stream_start = lax.axis_index("seq") * row_count
    local_idx = jnp.arange(row_count, dtype=jnp.int32)
    segment = segment_of(stream_start + local_idx, req_ends)
    before_dev = jnp.where(
        stream_start > 0, segment_of(jnp.reshape(stream_start - 1, (1,)), req_ends)[0], -1
    )
    x_cols = conv_in_x.shape[1]
    tail_rows = jnp.concatenate(
        [conv_in_x[row_count - (taps - 1) :], conv_in_bc[row_count - (taps - 1) :]], axis=1
    )
    edge_rows = from_behind(tail_rows, "seq", 1)
    ext_x = jnp.concatenate([edge_rows[:, :x_cols], conv_in_x])
    ext_bc = jnp.concatenate([edge_rows[:, x_cols:], conv_in_bc])
    ext_pos = stream_start - (taps - 1) + jnp.arange(row_count + taps - 1, dtype=jnp.int32)
    ext_segment = jnp.where(ext_pos >= 0, segment_of(ext_pos, req_ends), -1)
    conv_x_out = causal_conv(ext_x, conv_x, ext_segment, segment, row_count)
    conv_bc_out = causal_conv(ext_bc, conv_bc, ext_segment, segment, row_count)
    b_all = conv_bc_out[:, :state_size]
    c_all = conv_bc_out[:, state_size:]
    step_size = jax.nn.softplus(dt_raw.astype(jnp.float32) + dt_bias)
    log_decay = -step_size * jnp.exp(a_log)
    heads_x = conv_x_out.reshape(row_count, local_heads, head_width)

    def block_step(carried, block):
        state, end_acc = carried
        drive_x, b_rows, c_rows, decay_rows, step_rows, block_seg, before_seg, base = block
        length = block_seg.shape[0]
        cumulative = jnp.cumsum(decay_rows, axis=0)
        order = jnp.arange(length, dtype=jnp.int32)
        same = (block_seg[:, None] == block_seg[None, :]) & (order[:, None] >= order[None, :])
        log_gap = cumulative[:, None, :] - cumulative[None, :, :]
        decay = jnp.where(same[:, :, None], jnp.exp(jnp.where(same[:, :, None], log_gap, 0.0)), 0.0)
        scores = jnp.dot(c_rows, b_rows.T, preferred_element_type=jnp.float32)
        drive = drive_x.astype(jnp.float32) * step_rows[:, :, None]
        weights = scores[:, :, None] * decay
        outputs = jnp.einsum("tsh,shp->thp", weights, drive, precision=highest)
        c_float = c_rows.astype(jnp.float32)
        b_float = b_rows.astype(jnp.float32)
        entry = jnp.where((block_seg == before_seg)[:, None], jnp.exp(cumulative), 0.0)
        outputs = outputs + entry[:, :, None] * jnp.einsum(
            "tn,hpn->thp", c_float, state, precision=highest
        )
        last_seg = block_seg[length - 1]
        tail = jnp.where(
            (block_seg == last_seg)[:, None],
            jnp.exp(cumulative[length - 1][None, :] - cumulative),
            0.0,
        )
        persist = jnp.where(last_seg == before_seg, jnp.exp(cumulative[length - 1]), 0.0)
        new_state = persist[:, None, None] * state + jnp.einsum(
            "sh,shp,sn->hpn", tail, drive, b_float, precision=highest
        )
        local_end = end_pos - base
        inside = (local_end >= 0) & (local_end < length)

        def close_request(req, acc):
            end_row = jnp.clip(local_end[req], 0, length - 1)
            cum_end = cumulative[end_row]
            member = (block_seg == req)[:, None]
            end_weights = jnp.where(
                member, jnp.exp(jnp.where(member, cum_end[None, :] - cumulative, 0.0)), 0.0
            )
            fresh = jnp.einsum("sh,shp,sn->hpn", end_weights, drive, b_float, precision=highest)
            holding = jnp.where(req == before_seg, jnp.exp(cum_end), 0.0)
            value = jnp.where(inside[req], fresh + holding[:, None, None] * state, 0.0)
            return lax.dynamic_update_index_in_dim(acc, acc[req] + value, req, 0)

        end_acc = lax.fori_loop(block_seg[0], last_seg + 1, close_request, end_acc)
        return ((new_state, end_acc), outputs)

    block_count = row_count // BLOCK

    def blocked(values):
        return values.reshape((block_count, BLOCK) + values.shape[1:])

    before_rows = jnp.concatenate([jnp.reshape(before_dev, (1,)), segment[:-1]])
    block_base = stream_start + jnp.arange(block_count, dtype=jnp.int32) * BLOCK
    blocks = (
        blocked(heads_x),
        blocked(b_all),
        blocked(c_all),
        blocked(log_decay),
        blocked(step_size),
        blocked(segment),
        blocked(before_rows)[:, 0],
        block_base,
    )
    zero_state = jnp.zeros((local_heads, head_width, state_size), jnp.float32)
    zero_ends = jnp.zeros((req_count, local_heads, head_width, state_size), jnp.float32)
    (end_state, end_local), outputs = lax.scan(block_step, (zero_state, zero_ends), blocks)
    outputs = outputs.reshape(row_count, local_heads, head_width)
    cum_dev = jnp.cumsum(log_decay, axis=0)
    pass_decay = jnp.where(
        segment[row_count - 1] == before_dev, jnp.exp(cum_dev[row_count - 1]), 0.0
    )

    def hop(_, state):
        return from_behind(
            (pass_decay[:, None, None] * state + end_state).astype(jnp.bfloat16), "seq", 1
        ).astype(jnp.float32)

    state_in = lax.fori_loop(0, seq_count - 1, hop, zero_state)
    leading = jnp.where((segment == before_dev)[:, None], jnp.exp(cum_dev), 0.0)
    carried_in = jnp.einsum("tn,hpn->thp", c_all.astype(jnp.float32), state_in, precision=highest)
    mixed_y = (
        outputs
        + leading[:, :, None] * carried_in
        + d_skip[None, :, None] * heads_x.astype(jnp.float32)
    )
    dev_end = end_pos - stream_start
    on_dev = (dev_end >= 0) & (dev_end < row_count)
    end_row = jnp.clip(dev_end, 0, row_count - 1)
    holding = jnp.where((on_dev & (req_ids == before_dev))[:, None], jnp.exp(cum_dev[end_row]), 0.0)
    end_all = end_local + holding[:, :, None, None] * state_in[None]
    placed = jnp.zeros_like(end_all).at[cache_slot].set(end_all)
    state_cache = lax.psum_scatter(
        placed.astype(jnp.bfloat16), "seq", scatter_dimension=0, tiled=True
    ).astype(jnp.float32)
    gated_flat = mixed_y.reshape(row_count, local_heads * head_width) * jax.nn.silu(
        gate_raw.astype(jnp.float32)
    )
    square_part = jnp.sum(gated_flat * gated_flat, axis=1)
    square_sum = lax.psum(square_part, "exp")
    scaled = (gated_flat * lax.rsqrt(square_sum / DI + epsilon)[:, None] * norm_gain).astype(
        jnp.bfloat16
    )
    mix_term = jnp.dot(scaled, out_w, preferred_element_type=jnp.float32)
    row_start = lax.axis_index("exp") * own_rows
    mixer_out = lax.psum(mix_term.astype(jnp.bfloat16), "exp").astype(jnp.float32)
    residual_all = stream.astype(jnp.float32) + mixer_out
    normed_all = rms_rows(residual_all, post_gain).astype(jnp.bfloat16)
    residual = lax.dynamic_slice_in_dim(residual_all, row_start, own_rows, 0)
    normed = lax.dynamic_slice_in_dim(normed_all, row_start, own_rows, 0)
    shared_hidden = (
        jax.nn.silu(jnp.dot(normed_all, sh_gate, preferred_element_type=jnp.float32))
        * jnp.dot(normed_all, sh_up, preferred_element_type=jnp.float32)
    ).astype(jnp.bfloat16)
    shared = lax.psum_scatter(
        jnp.dot(shared_hidden, sh_down, preferred_element_type=jnp.float32).astype(jnp.bfloat16),
        "exp",
        scatter_dimension=0,
        tiled=True,
    ).astype(jnp.float32)
    top_count = routes.shape[1]
    owned = ex_gate.shape[0]
    experts = owned * seq_count
    capacity = own_rows * top_count * 4 // (3 * experts)
    flat_routes = routes.reshape(-1)
    onehot = (flat_routes[:, None] == jnp.arange(experts, dtype=jnp.int32)[None, :]).astype(
        jnp.int32
    )
    slot_rank = jnp.sum(onehot * (jnp.cumsum(onehot, axis=0) - 1), axis=1)
    slot_idx = flat_routes * capacity + slot_rank
    owner_tok = jnp.arange(own_rows * top_count, dtype=jnp.int32) // top_count
    slot_tok = jnp.full((experts * capacity,), own_rows, jnp.int32).at[slot_idx].set(owner_tok)
    padded = jnp.concatenate([normed, jnp.zeros((1, width), jnp.bfloat16)])
    outgoing = padded[slot_tok].reshape(seq_count, owned, capacity, width)
    received = lax.all_to_all(outgoing, "seq", split_axis=0, concat_axis=0, tiled=True)
    gate_part = jnp.einsum("secd,edf->secf", received, ex_gate, preferred_element_type=jnp.float32)
    up_part = jnp.einsum("secd,edf->secf", received, ex_up, preferred_element_type=jnp.float32)
    hidden = (jax.nn.silu(gate_part) * up_part).astype(jnp.bfloat16)
    expert_out = jnp.einsum(
        "secf,efd->secd", hidden, ex_down, preferred_element_type=jnp.float32
    ).astype(jnp.bfloat16)
    returned = lax.all_to_all(expert_out, "seq", split_axis=0, concat_axis=0, tiled=True)
    picked = returned.reshape(experts * capacity, width)[slot_idx].reshape(
        own_rows, top_count, width
    )
    routed = jnp.sum(gates[:, :, None] * picked.astype(jnp.float32), axis=1)
    layer_out = (residual + shared + routed).astype(jnp.bfloat16)
    return (layer_out, state_cache)


def solution(mesh):
    placed = (
        P(("seq", "exp"), None),
        P(),
        P(None, "exp"),
        P(None, "exp"),
        P(),
        P(None, "exp"),
        P(None, "exp"),
        P(),
        P("exp"),
        P("exp"),
        P("exp"),
        P("exp"),
        P("exp", None),
        P(),
        P(None, "exp"),
        P(None, "exp"),
        P("exp", None),
        P("seq", None, None),
        P("seq", None, None),
        P("seq", None, None),
        P(("seq", "exp"), None),
        P(("seq", "exp"), None),
        P(),
        P(),
    )
    return jax.shard_map(
        body,
        mesh=mesh,
        in_specs=placed,
        out_specs=(P(("seq", "exp"), None), P("seq", "exp", None, None)),
        check_vma=False,
    )
```

profile of v0, /device:TPU:0, one launch (start us, length us, event | category | flops | bytes accessed | tf_op | source)
XLA Modules:
  0.0 620.3 jit_solution(3403911844091310595)
XLA Ops:
  20.6 19.3 %all-gather.2.cloned.1.call-done = bf16[1024,1536]{1,0:T(8,128)(2,1)} async-done(((bf16[128,1536]{1,0:T(8,128)(2,1)}), bf16[1024,1536]{1,0:T(8,128)(2,1)}) %all-gather.2.cloned.1.call-update) | async-done | bytes 3145744 | tf_op jit(solution)/shard_map/all_gather | solution.py:71
  46.9 3.5 collective-permute-start.1
  58.2 3.6 multiply_convert_fusion.3
  68.3 127.9 %while.38 = (s32[]{:T(128)}, f32[6,64,128]{2,1,0:T(8,128)S(1)}, f32[16,6,64,128]{3,2,1,0:T(8,128)}, f32[2,512,6,64]{1,0,3,2:T(2,128)}, s32[2,512]{1,0:T(2,128)S(...) while((s32[]{:T(128)}, f32[6,64,128]{2,1,0:T(8,128)S(1)}, ...), condition=%wide.region_10.11_spmd.clone, body=%wide.region_5.10_spmd.clone.sunk | while | flops 2190904832 | bytes 14461588 | solution.py:171
  72.4 9.3 %fusion.159 = f32[512,6,64]{0,2,1:T(8,128)} fusion(f32[512,6]{0,1:T(8,128)S(1)} %copy.189, f32[512,512]{1,0:T(8,128)S(1)} %fusion.157, pred[512,512]{1,0:T(8,128)(4,1)S(1)} %fusion.158, f32[512,6]{0,1:T(8,128)S(1)} %get-tuple-element.568, bf16[2,512,6,64]{1,3,2,0:T(8,128)(2,1)} %get-tuple-element.690, s32[]{:T(128)} %get-tuple-element.661), kind=kOutput, calls=%fused_computation.30.clone.1 | convolution fusion | flops 1214644224 | bytes 2540032 | tf_op jit(solution)/shard_map/while/body/eval_jaxpr/tsh,shp->thp/dot_general | solution.py:117
  87.5 14.9 %dynamic_update_slice.12 = f32[2,512,6,64]{1,0,3,2:T(2,128)} dynamic-update-slice(f32[2,512,6,64]{1,0,3,2:T(2,128)} %get-tuple-element.664, f32[1,512,6,64]{1,0,3,2:T(1,128)S(1)} %copy.191, s32[]{:T(128)} %get-tuple-element.661, s32[]{:T(128)} %constant.71.clone.1..sunk, s32[]{:T(128)} %constant.71.clone.1..sunk, s32[]{:T(128)} %constant.71.clone.1..sunk) | dynamic-update-slice | bytes 1572868 | tf_op jit(solution)/shard_map/while/body/jit(dynamic_update_index_in_dim)/dynamic_update_slice | solution.py:171
  107.5 21.8 %while.40 = (s32[]{:T(128)}, f32[16,6,64,128]{3,2,1,0:T(8,128)}, s32[]{:T(128)}, pred[16]{0:T(512)(128)(4,1)S(1)}, s32[512]{0:T(512)S(1)}, /*index=5*/s32[16]{0:...) while((s32[]{:T(128)}, f32[16,6,64,128]{3,2,1,0:T(8,128)}, ...), condition=%wide.region_9.9_spmd, body=%wide.region_8.8_spmd.sunk | while | flops 302392832 | bytes 2097011 | solution.py:149
  136.3 9.3 %fusion.159 = f32[512,6,64]{0,2,1:T(8,128)} fusion(f32[512,6]{0,1:T(8,128)S(1)} %copy.189, f32[512,512]{1,0:T(8,128)S(1)} %fusion.157, pred[512,512]{1,0:T(8,128)(4,1)S(1)} %fusion.158, f32[512,6]{0,1:T(8,128)S(1)} %get-tuple-element.568, bf16[2,512,6,64]{1,3,2,0:T(8,128)(2,1)} %get-tuple-element.690, s32[]{:T(128)} %get-tuple-element.661), kind=kOutput, calls=%fused_computation.30.clone.1 | convolution fusion | flops 1214644224 | bytes 2540032 | tf_op jit(solution)/shard_map/while/body/eval_jaxpr/tsh,shp->thp/dot_general | solution.py:117
  151.5 14.9 %dynamic_update_slice.12 = f32[2,512,6,64]{1,0,3,2:T(2,128)} dynamic-update-slice(f32[2,512,6,64]{1,0,3,2:T(2,128)} %get-tuple-element.664, f32[1,512,6,64]{1,0,3,2:T(1,128)S(1)} %copy.191, s32[]{:T(128)} %get-tuple-element.661, s32[]{:T(128)} %constant.71.clone.1..sunk, s32[]{:T(128)} %constant.71.clone.1..sunk, s32[]{:T(128)} %constant.71.clone.1..sunk) | dynamic-update-slice | bytes 1572868 | tf_op jit(solution)/shard_map/while/body/jit(dynamic_update_index_in_dim)/dynamic_update_slice | solution.py:171
  171.5 21.8 %while.40 = (s32[]{:T(128)}, f32[16,6,64,128]{3,2,1,0:T(8,128)}, s32[]{:T(128)}, pred[16]{0:T(512)(128)(4,1)S(1)}, s32[512]{0:T(512)S(1)}, /*index=5*/s32[16]{0:...) while((s32[]{:T(128)}, f32[16,6,64,128]{3,2,1,0:T(8,128)}, ...), condition=%wide.region_9.9_spmd, body=%wide.region_8.8_spmd.sunk | while | flops 302392832 | bytes 2097011 | solution.py:149
  196.3 3.5 reshape.330
  199.8 126.1 %while.39 = (s32[]{:T(128)}, f32[6,64,128]{2,1,0:T(8,128)S(1)}, f32[6]{0:T(128)S(1)}, f32[6,64,128]{2,1,0:T(8,128)S(1)}, s32[]{:T(128)}, /*index=5*/s32[]{:T(128)}) while((s32[]{:T(128)}, f32[6,64,128]{2,1,0:T(8,128)S(1)}, f32[6]{0:T(128)S(1)}, f32[6,64,128]{2,1,0:T(8,128)S(1)}, s32[]{:T(128)}, /*index=5*/s32[]{:T(128)}) %tuple.118), condition=%wide.region_14.15_spmd.clone, body=%wide.region_13.14_spmd.clone.sunk | while | flops 245763 | bytes 1179791 | solution.py:183
  203.8 15.7 %collective-permute-start = (bf16[6,64,128]{2,1,0:T(8,128)(2,1)S(1)}, bf16[6,64,128]{2,1,0:T(8,128)(2,1)S(1)}, u32[]{:S(2)}, u32[]{:S(2)}) collective-permute-start(bf16[6,64,128]{2,1,0:T(8,128)(2,1)S(1)} %fusion.161), channel_id=1, source_target_pairs={{0,8},{8,16},{16,24},{24,32},{32,40},{40,48},{48,56},{56,64},{64,7... | collective-permute-start | bytes 294920 | tf_op jit(solution)/shard_map/while/body/eval_jaxpr/ppermute | solution.py:17
  221.9 4.4 collective-permute-start
  228.5 4.3 collective-permute-start
  235.2 4.3 collective-permute-start
  242.3 4.4 collective-permute-start
  249.7 4.4 collective-permute-start
  254.1 3.1 collective-permute-done
  257.3 4.4 collective-permute-start
  264.9 6.3 %collective-permute-start = (bf16[6,64,128]{2,1,0:T(8,128)(2,1)S(1)}, bf16[6,64,128]{2,1,0:T(8,128)(2,1)S(1)}, u32[]{:S(2)}, u32[]{:S(2)}) collective-permute-start(bf16[6,64,128]{2,1,0:T(8,128)(2,1)S(1)} %fusion.161), channel_id=1, source_target_pairs={{0,8},{8,16},{16,24},{24,32},{32,40},{40,48},{48,56},{56,64},{64,7... | collective-permute-start | bytes 294920 | tf_op jit(solution)/shard_map/while/body/eval_jaxpr/ppermute | solution.py:17
  273.6 6.3 %collective-permute-start = (bf16[6,64,128]{2,1,0:T(8,128)(2,1)S(1)}, bf16[6,64,128]{2,1,0:T(8,128)(2,1)S(1)}, u32[]{:S(2)}, u32[]{:S(2)}) collective-permute-start(bf16[6,64,128]{2,1,0:T(8,128)(2,1)S(1)} %fusion.161), channel_id=1, source_target_pairs={{0,8},{8,16},{16,24},{24,32},{32,40},{40,48},{48,56},{56,64},{64,7... | collective-permute-start | bytes 294920 | tf_op jit(solution)/shard_map/while/body/eval_jaxpr/ppermute | solution.py:17
  282.2 6.2 %collective-permute-start = (bf16[6,64,128]{2,1,0:T(8,128)(2,1)S(1)}, bf16[6,64,128]{2,1,0:T(8,128)(2,1)S(1)}, u32[]{:S(2)}, u32[]{:S(2)}) collective-permute-start(bf16[6,64,128]{2,1,0:T(8,128)(2,1)S(1)} %fusion.161), channel_id=1, source_target_pairs={{0,8},{8,16},{16,24},{24,32},{32,40},{40,48},{48,56},{56,64},{64,7... | collective-permute-start | bytes 294920 | tf_op jit(solution)/shard_map/while/body/eval_jaxpr/ppermute | solution.py:17
  290.7 6.5 %collective-permute-start = (bf16[6,64,128]{2,1,0:T(8,128)(2,1)S(1)}, bf16[6,64,128]{2,1,0:T(8,128)(2,1)S(1)}, u32[]{:S(2)}, u32[]{:S(2)}) collective-permute-start(bf16[6,64,128]{2,1,0:T(8,128)(2,1)S(1)} %fusion.161), channel_id=1, source_target_pairs={{0,8},{8,16},{16,24},{24,32},{32,40},{40,48},{48,56},{56,64},{64,7... | collective-permute-start | bytes 294920 | tf_op jit(solution)/shard_map/while/body/eval_jaxpr/ppermute | solution.py:17
  299.6 6.4 %collective-permute-start = (bf16[6,64,128]{2,1,0:T(8,128)(2,1)S(1)}, bf16[6,64,128]{2,1,0:T(8,128)(2,1)S(1)}, u32[]{:S(2)}, u32[]{:S(2)}) collective-permute-start(bf16[6,64,128]{2,1,0:T(8,128)(2,1)S(1)} %fusion.161), channel_id=1, source_target_pairs={{0,8},{8,16},{16,24},{24,32},{32,40},{40,48},{48,56},{56,64},{64,7... | collective-permute-start | bytes 294920 | tf_op jit(solution)/shard_map/while/body/eval_jaxpr/ppermute | solution.py:17
  308.3 6.4 %collective-permute-start = (bf16[6,64,128]{2,1,0:T(8,128)(2,1)S(1)}, bf16[6,64,128]{2,1,0:T(8,128)(2,1)S(1)}, u32[]{:S(2)}, u32[]{:S(2)}) collective-permute-start(bf16[6,64,128]{2,1,0:T(8,128)(2,1)S(1)} %fusion.161), channel_id=1, source_target_pairs={{0,8},{8,16},{16,24},{24,32},{32,40},{40,48},{48,56},{56,64},{64,7... | collective-permute-start | bytes 294920 | tf_op jit(solution)/shard_map/while/body/eval_jaxpr/ppermute | solution.py:17
  317.1 6.4 %collective-permute-start = (bf16[6,64,128]{2,1,0:T(8,128)(2,1)S(1)}, bf16[6,64,128]{2,1,0:T(8,128)(2,1)S(1)}, u32[]{:S(2)}, u32[]{:S(2)}) collective-permute-start(bf16[6,64,128]{2,1,0:T(8,128)(2,1)S(1)} %fusion.161), channel_id=1, source_target_pairs={{0,8},{8,16},{16,24},{24,32},{32,40},{40,48},{48,56},{56,64},{64,7... | collective-permute-start | bytes 294920 | tf_op jit(solution)/shard_map/while/body/eval_jaxpr/ppermute | solution.py:17
  326.0 3.7 multiply_add_fusion.1
  331.5 5.3 multiply_reduce_fusion.2
  336.9 12.4 %psum.14 = f32[1024]{0:T(1024)S(1)} all-reduce(f32[1024]{0:T(1024)S(1)} %get-tuple-element.369), channel_id=1, replica_groups=mesh['seq'=16,'exp'=8] {'exp'}, use_global_device_ids=true, to_apply=%region_16.17 | all-reduce | flops 1024 | bytes 8192 | tf_op jit(solution)/shard_map/psum | solution.py:204
  349.3 5.0 convolution_convert_fusion.1
  354.4 3.4 scatter_custom_fusion
  365.7 6.2 scatter_fusion
  371.9 3.6 convert_element_type.187
  375.4 55.3 %all-reduce.4.cloned.1.call-done = bf16[1024,1536]{1,0:T(8,128)(2,1)} async-done(((bf16[1024,1536]{1,0:T(8,128)(2,1)}), bf16[1024,1536]{1,0:T(8,128)(2,1)}) %all-reduce.4.cloned.1.call-update) | async-done | bytes 3145744 | tf_op jit(solution)/shard_map/psum | solution.py:210
  430.7 5.7 convert_add_fusion
  439.4 5.6 gather_fusion
  445.0 7.3 %all-to-all-start = ((bf16[16,4,16,1536]{3,2,1,0:T(8,128)(2,1)}), bf16[16,4,16,1536]{3,2,1,0:T(8,128)(2,1)}, u32[]{:S(2)}, u32[]{:S(2)}) async-start(bf16[16,4,16,1536]{3,2,1,0:T(8,128)(2,1)} %bitcast.253), calls=%async_computation.1 | async-start | bytes 6291456 | tf_op jit(solution)/shard_map/all_to_all | solution.py:239
  454.4 6.2 %convolution_convert_fusion = bf16[1024,1536]{1,0:T(8,128)(2,1)} fusion(bf16[128,1536]{1,0:T(8,128)(2,1)} %param.46, bf16[1024,1536]{1,0:T(8,128)(2,1)S(1)} %copy-done.5, bf16[1536,128]{1,0:T(8,128)(2,1)} %param.45, f32[1024,128]{1,0:T(8,128)} %fusion.118), kind=kOutput, calls=%fused_computation.87 | convolution fusion | flops 807665664 | bytes 7602176 | tf_op jit(solution)/shard_map/dot_general | solution.py:220
  460.6 34.5 %all-to-all-done = bf16[16,4,16,1536]{3,2,1,0:T(8,128)(2,1)} async-done(((bf16[16,4,16,1536]{3,2,1,0:T(8,128)(2,1)}), bf16[16,4,16,1536]{3,2,1,0:T(8,128)(2,1)}, u32[]{:S(2)}, u32[]{:S(2)}) %all-to-all-start) | async-done | bytes 3145760 | tf_op jit(solution)/shard_map/all_to_all | solution.py:239
  495.2 6.9 %fusion.50 = f32[4,16,16,512]{3,2,1,0:T(8,128)} fusion(bf16[4,1536,512]{2,1,0:T(8,128)(2,1)} %param.47, bf16[16,4,16,1536]{3,2,1,0:T(8,128)(2,1)} %all-to-all-done), kind=kOutput, calls=%fused_computation.82 | convolution fusion | flops 1610612736 | bytes 11534336 | tf_op jit(solution)/shard_map/secd,edf->secf/dot_general | solution.py:240
  502.1 9.7 %fusion.55 = bf16[16,4,16,1536]{3,2,0,1:T(8,128)(2,1)S(1)} fusion(bf16[4,512,1536]{2,1,0:T(8,128)(2,1)} %param.49, f32[4,16,16,512]{3,2,1,0:T(8,128)} %fusion.50, bf16[4,1536,512]{2,1,0:T(8,128)(2,1)} %param.48, bf16[16,4,16,1536]{3,2,1,0:T(8,128)(2,1)} %all-to-all-done), kind=kOutput, calls=%fused_computation.90 | convolution fusion | flops 3225944064 | bytes 20971520 | tf_op jit(solution)/shard_map/secf,efd->secd/dot_general | solution.py:243
  513.7 4.1 all-to-all-start.1
  518.0 41.3 %reduce-scatter.7.cloned.1.call-done = bf16[1,6,64,128]{3,2,1,0:T(8,128)(2,1)} async-done(((bf16[16,6,64,128]{3,2,1,0:T(8,128)(2,1)}), bf16[1,6,64,128]{3,2,1,0:T(8,128)(2,1)}) %reduce-scatter.7.cloned.1.call-update) | async-done | bytes 98320
  560.9 3.8 gather_fusion.1
  564.7 5.1 reshape.339
  569.8 5.1 multiply_reduce_fusion
  574.9 36.3 %reduce-scatter.5.cloned.1.call-done = bf16[128,1536]{1,0:T(8,128)(2,1)} async-done(((bf16[1024,1536]{1,0:T(8,128)(2,1)}), bf16[128,1536]{1,0:T(8,128)(2,1)}) %reduce-scatter.5.cloned.1.call-update) | async-done | bytes 393232 | tf_op jit(solution)/shard_map/reduce_scatter | solution.py:219
  (294 shorter events, 142.1 us)
Async XLA Ops:
  7.2 342.1 %copy-start = (bf16[384,1536]{1,0:T(8,128)(2,1)S(1)}, bf16[384,1536]{1,0:T(8,128)(2,1)}, u32[]{:S(2)}) copy-start(bf16[384,1536]{1,0:T(8,128)(2,1)} %param.42) | copy-start | bytes 3538948
  7.2 35.5 %copy-start.20 = (f32[1536]{0:T(1024)S(1)}, f32[1536]{0:T(1024)}, u32[]{:S(2)}) copy-start(f32[1536]{0:T(1024)} %param.31) | copy-start | bytes 18436
  7.2 32.7 %all-gather.2.cloned.1.call-start = ((), (), s32[]{:S(2)}) async-start(), calls=%async_computation.4 | async-start | bytes 3538944 | tf_op jit(solution)/shard_map/all_gather | solution.py:71
  7.9 422.8 %all-reduce.4.cloned.1.call-start = ((), (), s32[]{:S(2)}) async-start(), calls=%async_computation.5 | async-start | bytes 6291456 | tf_op jit(solution)/shard_map/psum | solution.py:210
  9.5 30.4 %copy-start.22 = (s32[16]{0:T(128)}, s32[16]{0:T(128)S(1)}, u32[]{:S(2)}) copy-start(s32[16]{0:T(128)S(1)} %get-tuple-element.280) | copy-start | bytes 196
  44.0 7.3 %copy-start.7 = (bf16[1024,1536]{1,0:T(8,128)(2,1)}, bf16[1024,1536]{1,0:T(8,128)(2,1)S(1)}, u32[]{:S(2)}) copy-start(bf16[1024,1536]{1,0:T(8,128)(2,1)S(1)} %fusion.45) | copy-start | bytes 9437188
  45.8 4.5 copy-start.18
  45.9 4.5 copy-start.26
  46.8 7.7 %copy-start.15 = (bf16[1024,256]{1,0:T(8,128)(2,1)}, bf16[1024,256]{1,0:T(8,128)(2,1)S(1)}, u32[]{:S(2)}) copy-start(bf16[1024,256]{1,0:T(8,128)(2,1)S(1)} %convolution_convert_fusion.4) | copy-start | bytes 1572868
  46.9 7.6 %collective-permute-start.1 = (bf16[3,640]{1,0:T(4,128)(2,1)S(1)}, bf16[3,640]{1,0:T(4,128)(2,1)S(1)}, u32[]{:S(2)}, u32[]{:S(2)}) collective-permute-start(bf16[3,640]{1,0:T(4,128)(2,1)S(1)} %pad_maximum_fusion.2), channel_id=1, source_target_pairs={{0,8},{8,16},{16,24},{24,32},{32,40},{40,48},{48,56},{56,64},{64,7... | collective-permute-start | bytes 11528 | tf_op jit(solution)/shard_map/ppermute | solution.py:17
  61.8 6.6 %copy-start.14 = (bf16[1024,256]{1,0:T(8,128)(2,1)}, bf16[1024,256]{1,0:T(8,128)(2,1)S(1)}, u32[]{:S(2)}) copy-start(bf16[1024,256]{1,0:T(8,128)(2,1)S(1)} %multiply_convert_fusion.3) | copy-start | bytes 1572868
  196.2 129.7 %copy-start.13 = (f32[1024,384]{0,1:T(8,128)S(1)}, f32[1024,384]{0,1:T(8,128)}, u32[]{:S(2)}) copy-start(f32[1024,384]{0,1:T(8,128)} %copy.134) | copy-start | bytes 4718596
  196.3 129.7 %copy-start.17 = (f32[1024,6]{0,1:T(8,128)S(1)}, f32[1024,6]{0,1:T(8,128)}, u32[]{:S(2)}) copy-start(f32[1024,6]{0,1:T(8,128)} %exponential_select_fusion.3) | copy-start | bytes 73732
  196.3 129.7 %copy-start.27 = (f32[6]{0:T(128)S(1)}, f32[6]{0:T(128)}, u32[]{:S(2)}) copy-start(f32[6]{0:T(128)} %param.40) | copy-start | bytes 76
  199.9 3.7 collective-permute-start
  203.8 17.9 %collective-permute-start = (bf16[6,64,128]{2,1,0:T(8,128)(2,1)S(1)}, bf16[6,64,128]{2,1,0:T(8,128)(2,1)S(1)}, u32[]{:S(2)}, u32[]{:S(2)}) collective-permute-start(bf16[6,64,128]{2,1,0:T(8,128)(2,1)S(1)} %fusion.161), channel_id=1, source_target_pairs={{0,8},{8,16},{16,24},{24,32},{32,40},{40,48},{48,56},{56,64},{64,7... | collective-permute-start | bytes 294920 | tf_op jit(solution)/shard_map/while/body/eval_jaxpr/ppermute | solution.py:17
  221.9 6.6 %collective-permute-start = (bf16[6,64,128]{2,1,0:T(8,128)(2,1)S(1)}, bf16[6,64,128]{2,1,0:T(8,128)(2,1)S(1)}, u32[]{:S(2)}, u32[]{:S(2)}) collective-permute-start(bf16[6,64,128]{2,1,0:T(8,128)(2,1)S(1)} %fusion.161), channel_id=1, source_target_pairs={{0,8},{8,16},{16,24},{24,32},{32,40},{40,48},{48,56},{56,64},{64,7... | collective-permute-start | bytes 294920 | tf_op jit(solution)/shard_map/while/body/eval_jaxpr/ppermute | solution.py:17
  228.5 6.5 %collective-permute-start = (bf16[6,64,128]{2,1,0:T(8,128)(2,1)S(1)}, bf16[6,64,128]{2,1,0:T(8,128)(2,1)S(1)}, u32[]{:S(2)}, u32[]{:S(2)}) collective-permute-start(bf16[6,64,128]{2,1,0:T(8,128)(2,1)S(1)} %fusion.161), channel_id=1, source_target_pairs={{0,8},{8,16},{16,24},{24,32},{32,40},{40,48},{48,56},{56,64},{64,7... | collective-permute-start | bytes 294920 | tf_op jit(solution)/shard_map/while/body/eval_jaxpr/ppermute | solution.py:17
  235.2 7.0 %collective-permute-start = (bf16[6,64,128]{2,1,0:T(8,128)(2,1)S(1)}, bf16[6,64,128]{2,1,0:T(8,128)(2,1)S(1)}, u32[]{:S(2)}, u32[]{:S(2)}) collective-permute-start(bf16[6,64,128]{2,1,0:T(8,128)(2,1)S(1)} %fusion.161), channel_id=1, source_target_pairs={{0,8},{8,16},{16,24},{24,32},{32,40},{40,48},{48,56},{56,64},{64,7... | collective-permute-start | bytes 294920 | tf_op jit(solution)/shard_map/while/body/eval_jaxpr/ppermute | solution.py:17
  242.3 7.2 %collective-permute-start = (bf16[6,64,128]{2,1,0:T(8,128)(2,1)S(1)}, bf16[6,64,128]{2,1,0:T(8,128)(2,1)S(1)}, u32[]{:S(2)}, u32[]{:S(2)}) collective-permute-start(bf16[6,64,128]{2,1,0:T(8,128)(2,1)S(1)} %fusion.161), channel_id=1, source_target_pairs={{0,8},{8,16},{16,24},{24,32},{32,40},{40,48},{48,56},{56,64},{64,7... | collective-permute-start | bytes 294920 | tf_op jit(solution)/shard_map/while/body/eval_jaxpr/ppermute | solution.py:17
  249.7 7.5 %collective-permute-start = (bf16[6,64,128]{2,1,0:T(8,128)(2,1)S(1)}, bf16[6,64,128]{2,1,0:T(8,128)(2,1)S(1)}, u32[]{:S(2)}, u32[]{:S(2)}) collective-permute-start(bf16[6,64,128]{2,1,0:T(8,128)(2,1)S(1)} %fusion.161), channel_id=1, source_target_pairs={{0,8},{8,16},{16,24},{24,32},{32,40},{40,48},{48,56},{56,64},{64,7... | collective-permute-start | bytes 294920 | tf_op jit(solution)/shard_map/while/body/eval_jaxpr/ppermute | solution.py:17
  257.3 7.5 %collective-permute-start = (bf16[6,64,128]{2,1,0:T(8,128)(2,1)S(1)}, bf16[6,64,128]{2,1,0:T(8,128)(2,1)S(1)}, u32[]{:S(2)}, u32[]{:S(2)}) collective-permute-start(bf16[6,64,128]{2,1,0:T(8,128)(2,1)S(1)} %fusion.161), channel_id=1, source_target_pairs={{0,8},{8,16},{16,24},{24,32},{32,40},{40,48},{48,56},{56,64},{64,7... | collective-permute-start | bytes 294920 | tf_op jit(solution)/shard_map/while/body/eval_jaxpr/ppermute | solution.py:17
  264.9 8.6 %collective-permute-start = (bf16[6,64,128]{2,1,0:T(8,128)(2,1)S(1)}, bf16[6,64,128]{2,1,0:T(8,128)(2,1)S(1)}, u32[]{:S(2)}, u32[]{:S(2)}) collective-permute-start(bf16[6,64,128]{2,1,0:T(8,128)(2,1)S(1)} %fusion.161), channel_id=1, source_target_pairs={{0,8},{8,16},{16,24},{24,32},{32,40},{40,48},{48,56},{56,64},{64,7... | collective-permute-start | bytes 294920 | tf_op jit(solution)/shard_map/while/body/eval_jaxpr/ppermute | solution.py:17
  273.6 8.5 %collective-permute-start = (bf16[6,64,128]{2,1,0:T(8,128)(2,1)S(1)}, bf16[6,64,128]{2,1,0:T(8,128)(2,1)S(1)}, u32[]{:S(2)}, u32[]{:S(2)}) collective-permute-start(bf16[6,64,128]{2,1,0:T(8,128)(2,1)S(1)} %fusion.161), channel_id=1, source_target_pairs={{0,8},{8,16},{16,24},{24,32},{32,40},{40,48},{48,56},{56,64},{64,7... | collective-permute-start | bytes 294920 | tf_op jit(solution)/shard_map/while/body/eval_jaxpr/ppermute | solution.py:17
  282.2 8.4 %collective-permute-start = (bf16[6,64,128]{2,1,0:T(8,128)(2,1)S(1)}, bf16[6,64,128]{2,1,0:T(8,128)(2,1)S(1)}, u32[]{:S(2)}, u32[]{:S(2)}) collective-permute-start(bf16[6,64,128]{2,1,0:T(8,128)(2,1)S(1)} %fusion.161), channel_id=1, source_target_pairs={{0,8},{8,16},{16,24},{24,32},{32,40},{40,48},{48,56},{56,64},{64,7... | collective-permute-start | bytes 294920 | tf_op jit(solution)/shard_map/while/body/eval_jaxpr/ppermute | solution.py:17
  290.7 8.7 %collective-permute-start = (bf16[6,64,128]{2,1,0:T(8,128)(2,1)S(1)}, bf16[6,64,128]{2,1,0:T(8,128)(2,1)S(1)}, u32[]{:S(2)}, u32[]{:S(2)}) collective-permute-start(bf16[6,64,128]{2,1,0:T(8,128)(2,1)S(1)} %fusion.161), channel_id=1, source_target_pairs={{0,8},{8,16},{16,24},{24,32},{32,40},{40,48},{48,56},{56,64},{64,7... | collective-permute-start | bytes 294920 | tf_op jit(solution)/shard_map/while/body/eval_jaxpr/ppermute | solution.py:17
  299.6 8.6 %collective-permute-start = (bf16[6,64,128]{2,1,0:T(8,128)(2,1)S(1)}, bf16[6,64,128]{2,1,0:T(8,128)(2,1)S(1)}, u32[]{:S(2)}, u32[]{:S(2)}) collective-permute-start(bf16[6,64,128]{2,1,0:T(8,128)(2,1)S(1)} %fusion.161), channel_id=1, source_target_pairs={{0,8},{8,16},{16,24},{24,32},{32,40},{40,48},{48,56},{56,64},{64,7... | collective-permute-start | bytes 294920 | tf_op jit(solution)/shard_map/while/body/eval_jaxpr/ppermute | solution.py:17
  308.3 8.6 %collective-permute-start = (bf16[6,64,128]{2,1,0:T(8,128)(2,1)S(1)}, bf16[6,64,128]{2,1,0:T(8,128)(2,1)S(1)}, u32[]{:S(2)}, u32[]{:S(2)}) collective-permute-start(bf16[6,64,128]{2,1,0:T(8,128)(2,1)S(1)} %fusion.161), channel_id=1, source_target_pairs={{0,8},{8,16},{16,24},{24,32},{32,40},{40,48},{48,56},{56,64},{64,7... | collective-permute-start | bytes 294920 | tf_op jit(solution)/shard_map/while/body/eval_jaxpr/ppermute | solution.py:17
  317.1 8.6 %collective-permute-start = (bf16[6,64,128]{2,1,0:T(8,128)(2,1)S(1)}, bf16[6,64,128]{2,1,0:T(8,128)(2,1)S(1)}, u32[]{:S(2)}, u32[]{:S(2)}) collective-permute-start(bf16[6,64,128]{2,1,0:T(8,128)(2,1)S(1)} %fusion.161), channel_id=1, source_target_pairs={{0,8},{8,16},{16,24},{24,32},{32,40},{40,48},{48,56},{56,64},{64,7... | collective-permute-start | bytes 294920 | tf_op jit(solution)/shard_map/while/body/eval_jaxpr/ppermute | solution.py:17
  325.9 5.6 copy-start.11
  331.5 17.8 %copy-start.30 = (f32[384]{0:T(512)S(1)}, f32[384]{0:T(512)}, u32[]{:S(2)}) copy-start(f32[384]{0:T(512)} %param.41) | copy-start | bytes 4612
  349.3 5.1 copy-start.19
  349.3 8.5 %copy-start.25 = (s32[16]{0:T(128)S(1)}, s32[16]{0:T(128)}, u32[]{:S(2)}) copy-start(s32[16]{0:T(128)} %get-tuple-element.278) | copy-start | bytes 196
  349.3 8.5 %copy-start.23 = (s32[16]{0:T(128)S(1)}, s32[16]{0:T(128)}, u32[]{:S(2)}) copy-start(s32[16]{0:T(128)} %copy-done.22) | copy-start | bytes 196
  349.3 8.5 %copy-start.31 = (s32[16]{0:T(128)S(1)}, s32[16]{0:T(128)}, u32[]{:S(2)}) copy-start(s32[16]{0:T(128)} %param.53) | copy-start | bytes 196
  354.3 6.3 %copy-start.6 = (f32[16,6,64,128]{3,2,1,0:T(8,128)S(1)}, f32[16,6,64,128]{3,2,1,0:T(8,128)}, u32[]{:S(2)}) copy-start(f32[16,6,64,128]{3,2,1,0:T(8,128)} %get-tuple-element.154) | copy-start | bytes 9437188
  354.3 6.3 %copy-start.12 = (f32[6,64,128]{2,1,0:T(8,128)S(1)}, f32[6,64,128]{2,1,0:T(8,128)}, u32[]{:S(2)}) copy-start(f32[6,64,128]{2,1,0:T(8,128)} %copy-done.11) | copy-start | bytes 589828
  354.3 204.9 %reduce-scatter.7.cloned.1.call-start = ((), (), s32[]{:S(2)}) async-start(), calls=%async_computation.7 | async-start | bytes 1671168
  371.9 58.9 %copy-start.3 = (bf16[1024,1536]{1,0:T(8,128)(2,1)S(1)}, bf16[1024,1536]{1,0:T(8,128)(2,1)}, u32[]{:S(2)}) copy-start(bf16[1024,1536]{1,0:T(8,128)(2,1)} %all-gather.2.cloned.1.call-done) | copy-start | bytes 9437188
  375.4 61.0 %copy-start.21 = (f32[1536]{0:T(1024)S(1)}, f32[1536]{0:T(1024)}, u32[]{:S(2)}) copy-start(f32[1536]{0:T(1024)} %param.43) | copy-start | bytes 18436
  430.7 5.7 copy-start.8
  445.0 7.6 %copy-start.5 = (bf16[1024,1536]{1,0:T(8,128)(2,1)S(1)}, bf16[1024,1536]{1,0:T(8,128)(2,1)}, u32[]{:S(2)}) copy-start(bf16[1024,1536]{1,0:T(8,128)(2,1)} %copy-done.4) | copy-start | bytes 9437188
  445.0 7.6 %copy-start.16 = (bf16[1536,128]{1,0:T(8,128)(2,1)S(1)}, bf16[1536,128]{1,0:T(8,128)(2,1)}, u32[]{:S(2)}) copy-start(bf16[1536,128]{1,0:T(8,128)(2,1)} %param.44) | copy-start | bytes 1179652
  445.0 50.2 %all-to-all-start = ((bf16[16,4,16,1536]{3,2,1,0:T(8,128)(2,1)}), bf16[16,4,16,1536]{3,2,1,0:T(8,128)(2,1)}, u32[]{:S(2)}, u32[]{:S(2)}) async-start(bf16[16,4,16,1536]{3,2,1,0:T(8,128)(2,1)} %bitcast.253), calls=%async_computation.1 | async-start | bytes 6291456 | tf_op jit(solution)/shard_map/all_to_all | solution.py:239
  452.3 158.9 %reduce-scatter.5.cloned.1.call-start = ((), (), s32[]{:S(2)}) async-start(), calls=%async_computation.6 | async-start | bytes 3538944 | tf_op jit(solution)/shard_map/reduce_scatter | solution.py:219
  513.7 4.1 copy-start.24
  513.7 47.2 %all-to-all-start.1 = ((bf16[16,4,16,1536]{3,2,1,0:T(8,128)(2,1)}), bf16[16,4,16,1536]{3,2,1,0:T(8,128)(2,1)S(1)}, u32[]{:S(2)}, u32[]{:S(2)}) async-start(bf16[16,4,16,1536]{3,2,1,0:T(8,128)(2,1)} %copy.144), calls=%async_computation.2 | async-start | bytes 6291456 | tf_op jit(solution)/shard_map/all_to_all | solution.py:246
  564.7 48.6 %copy-start.1 = (bf16[384,1536]{1,0:T(8,128)(2,1)S(1)}, bf16[384,1536]{1,0:T(8,128)(2,1)}, u32[]{:S(2)}) copy-start(bf16[384,1536]{1,0:T(8,128)(2,1)} %param.42) | copy-start | bytes 3538948
  (6 other events, 14.2 us)
Sparse Core Ops, SparseCore 0:
  9.7 30.1 all-gather.1
  354.5 76.2 all-reduce.3
  434.0 125.2 reduce-scatter.6
  561.5 49.5 reduce-scatter.4
where the time goes:
time: 631 us; the launch traced here: 620 us
  waiting for transfers between devices  223 us (35%)
  local copies, waits for them, and re-layouts  103 us (16%)
  starting transfers between devices  103 us (16%)
  matrix products  78 us (12%)
  other arithmetic  56.7 us (9%)
  loops' own time  28.1 us (4%)
  between operations  16 us (3%)
  blocking collectives  12.4 us (2%)
    ppermute x16, starting transfers between devices, from_behind(): return lax.ppermute(block, axis, route)  91.2 us
    psum x1, waiting for transfers between devices, body(): lax.psum(mix_term.astype(jnp.bfloat16), 'exp').astype(jnp.float32)  55.3 us
    unnamed x5, waiting for transfers between devices  42 us
    reduce_scatter x1, waiting for transfers between devices, body(): lax.psum_scatter(jnp.dot(shared_hidden, sh_down, preferred_element_type=j...  36.3 us
    ppermute x16, waiting for transfers between devices, from_behind(): return lax.ppermute(block, axis, route)  36.1 us
    all_to_all x1, waiting for transfers between devices, body(): lax.all_to_all(outgoing, 'seq', split_axis=0, concat_axis=0, tiled=True)  34.5 us
    dynamic_update_slice x4, local copies, waits for them, and re-layouts, body(): lax.scan(block_step, (zero_state, zero_ends), blocks)  31.4 us
    another operation x2, loops' own time, block_step(): end_acc = lax.fori_loop(block_seg[0], last_seg + 1, close_request, end_acc)  23.4 us
  transfers between devices with their start and end apart: 22, of which 20 were waited for; matrix products, arithmetic and copies ran while one was open for 15% of the time, Pallas kernels for 0%

commit v1 on v0

v1 whole, which is shorter than its diff:
```python
import functools

import jax
import jax.numpy as jnp
from jax import lax
from jax.experimental import pallas as pl
from jax.experimental.pallas import tpu as pltpu
from jax.sharding import PartitionSpec as P

EPS = 1e-05
HIGH = lax.Precision.HIGHEST
F32 = jnp.float32
BF16 = jnp.bfloat16
LANES = 128
ROWS = 128
CHUNK = 128
CAP = 16
HEADS = 6
HALF = 64
WIDE = 384
STATE = 128
DI = 3072
VM = pl.BlockSpec(memory_space=pltpu.VMEM)
SM = pl.BlockSpec(memory_space=pltpu.SMEM)
PLUS = [(i, (i + 2) % 8) for i in range(8)]
MINUS = [(i, (i + 6) % 8) for i in range(8)]
MATE = [(i, i ^ 1) for i in range(8)]


def silu(v):
    return v * (1.0 / (1.0 + jnp.exp(-v)))


def ahead(block, distance):
    return lax.ppermute(block, "seq", [(i, i + distance) for i in range(16 - distance)])


def over_exp(block, route):
    return lax.ppermute(block, "exp", route)


def spread(cols):
    rows = cols.shape[0]
    left = lax.broadcasted_iota(jnp.int32, (rows, LANES), 1) < HALF
    parts = []
    for pair in range(HEADS // 2):
        first = jnp.broadcast_to(cols[:, 2 * pair : 2 * pair + 1], (rows, LANES))
        second = jnp.broadcast_to(cols[:, 2 * pair + 1 : 2 * pair + 2], (rows, LANES))
        parts.append(jnp.where(left, first, second))
    return jnp.concatenate(parts, axis=1)


def gather_exp(own):
    half = own.shape[0] // 2
    up = over_exp(own, PLUS)
    down = over_exp(own, MINUS)
    mate = over_exp(own, MATE)
    far_a = over_exp(up[:half], PLUS)
    far_b = over_exp(down[half:], MINUS)
    up_mate = over_exp(up, MATE)
    down_mate = over_exp(down, MATE)
    far = jnp.concatenate([far_a, far_b])
    far_mate = over_exp(far, MATE)
    return (own, mate, up, up_mate, down, down_mate, far, far_mate)


def project_kernel(where_ref, b0, b1, b2, b3, b4, b5, b6, b7, gain, w_conv, w_dt, w_z, bias, conv_out, step_out, z_out, normed):
    chip = where_ref[0] // 2
    core = lax.rem(where_ref[0], 2)
    for slot, (pair, offset) in enumerate((((b0, b1), 0), ((b2, b3), 3), ((b4, b5), 1), ((b6, b7), 2))):
        for ref, place in ((pair[0], core), (pair[1], 1 - core)):
            vals = ref[...].astype(F32)
            meansq = jnp.mean(vals * vals, axis=-1, keepdims=True)
            start = pl.multiple_of(place * ROWS, ROWS)
            normed[pl.ds(start, ROWS), :] = (vals * lax.rsqrt(meansq + EPS) * gain[...]).astype(BF16)
        rows = normed[...]
        start = pl.multiple_of(lax.rem(chip + offset, 4) * (2 * ROWS), 2 * ROWS)
        conv_out[pl.ds(start, 2 * ROWS), :] = jnp.dot(rows, w_conv[...], preferred_element_type=F32).astype(BF16)
        raw = jnp.dot(rows, w_dt[...], preferred_element_type=F32).astype(BF16).astype(F32) + bias[...]
        step_out[pl.ds(start, 2 * ROWS), :] = jnp.maximum(raw, 0.0) + jnp.log1p(jnp.exp(-jnp.abs(raw)))
        gate = jnp.dot(rows, w_z[...], preferred_element_type=F32).astype(BF16).astype(F32)
        z_out[pl.ds(start, 2 * ROWS), :] = silu(gate)


def scan_kernel(meta, conv_in, edge, keep, seg_col, step_in, rate, w_conv, x_out, bc_out, cum_out, lead_out, state_out, send_out, state):
    state[...] = jnp.zeros_like(state)
    rows_i = lax.broadcasted_iota(jnp.int32, (CHUNK, CHUNK), 0)
    cols_i = lax.broadcasted_iota(jnp.int32, (CHUNK, CHUNK), 1)
    lower = (rows_i >= cols_i).astype(F32)
    before_dev = meta[0]

    def chunk(c, past):
        start = pl.multiple_of(c * CHUNK, CHUNK)
        prior_at = pl.multiple_of(jnp.maximum(start - 16, 0), 16)
        prior = jnp.where(c == 0, edge[...].astype(F32), conv_in[pl.ds(prior_at, 16), :].astype(F32))
        here = conv_in[pl.ds(start, CHUNK), :].astype(F32)
        joined = jnp.concatenate([prior, here], axis=0)
        kept = keep[pl.ds(start, CHUNK), :]
        total = here * w_conv[3:4, :]
        for lag in (1, 2, 3):
            moved = pltpu.roll(joined, lag, 0)[16:, :]
            total = total + (kept[:, lag : lag + 1] * moved) * w_conv[3 - lag : 4 - lag, :]
        mixed = silu(total).astype(BF16)
        x_out[pl.ds(start, CHUNK), :] = mixed[:, :WIDE]
        bc_out[pl.ds(start, CHUNK), :] = mixed[:, WIDE:]
        step = step_in[pl.ds(start, CHUNK), :]
        decay = -step * rate[...]
        cum = jnp.dot(lower, decay, precision=HIGH, preferred_element_type=F32)
        cum_out[pl.ds(start, CHUNK), :] = cum
        seg = seg_col[pl.ds(start, CHUNK), :]
        lead_out[pl.ds(start, CHUNK), :] = jnp.where(seg == before_dev, jnp.exp(past + cum), 0.0)
        last = cum[CHUNK - 1 : CHUNK, :]
        last_seg = meta[8 + 8 + c]
        tail = jnp.where(seg == last_seg, jnp.exp(last - cum), 0.0)
        drive = mixed[:, :WIDE].astype(F32) * spread(step * tail)
        fresh = lax.dot_general(
            mixed[:, WIDE : WIDE + STATE], drive.astype(BF16), (((0,), (0,)), ((), ())), preferred_element_type=F32
        )
        held = state[...]
        state_out[c] = held.astype(BF16)
        persist = jnp.where(last_seg == meta[8 + c], jnp.exp(last), 0.0)
        state[...] = spread(jnp.broadcast_to(persist, (8, LANES)))[:1, :] * held + fresh
        return past + last

    past = lax.fori_loop(0, 8, chunk, jnp.zeros((1, LANES), F32))
    send_out[:STATE, :] = state[...].astype(BF16)
    passed = jnp.where(meta[8 + 8 + 7] == before_dev, jnp.exp(past), 0.0)
    wide = spread(jnp.broadcast_to(passed, (16, LANES)))
    high = wide.astype(BF16)
    low = (wide - high.astype(F32)).astype(BF16)
    row = lax.broadcasted_iota(jnp.int32, (16, WIDE), 0)
    send_out[STATE:, :] = jnp.where(row == 0, high, low)


def local_kernel(meta, x_in, bc_in, cum_in, step_in, seg_col, seg_row, state_in, skip, y_out, ends_out):
    rows_i = lax.broadcasted_iota(jnp.int32, (CHUNK, CHUNK), 0)
    cols_i = lax.broadcasted_iota(jnp.int32, (CHUNK, CHUNK), 1)
    causal = rows_i >= cols_i
    left = lax.broadcasted_iota(jnp.int32, (CHUNK, LANES), 1) < HALF

    def chunk(c, carry):
        start = pl.multiple_of(c * CHUNK, CHUNK)
        x = x_in[pl.ds(start, CHUNK), :].astype(F32)
        bc = bc_in[pl.ds(start, CHUNK), :]
        b_rows, c_rows = bc[:, :STATE], bc[:, STATE:]
        cum = cum_in[pl.ds(start, CHUNK), :]
        cum_t = cum.T
        seg = seg_col[pl.ds(start, CHUNK), :]
        mask = causal & (seg == seg_row[pl.ds(c, 1), :])
        scores = lax.dot_general(c_rows, b_rows, (((1,), (1,)), ((), ())), preferred_element_type=F32)
        scores = jnp.where(mask, scores, 0.0)
        drive = x * spread(step_in[pl.ds(start, CHUNK), :])
        drive_b = drive.astype(BF16)
        held = state_in[c]
        before = meta[8 + c]
        entry = jnp.where(seg == before, jnp.exp(cum), 0.0)
        carried = jnp.dot(c_rows, held, preferred_element_type=F32)
        total = spread(entry) * carried + skip[...] * x
        parts = []
        for pair in range(HEADS // 2):
            block = drive_b[:, pair * LANES : (pair + 1) * LANES]
            zero = jnp.zeros_like(block)
            acc = None
            for side in (0, 1):
                head = 2 * pair + side
                gap = jnp.minimum(cum[:, head : head + 1] - cum_t[head : head + 1, :], 0.0)
                weights = (scores * jnp.exp(gap)).astype(BF16)
                value = jnp.where(left, block, zero) if side == 0 else jnp.where(left, zero, block)
                term = jnp.dot(weights, value, preferred_element_type=F32)
                acc = term if acc is None else acc + term
            parts.append(acc)
        y_out[pl.ds(start, CHUNK), :] = total + jnp.concatenate(parts, axis=1)
        held_f = held.astype(F32)

        def close(req, inner):
            at = meta[32 + req] - start

            @pl.when((at >= 0) & (at < CHUNK))
            def _():
                cum_end = cum_in[pl.ds(start + at, 1), :]
                weight = jnp.where(seg == req, jnp.exp(jnp.minimum(cum_end - cum, 0.0)), 0.0)
                fresh = lax.dot_general(
                    b_rows, (drive * spread(weight)).astype(BF16), (((0,), (0,)), ((), ())), preferred_element_type=F32
                )
                hold = jnp.where(req == before, jnp.exp(cum_end), 0.0)
                hold = spread(jnp.broadcast_to(hold, (8, LANES)))[:1, :]
                ends_out[meta[48 + req]] = (fresh + hold * held_f).astype(BF16)

            return inner

        lax.fori_loop(meta[24 + c], meta[8 + 8 + c] + 1, close, 0)
        return carry

    lax.fori_loop(0, 8, chunk, 0)


def out_kernel(where_ref, y_in, bc_in, lead_in, z_in, state_in, norm_gain, w_out, out, gated, squares, *, mate):
    chip = where_ref[0] // 2
    core = lax.rem(where_ref[0], 2)
    if mate:
        core = 1 - core
    for rel in range(4):
        start = pl.multiple_of((lax.rem(chip + rel, 4) * 2 + core) * ROWS, ROWS)
        c_rows = bc_in[pl.ds(start, ROWS), STATE:]
        carried = jnp.dot(c_rows, state_in[...], preferred_element_type=F32)
        y = y_in[pl.ds(start, ROWS), :] + spread(lead_in[pl.ds(start, ROWS), :]) * carried
        g = y * z_in[pl.ds(start, ROWS), :]
        out[rel, :, 1536:] = jnp.broadcast_to(jnp.sum(g * g, axis=1, keepdims=True), (ROWS, LANES)).astype(BF16)
        gated[rel * ROWS : (rel + 1) * ROWS, :] = (g * norm_gain[...]).astype(BF16)
    for rel in range(4):
        out[rel, :, :1536] = jnp.dot(
            gated[rel * ROWS : (rel + 1) * ROWS, :], w_out[...], preferred_element_type=F32
        ).astype(BF16)


def enter_kernel(h0, p_a, p_b, q_a, q_b, tokens, gain, spots, residual_out, normed_out, outgoing):
    first = h0[:HALF, :] + p_b[:HALF, :].astype(F32) + q_a[...].astype(F32)
    second = h0[HALF:, :] + p_a[HALF:, :].astype(F32) + q_b[...].astype(F32)
    both = jnp.concatenate([first, second], axis=0)
    scale = lax.rsqrt(both[:, 1536:1537] * (1.0 / DI) + EPS)
    residual = tokens[...].astype(F32) + both[:, :1536] * scale
    residual_out[...] = residual
    meansq = jnp.mean(residual * residual, axis=-1, keepdims=True)
    normed = (residual * lax.rsqrt(meansq + EPS) * gain[...]).astype(BF16)
    normed_out[...] = normed
    outgoing[...] = jnp.dot(spots[...], normed, preferred_element_type=F32).astype(BF16)


def expert_kernel(rows_ref, gate, up, down, out):
    rows = rows_ref[...].reshape(256, 1536)
    g = jnp.dot(rows, gate[...], preferred_element_type=F32)
    u = jnp.dot(rows, up[...], preferred_element_type=F32)
    hidden = (silu(g) * u).astype(BF16)
    out[...] = jnp.dot(hidden, down[...], preferred_element_type=F32).astype(BF16).reshape(16, CAP, 1536)


def shared_kernel(rows_ref, w0, w1, w2, w3, w4, w5, w6, w7, residual, out):
    rows = rows_ref[...]
    total = residual[...]
    for w in (w0, w1, w2, w3, w4, w5, w6, w7):
        both = lax.dot_general(rows, w[:256, :], (((1,), (1,)), ((), ())), preferred_element_type=F32)
        hidden = (silu(both[:, :128]) * both[:, 128:]).astype(BF16)
        total = total + jnp.dot(hidden, w[256:, :], preferred_element_type=F32)
    out[...] = total


def leave_kernel(returned, high, low, base, out):
    rows = returned[...]
    routed = jnp.dot(high[...], rows, preferred_element_type=F32) + jnp.dot(low[...], rows, preferred_element_type=F32)
    out[...] = (base[...] + routed).astype(BF16)


def shape(dims, dtype):
    return jax.ShapeDtypeStruct(dims, dtype)


def body(
    tokens,
    in_gain,
    in_z,
    in_x,
    in_bc,
    in_dt,
    conv_x,
    conv_bc,
    dt_bias,
    a_log,
    d_skip,
    norm_gain,
    out_w,
    post_gain,
    sh_gate,
    sh_up,
    sh_down,
    ex_gate,
    ex_up,
    ex_down,
    routes,
    gates,
    lengths,
    cache_slot,
):
    seq_idx = lax.axis_index("seq")
    exp_idx = lax.axis_index("exp")
    where_am_i = jnp.reshape(exp_idx, (1,)).astype(jnp.int32)
    width = tokens.shape[1]
    row_count = 8 * ROWS
    pad_heads = ((0, LANES - HEADS),)

    blocks = gather_exp(tokens)

    reqs = jnp.arange(16, dtype=jnp.int32)
    ends = jnp.sum(jnp.where(reqs[:, None] >= reqs[None, :], lengths[None, :], 0), axis=1)
    stream_start = (seq_idx * row_count).astype(jnp.int32)

    def seg_at(positions):
        found = jnp.sum((positions[..., None] >= ends).astype(jnp.int32), axis=-1)
        return jnp.where(positions >= 0, found, -1)

    local = jnp.arange(row_count, dtype=jnp.int32)
    segment = seg_at(stream_start + local)
    seg_col = segment[:, None]
    seg_row = segment.reshape(8, CHUNK)
    keep = jnp.stack(
        [(seg_at(stream_start + local - lag) == segment).astype(F32) for lag in range(4)], axis=1
    )
    bases = stream_start + CHUNK * jnp.arange(8, dtype=jnp.int32)
    before = seg_at(bases - 1)
    meta = jnp.concatenate(
        [before, before, seg_at(bases + CHUNK - 1), seg_at(bases), ends - 1 - stream_start, cache_slot]
    ).astype(jnp.int32)
    before_dev = before[0]

    picks = (routes[:, :, None] == jnp.arange(64, dtype=jnp.int32)).astype(F32)
    named = jnp.sum(picks, axis=1)
    weight = jnp.sum(picks * gates[:, :, None], axis=1)
    earlier = (jnp.arange(ROWS)[:, None] > jnp.arange(ROWS)[None, :]).astype(BF16)
    rank = jnp.dot(earlier, named.astype(BF16), preferred_element_type=F32)
    rank = jnp.where(named > 0, rank, -1.0)
    slots = jnp.arange(1024, dtype=jnp.int32)
    fan = (slots[None, :] // CAP == jnp.arange(64, dtype=jnp.int32)[:, None]).astype(BF16)
    rank_wide = jnp.dot(rank.astype(BF16), fan, preferred_element_type=F32)
    hit = rank_wide == (slots % CAP).astype(F32)[None, :]
    w_high = weight.astype(BF16)
    w_low = (weight - w_high.astype(F32)).astype(BF16)
    mix_high = jnp.where(hit, jnp.dot(w_high, fan, preferred_element_type=F32), 0.0).astype(BF16)
    mix_low = jnp.where(hit, jnp.dot(w_low, fan, preferred_element_type=F32), 0.0).astype(BF16)
    spots = hit.astype(BF16).T

    w_conv_in = jnp.concatenate([in_x, in_bc], axis=1)
    w_dt = jnp.pad(in_dt, ((0, 0),) + pad_heads)
    bias = jnp.pad(dt_bias, pad_heads)[None, :]
    rate = jnp.pad(jnp.exp(a_log), pad_heads)[None, :]
    taps = jnp.concatenate([conv_x, conv_bc], axis=1)
    skip = jnp.repeat(d_skip, HALF)[None, :]

    conv_in, step, z = pl.pallas_call(
        project_kernel,
        out_shape=(shape((row_count, 640), BF16), shape((row_count, LANES), F32), shape((row_count, WIDE), F32)),
        in_specs=[SM] + [VM] * 13,
        out_specs=(VM, VM, VM),
        scratch_shapes=[pltpu.VMEM((2 * ROWS, width), BF16)],
        name="project",
    )(where_am_i, *blocks, in_gain[None, :], w_conv_in, w_dt, in_z, bias)

    edge = ahead(conv_in[row_count - 16 :], 1)
    x_rows, bc_rows, cum, lead, states, sent = pl.pallas_call(
        scan_kernel,
        out_shape=(
            shape((row_count, WIDE), BF16),
            shape((row_count, 2 * STATE), BF16),
            shape((row_count, LANES), F32),
            shape((row_count, LANES), F32),
            shape((8, STATE, WIDE), BF16),
            shape((STATE + 16, WIDE), BF16),
        ),
        in_specs=[SM] + [VM] * 7,
        out_specs=(VM,) * 6,
        scratch_shapes=[pltpu.VMEM((STATE, WIDE), F32)],
        name="scan",
    )(meta, conv_in, edge, keep, seg_col, step, rate, taps)

    def split(message):
        factor = message[STATE : STATE + 1].astype(F32) + message[STATE + 1 : STATE + 2].astype(F32)
        return message[:STATE].astype(F32), factor

    def joined(state, factor):
        high = factor.astype(BF16)
        low = (factor - high.astype(F32)).astype(BF16)
        return jnp.concatenate([state.astype(BF16), high, low, jnp.zeros((14, WIDE), BF16)])

    got = ahead(sent, 1)
    y_local, ends_local = pl.pallas_call(
        local_kernel,
        out_shape=(shape((row_count, WIDE), F32), shape((16, STATE, WIDE), BF16)),
        in_specs=[SM] + [VM] * 8,
        out_specs=(VM, VM),
        name="local",
    )(meta, x_rows, bc_rows, cum, step, seg_col, seg_row, states, skip)
    own_state, own_factor = split(sent)
    got_state, got_factor = split(got)
    two = joined(own_state + own_factor * got_state, own_factor * got_factor)
    near_state, near_factor = split(ahead(two, 1))
    entering = near_state + near_factor * ahead(two[:STATE], 3).astype(F32)
    entering_b = entering.astype(BF16)

    open_req = jnp.maximum(before_dev, 0)
    open_end = meta[32 + open_req]
    holds = (before_dev >= 0) & (open_end >= 0) & (open_end < row_count)
    hold_row = lax.dynamic_slice_in_dim(lead, jnp.clip(open_end, 0, row_count - 1), 1, 0)
    hold_row = jnp.where(holds, jnp.repeat(hold_row[:, :HEADS], HALF, axis=1), 0.0)
    open_slot = cache_slot[open_req]
    open_value = lax.dynamic_index_in_dim(ends_local, open_slot, 0, False).astype(F32)
    open_value = jnp.where(holds, open_value + hold_row * entering, open_value).astype(BF16)
    ends_local = lax.dynamic_update_index_in_dim(ends_local, open_value, open_slot, 0)
    ends_all = lax.all_to_all(ends_local, "seq", split_axis=0, concat_axis=0, tiled=True)
    my_req = jnp.sum(jnp.where(cache_slot == seq_idx, reqs, 0))
    source = (ends[my_req] - 1) // row_count
    final = lax.dynamic_index_in_dim(ends_all, source, 0, False).astype(F32)
    state_cache = final.T.reshape(1, HEADS, HALF, STATE)

    def project_out(mate):
        return pl.pallas_call(
            functools.partial(out_kernel, mate=mate),
            out_shape=shape((4, ROWS, width + LANES), BF16),
            in_specs=[SM] + [VM] * 7,
            out_specs=VM,
            scratch_shapes=[pltpu.VMEM((4 * ROWS, WIDE), BF16), pltpu.VMEM((8, LANES), F32)],
            name="out_mate" if mate else "out_own",
        )(where_am_i, y_local, bc_rows, lead, z, entering_b, norm_gain[None, :], out_w)

    swapped = over_exp(project_out(True), MATE)
    summed = project_out(False).astype(F32) + swapped.astype(F32)
    h0, h1, h2, h3 = summed[0], summed[1], summed[2], summed[3]
    p_a = over_exp(jnp.concatenate([h2[:HALF], h1[HALF:]]).astype(BF16), PLUS)
    p_b = over_exp(jnp.concatenate([h3[:HALF], h2[HALF:]]).astype(BF16), MINUS)
    q_a = over_exp((h1[:HALF] + p_a[:HALF].astype(F32)).astype(BF16), PLUS)
    q_b = over_exp((h3[HALF:] + p_b[HALF:].astype(F32)).astype(BF16), MINUS)

    residual, normed, outgoing = pl.pallas_call(
        enter_kernel,
        out_shape=(shape((ROWS, width), F32), shape((ROWS, width), BF16), shape((1024, width), BF16)),
        in_specs=[VM] * 8,
        out_specs=(VM, VM, VM),
        name="enter",
    )(h0, p_a, p_b, q_a, q_b, tokens, post_gain[None, :], spots)

    received = lax.all_to_all(
        outgoing.reshape(16, 4, CAP, width), "seq", split_axis=0, concat_axis=0, tiled=True
    )
    packed = jnp.concatenate([sh_gate.T, sh_up.T, sh_down])
    packed, normed = lax.optimization_barrier((packed, normed))
    groups = gather_exp(packed)
    base = pl.pallas_call(
        shared_kernel,
        out_shape=shape((ROWS, width), F32),
        in_specs=[VM] * 10,
        out_specs=VM,
        name="shared",
    )(normed, *groups, residual)
    answers = pl.pallas_call(
        expert_kernel,
        out_shape=shape((16, 4, CAP, width), BF16),
        grid=(4,),
        in_specs=[
            pl.BlockSpec((16, None, CAP, width), lambda e: (0, e, 0, 0)),
            pl.BlockSpec((None, width, 512), lambda e: (e, 0, 0)),
            pl.BlockSpec((None, width, 512), lambda e: (e, 0, 0)),
            pl.BlockSpec((None, 512, width), lambda e: (e, 0, 0)),
        ],
        out_specs=pl.BlockSpec((16, None, CAP, width), lambda e: (0, e, 0, 0)),
        name="experts",
    )(received, ex_gate, ex_up, ex_down)
    returned = lax.all_to_all(answers, "seq", split_axis=0, concat_axis=0, tiled=True)
    layer_out = pl.pallas_call(
        leave_kernel,
        out_shape=shape((ROWS, width), BF16),
        in_specs=[VM] * 4,
        out_specs=VM,
        name="leave",
    )(returned.reshape(1024, width), mix_high, mix_low, base)
    return (layer_out, state_cache)


def solution(mesh):
    placed = (
        P(("seq", "exp"), None),
        P(),
        P(None, "exp"),
        P(None, "exp"),
        P(),
        P(None, "exp"),
        P(None, "exp"),
        P(),
        P("exp"),
        P("exp"),
        P("exp"),
        P("exp"),
        P("exp", None),
        P(),
        P(None, "exp"),
        P(None, "exp"),
        P("exp", None),
        P("seq", None, None),
        P("seq", None, None),
        P("seq", None, None),
        P(("seq", "exp"), None),
        P(("seq", "exp"), None),
        P(),
        P(),
    )
    return jax.shard_map(
        body,
        mesh=mesh,
        in_specs=placed,
        out_specs=(P(("seq", "exp"), None), P("seq", "exp", None, None)),
        check_vma=False,
    )
```

time: 631 us -> 258 us (0.41); the launches traced: 620 us -> 256 us
  waiting for transfers between devices: 223 us -> 71.4 us
  local copies, waits for them, and re-layouts: 103 us -> 27.5 us
  matrix products: 78 us -> 3.17 us
  Pallas kernels: 0 us -> 66.9 us
  starting transfers between devices: 103 us -> 59.1 us
  other arithmetic: 56.7 us -> 20.5 us
  loops' own time: 28.1 us -> 0 us
  blocking collectives: 12.4 us -> 0 us
  between operations: 16 us -> 7.22 us
    dot_general x22 -> x3, matrix products: 78 us -> 3.17 us  [the longest x1 1.25 us: body(): rank_wide = jnp.dot(rank.astype(BF16), fan, preferred_element_type=F32)]
    pallas_call x0 -> x9, Pallas kernels: none -> 66.9 us  [the longest x1 11.4 us: body(): pl.pallas_call(expert_kernel, out_shape=shape((16, 4, CAP, width), BF16),...]
    psum x1 -> x0, waiting for transfers between devices: 55.3 us -> none  [body(): lax.psum(mix_term.astype(jnp.bfloat16), 'exp').astype(jnp.float32)]
    ppermute x16 -> x25, starting transfers between devices: 91.2 us -> 41.2 us  [the longest x21 20.8 us: over_exp(): return lax.ppermute(block, 'exp', route)]
    unnamed x5 -> x0, waiting for transfers between devices: 42 us -> none
    reduce_scatter x1 -> x0, waiting for transfers between devices: 36.3 us -> none  [body(): lax.psum_scatter(jnp.dot(shared_hidden, sh_down, preferred_element_type=j...]
    dynamic_update_slice x4 -> x0, local copies, waits for them, and re-layouts: 31.4 us -> none  [body(): lax.scan(block_step, (zero_state, zero_ends), blocks)]
    another operation x4 -> x0, loops' own time: 28.1 us -> none  [the longest x2 23.4 us: block_step(): end_acc = lax.fori_loop(block_seg[0], last_seg + 1, close_request, end_acc)]
  transfers between devices with their start and end apart: 22 -> 28, of which waited for: 20 -> 12; matrix products, arithmetic and copies ran while one was open for 15% -> 15% of each run, Pallas kernels for 0% -> 13%
where the time goes in v1:
time: 258 us; the launch traced here: 256 us
  waiting for transfers between devices  71.4 us (28%)
  Pallas kernels  66.9 us (26%)
  starting transfers between devices  59.1 us (23%)
  local copies, waits for them, and re-layouts  27.5 us (11%)
  other arithmetic  20.5 us (8%)
  between operations  7.22 us (3%)
  matrix products  3.17 us (1%)
    all_to_all x1, waiting for transfers between devices, body(): lax.all_to_all(outgoing.reshape(16, 4, CAP, width), 'seq', split_axis=0,...  34.1 us
    ppermute x21, waiting for transfers between devices, over_exp(): return lax.ppermute(block, 'exp', route)  28.9 us
    ppermute x21, starting transfers between devices, over_exp(): return lax.ppermute(block, 'exp', route)  20.8 us
    ppermute x4, starting transfers between devices, ahead(): lax.ppermute(block, 'seq', [(i, i + distance) for i in range(16 - distanc...  20.4 us
    pallas_call x1, Pallas kernels, body(): pl.pallas_call(expert_kernel, out_shape=shape((16, 4, CAP, width), BF16),...  11.4 us
    pallas_call x1, Pallas kernels, body(): pl.pallas_call(project_kernel, out_shape=(shape((row_count, 640), BF16),...  10.2 us
    pallas_call x2, Pallas kernels, project_out(): pl.pallas_call(functools.partial(out_kernel, mate=mate), out_shape=shape(...  9.97 us
    pallas_call x1, Pallas kernels, body(): pl.pallas_call(local_kernel, out_shape=(shape((row_count, WIDE), F32), sh...  9.64 us
  transfers between devices with their start and end apart: 28, of which 12 were waited for; matrix products, arithmetic and copies ran while one was open for 15% of the time, Pallas kernels for 13%

profile of v1, /device:TPU:0, one launch (start us, length us, event | category | flops | bytes accessed | tf_op | source)
XLA Modules:
  0.0 255.8 jit_solution(14208448590005661673)
XLA Ops:
  0.6 1.8 collective-permute-start.1
  2.4 1.5 collective-permute-start.3
  10.5 2.7 %collective-permute-done.1.b2 = bf16[128,1536]{1,0:T(8,128)(2,1)S(1)} collective-permute-done((bf16[128,1536]{1,0:T(8,128)(2,1)}, bf16[128,1536]{1,0:T(8,128)(2,1)S(1)}, u32[]{:S(2)}, u32[]{:S(2)}) %collective-permute-start.1) | collective-permute-done | bytes 393248 | tf_op jit(solution)/shard_map/ppermute | solution.py:39
  13.6 3.0 %collective-permute-start.6 = (bf16[64,1536]{1,0:T(8,128)(2,1)S(1)}, bf16[64,1536]{1,0:T(8,128)(2,1)S(1)}, u32[]{:S(2)}, u32[]{:S(2)}) collective-permute-start(bf16[64,1536]{1,0:T(8,128)(2,1)S(1)} %slice.138), channel_id=1, source_target_pairs={{0,6},{1,7},{2,0},{3,1},{4,2},{5,3},{6,4},{7,5},{8,14},{9,15},{10,... | collective-permute-start | bytes 589832 | tf_op jit(solution)/shard_map/ppermute | solution.py:39
  17.1 3.3 %collective-permute-done.5 = bf16[64,1536]{1,0:T(8,128)(2,1)S(1)} collective-permute-done((bf16[64,1536]{1,0:T(8,128)(2,1)S(1)}, bf16[64,1536]{1,0:T(8,128)(2,1)S(1)}, u32[]{:S(2)}, u32[]{:S(2)}) %collective-permute-start.5) | collective-permute-done | bytes 196640 | tf_op jit(solution)/shard_map/ppermute | solution.py:39
  21.1 2.6 %pad_maximum_fusion.w_conv = bf16[1536,640]{1,0:T(8,128)(2,1)} fusion(bf16[1536,256]{1,0:T(8,128)(2,1)} %param.28, bf16[1536,384]{1,0:T(8,128)(2,1)S(1)} %copy-done.4), kind=kLoop, calls=%fused_computation.1 | loop fusion | flops 3932160 | bytes 3932160 | tf_op jit(solution)/shard_map/concatenate | solution.py:330
  24.8 10.2 %project.1 = (bf16[1024,640]{1,0:T(8,128)(2,1)}, f32[1024,128]{1,0:T(8,128)}, f32[1024,384]{1,0:T(8,128)}) custom-call(s32[1]{0:T(128)} %bitcast.where_ref, bf16[128,1536]{1,0:T(8,128)(2,1)} %tokens.1, bf16[128,1536]{1,0:T(8,128)(2,1)} %collective-permute-done.b1, bf16[128,1536]{1,0:T(8,128)(2,1)} %copy-done.5, bf16[128,1536]{1,0:T(8,128)(2,1)} %copy-done.8, ...), custom_call_target="tpu_custom_call" | custom-call | tf_op jit(solution)/shard_map/project/pallas_call | solution.py:337
  35.8 3.7 %collective-permute-start.8 = (bf16[16,640]{1,0:T(8,128)(2,1)S(1)}, bf16[16,640]{1,0:T(8,128)(2,1)S(1)}, u32[]{:S(2)}, u32[]{:S(2)}) collective-permute-start(bf16[16,640]{1,0:T(8,128)(2,1)S(1)} %slice.108), channel_id=1, source_target_pairs={{0,8},{8,16},{16,24},{24,32},{32,40},{40,48},{48,56},{56,64},{64,7... | collective-permute-start | bytes 61448 | tf_op jit(solution)/shard_map/ppermute | solution.py:35
  40.1 1.0 copy.67.keep
  42.3 8.6 %scan.1 = (bf16[1024,384]{1,0:T(8,128)(2,1)}, bf16[1024,256]{1,0:T(8,128)(2,1)}, f32[1024,128]{1,0:T(8,128)}, f32[1024,128]{1,0:T(8,128)}, bf16[8,128,384]{2,1,0:T(8,128)(2,1)}, /*index=5*/bf16[144,384]{1,0:T(8,128)(2,1)}) custom-call(s32[64]{0:T(128)} %concatenate.29.meta, bf16[1024,640]{1,0:T(8,128)(2,1)} %get-tuple-element.18.conv_in, ...), custom_call_target="tpu_custom_call" | custom-call | tf_op jit(solution)/shard_map/scan/pallas_call | solution.py:347
  50.9 3.8 %collective-permute-start.9 = (bf16[144,384]{1,0:T(8,128)(2,1)}, bf16[144,384]{1,0:T(8,128)(2,1)S(1)}, u32[]{:S(2)}, u32[]{:S(2)}) collective-permute-start(bf16[144,384]{1,0:T(8,128)(2,1)} %get-tuple-element.27), channel_id=1, source_target_pairs={{0,8},{8,16},{16,24},{24,32},{32,40},{40,48},{48,56},{56,64},{64,7... | collective-permute-start | bytes 331784 | tf_op jit(solution)/shard_map/ppermute | solution.py:35
  54.8 2.9 %collective-permute-done.9 = bf16[144,384]{1,0:T(8,128)(2,1)S(1)} collective-permute-done((bf16[144,384]{1,0:T(8,128)(2,1)}, bf16[144,384]{1,0:T(8,128)(2,1)S(1)}, u32[]{:S(2)}, u32[]{:S(2)}) %collective-permute-start.9) | collective-permute-done | bytes 110624 | tf_op jit(solution)/shard_map/ppermute | solution.py:35
  59.6 4.5 %collective-permute-start.10 = (bf16[144,384]{1,0:T(8,128)(2,1)S(1)}, bf16[144,384]{1,0:T(8,128)(2,1)S(1)}, u32[]{:S(2)}, u32[]{:S(2)}) collective-permute-start(bf16[144,384]{1,0:T(8,128)(2,1)S(1)} %maximum_maximum_fusion), channel_id=1, source_target_pairs={{0,8},{8,16},{16,24},{24,32},{32,40},{40,48},{48,56},{56,64},{64,7... | collective-permute-start | bytes 331784 | tf_op jit(solution)/shard_map/ppermute | solution.py:35
  65.9 9.6 %local.1 = (f32[1024,384]{1,0:T(8,128)}, bf16[16,128,384]{2,1,0:T(8,128)(2,1)}) custom-call(s32[64]{0:T(128)} %concatenate.29.meta, bf16[1024,384]{1,0:T(8,128)(2,1)} %get-tuple-element.20.x_in, bf16[1024,256]{1,0:T(8,128)(2,1)} %get-tuple-element.21.bc_in, f32[1024,128]{1,0:T(8,128)} %get-tuple-element.22.cum_in, f32[1024,128]{1,0:T(8,128)} %get-tuple-element.19.step_in, ...), custom_call_target="tpu_custom_call" | custom-call | tf_op jit(solution)/shard_map/local/pallas_call | solution.py:373
  75.6 8.4 %collective-permute-start.11 = (bf16[128,384]{1,0:T(8,128)(2,1)S(1)}, bf16[128,384]{1,0:T(8,128)(2,1)S(1)}, u32[]{:S(2)}, u32[]{:S(2)}) collective-permute-start(bf16[128,384]{1,0:T(8,128)(2,1)S(1)} %add_convert_fusion), channel_id=1, source_target_pairs={{0,24},{8,32},{16,40},{24,48},{32,56},{40,64},{48,72},{56,80},{64,... | collective-permute-start | bytes 294920 | tf_op jit(solution)/shard_map/ppermute | solution.py:35
  84.0 2.1 collective-permute-done.11
  87.5 5.0 %out_mate.1 = bf16[4,128,1664]{2,1,0:T(8,128)(2,1)} custom-call(s32[1]{0:T(128)} %bitcast.where_ref, f32[1024,384]{1,0:T(8,128)} %get-tuple-element.24.y_in, bf16[1024,256]{1,0:T(8,128)(2,1)} %get-tuple-element.21.bc_in, f32[1024,128]{1,0:T(8,128)} %get-tuple-element.25.lead_in, f32[1024,384]{1,0:T(8,128)} %get-tuple-element.26.z_in, ...), custom_call_target="tpu_custom_call" | custom-call | tf_op jit(solution)/shard_map/out_mate/pallas_call | solution.py:403
  93.8 5.0 %out_own.1 = bf16[4,128,1664]{2,1,0:T(8,128)(2,1)} custom-call(s32[1]{0:T(128)} %bitcast.where_ref, f32[1024,384]{1,0:T(8,128)} %get-tuple-element.24.y_in, bf16[1024,256]{1,0:T(8,128)(2,1)} %get-tuple-element.21.bc_in, f32[1024,128]{1,0:T(8,128)} %get-tuple-element.25.lead_in, f32[1024,384]{1,0:T(8,128)} %get-tuple-element.26.z_in, ...), custom_call_target="tpu_custom_call" | custom-call | tf_op jit(solution)/shard_map/out_own/pallas_call | solution.py:403
  98.7 2.4 fusion.43
  102.0 3.1 %collective-permute-start.14 = (bf16[128,1664]{1,0:T(8,128)(2,1)}, bf16[128,1664]{1,0:T(8,128)(2,1)}, u32[]{:S(2)}, u32[]{:S(2)}) collective-permute-start(bf16[128,1664]{1,0:T(8,128)(2,1)} %pad_maximum_fusion.3), channel_id=1, source_target_pairs={{0,6},{1,7},{2,0},{3,1},{4,2},{5,3},{6,4},{7,5},{8,14},{9,15},{10,... | collective-permute-start | bytes 1277960 | tf_op jit(solution)/shard_map/ppermute | solution.py:39
  105.9 1.3 convolution_compare_fusion
  108.0 1.8 copy.68.spots
  110.4 4.8 %collective-permute-done.14.p_b = bf16[128,1664]{1,0:T(8,128)(2,1)} collective-permute-done((bf16[128,1664]{1,0:T(8,128)(2,1)}, bf16[128,1664]{1,0:T(8,128)(2,1)}, u32[]{:S(2)}, u32[]{:S(2)}) %collective-permute-start.14) | collective-permute-done | bytes 426016 | tf_op jit(solution)/shard_map/ppermute | solution.py:39
  115.2 4.2 %collective-permute-done.13.p_a = bf16[128,1664]{1,0:T(8,128)(2,1)} collective-permute-done((bf16[128,1664]{1,0:T(8,128)(2,1)}, bf16[128,1664]{1,0:T(8,128)(2,1)}, u32[]{:S(2)}, u32[]{:S(2)}) %collective-permute-start.13) | collective-permute-done | bytes 426016 | tf_op jit(solution)/shard_map/ppermute | solution.py:39
  119.4 1.1 fusion.6
  120.6 3.2 %collective-permute-start.16 = (bf16[64,1664]{1,0:T(8,128)(2,1)S(1)}, bf16[64,1664]{1,0:T(8,128)(2,1)}, u32[]{:S(2)}, u32[]{:S(2)}) collective-permute-start(bf16[64,1664]{1,0:T(8,128)(2,1)S(1)} %get-tuple-element.47), channel_id=1, source_target_pairs={{0,6},{1,7},{2,0},{3,1},{4,2},{5,3},{6,4},{7,5},{8,14},{9,15},{10,... | collective-permute-start | bytes 638984 | tf_op jit(solution)/shard_map/ppermute | solution.py:39
  123.8 1.0 slice_bitcast_fusion.h0
  124.8 3.5 %collective-permute-done.15.q_a = bf16[64,1664]{1,0:T(8,128)(2,1)S(1)} collective-permute-done((bf16[64,1664]{1,0:T(8,128)(2,1)S(1)}, bf16[64,1664]{1,0:T(8,128)(2,1)S(1)}, u32[]{:S(2)}, u32[]{:S(2)}) %collective-permute-start.15) | collective-permute-done | bytes 213024 | tf_op jit(solution)/shard_map/ppermute | solution.py:39
  129.0 4.7 %enter.1 = (f32[128,1536]{1,0:T(8,128)}, bf16[128,1536]{1,0:T(8,128)(2,1)}, bf16[1024,1536]{1,0:T(8,128)(2,1)}) custom-call(f32[128,1664]{1,0:T(8,128)} %slice_bitcast_fusion.h0, bf16[128,1664]{1,0:T(8,128)(2,1)} %collective-permute-done.13.p_a, bf16[128,1664]{1,0:T(8,128)(2,1)} %collective-permute-done.14.p_b, bf16[64,1664]{1,0:T(8,128)(2,1)} %copy-done.16, ...), custom_call_target="tpu_custom_call" | custom-call | tf_op jit(solution)/shard_map/enter/pallas_call | solution.py:420
  133.8 6.8 %all-to-all-start = ((bf16[16,4,16,1536]{3,2,1,0:T(8,128)(2,1)}), bf16[16,4,16,1536]{3,2,1,0:T(8,128)(2,1)S(1)}, u32[]{:S(2)}, u32[]{:S(2)}) async-start(bf16[16,4,16,1536]{3,2,1,0:T(8,128)(2,1)} %bitcast.62), calls=%async_computation | async-start | bytes 6291456 | tf_op jit(solution)/shard_map/all_to_all | solution.py:428
  147.6 34.1 %all-to-all-done.rows_ref = bf16[16,4,16,1536]{3,2,1,0:T(8,128)(2,1)S(1)} async-done(((bf16[16,4,16,1536]{3,2,1,0:T(8,128)(2,1)}), bf16[16,4,16,1536]{3,2,1,0:T(8,128)(2,1)S(1)}, u32[]{:S(2)}, u32[]{:S(2)}) %all-to-all-start) | async-done | bytes 3145760 | tf_op jit(solution)/shard_map/all_to_all | solution.py:428
  181.7 4.4 %all-to-all-start.2 = ((bf16[16,128,384]{2,1,0:T(8,128)(2,1)}), bf16[16,128,384]{2,1,0:T(8,128)(2,1)}, u32[]{:S(2)}, u32[]{:S(2)}) async-start(bf16[16,128,384]{2,1,0:T(8,128)(2,1)} %fusion.15), calls=%async_computation.2 | async-start | bytes 3145728 | tf_op jit(solution)/shard_map/all_to_all | solution.py:396
  186.1 1.2 copy.69
  187.3 1.9 copy.70
  189.2 2.2 pad_maximum_fusion.1.w0
  191.4 3.2 %collective-permute-start.20 = (bf16[384,1536]{1,0:T(8,128)(2,1)}, bf16[384,1536]{1,0:T(8,128)(2,1)}, u32[]{:S(2)}, u32[]{:S(2)}) collective-permute-start(bf16[384,1536]{1,0:T(8,128)(2,1)} %pad_maximum_fusion.1.w0), channel_id=1, source_target_pairs={{0,6},{1,7},{2,0},{3,1},{4,2},{5,3},{6,4},{7,5},{8,14},{9,15},{10,... | collective-permute-start | bytes 3538952 | tf_op jit(solution)/shard_map/ppermute | solution.py:39
  194.7 11.4 %experts.1 = bf16[16,4,16,1536]{3,2,1,0:T(8,128)(2,1)} custom-call(bf16[16,4,16,1536]{3,2,1,0:T(8,128)(2,1)} %copy-done, bf16[4,1536,512]{2,1,0:T(8,128)(2,1)} %gate.1, bf16[4,1536,512]{2,1,0:T(8,128)(2,1)} %up.1, bf16[4,512,1536]{2,1,0:T(8,128)(2,1)} %down.1), custom_call_target="tpu_custom_call" | custom-call | tf_op jit(solution)/shard_map/experts/pallas_call | solution.py:441
  206.5 6.7 %all-to-all-start.1 = ((bf16[16,4,16,1536]{3,2,1,0:T(8,128)(2,1)}), bf16[16,4,16,1536]{3,2,1,0:T(8,128)(2,1)S(1)}, u32[]{:S(2)}, u32[]{:S(2)}) async-start(bf16[16,4,16,1536]{3,2,1,0:T(8,128)(2,1)} %experts.1), calls=%async_computation.1 | async-start | bytes 6291456 | tf_op jit(solution)/shard_map/all_to_all | solution.py:454
  213.2 3.7 %collective-permute-done.18.w2 = bf16[384,1536]{1,0:T(8,128)(2,1)} collective-permute-done((bf16[384,1536]{1,0:T(8,128)(2,1)}, bf16[384,1536]{1,0:T(8,128)(2,1)}, u32[]{:S(2)}, u32[]{:S(2)}) %collective-permute-start.18) | collective-permute-done | bytes 1179680 | tf_op jit(solution)/shard_map/ppermute | solution.py:39
  216.9 1.1 slice.154
  218.1 1.1 slice.155
  219.2 3.3 %collective-permute-start.23 = (bf16[192,1536]{1,0:T(8,128)(2,1)S(1)}, bf16[192,1536]{1,0:T(8,128)(2,1)S(1)}, u32[]{:S(2)}, u32[]{:S(2)}) collective-permute-start(bf16[192,1536]{1,0:T(8,128)(2,1)S(1)} %slice.155), channel_id=1, source_target_pairs={{0,6},{1,7},{2,0},{3,1},{4,2},{5,3},{6,4},{7,5},{8,14},{9,15},{10,... | collective-permute-start | bytes 1769480 | tf_op jit(solution)/shard_map/ppermute | solution.py:39
  223.0 6.7 %collective-permute-done.22 = bf16[192,1536]{1,0:T(8,128)(2,1)S(1)} collective-permute-done((bf16[192,1536]{1,0:T(8,128)(2,1)S(1)}, bf16[192,1536]{1,0:T(8,128)(2,1)S(1)}, u32[]{:S(2)}, u32[]{:S(2)}) %collective-permute-start.22) | collective-permute-done | bytes 589856 | tf_op jit(solution)/shard_map/ppermute | solution.py:39
  235.3 1.0 fusion.high
  238.9 8.4 %shared.1.base = f32[128,1536]{1,0:T(8,128)} custom-call(bf16[128,1536]{1,0:T(8,128)(2,1)} %get-tuple-element.30.rows_ref, bf16[384,1536]{1,0:T(8,128)(2,1)} %pad_maximum_fusion.1.w0, bf16[384,1536]{1,0:T(8,128)(2,1)} %collective-permute-done.17.w1, bf16[384,1536]{1,0:T(8,128)(2,1)} %collective-permute-done.18.w2, ...), custom_call_target="tpu_custom_call" | custom-call | tf_op jit(solution)/shard_map/shared/pallas_call | solution.py:434
  247.3 2.8 %all-to-all-done.1 = bf16[16,4,16,1536]{3,2,1,0:T(8,128)(2,1)S(1)} async-done(((bf16[16,4,16,1536]{3,2,1,0:T(8,128)(2,1)}), bf16[16,4,16,1536]{3,2,1,0:T(8,128)(2,1)S(1)}, u32[]{:S(2)}, u32[]{:S(2)}) %all-to-all-start.1) | async-done | bytes 3145760 | tf_op jit(solution)/shard_map/all_to_all | solution.py:454
  250.2 1.6 copy-done.1
  251.8 4.0 %leave.1 = bf16[128,1536]{1,0:T(8,128)(2,1)} custom-call(bf16[1024,1536]{1,0:T(8,128)(2,1)} %bitcast.61, bf16[128,1024]{1,0:T(8,128)(2,1)} %fusion.high, bf16[128,1024]{1,0:T(8,128)(2,1)} %fusion.1.low, f32[128,1536]{1,0:T(8,128)} %shared.1.base), custom_call_target="tpu_custom_call" | custom-call | tf_op jit(solution)/shard_map/leave/pallas_call | solution.py:455
  (175 shorter events, 32.0 us)
Async XLA Ops:
  0.6 12.5 %collective-permute-start.1 = (bf16[128,1536]{1,0:T(8,128)(2,1)}, bf16[128,1536]{1,0:T(8,128)(2,1)S(1)}, u32[]{:S(2)}, u32[]{:S(2)}) collective-permute-start(bf16[128,1536]{1,0:T(8,128)(2,1)} %tokens.1), channel_id=1, source_target_pairs={{0,2},{1,3},{2,4},{3,5},{4,6},{5,7},{6,0},{7,1},{8,10},{9,11},{10,... | collective-permute-start | bytes 1179656 | tf_op jit(solution)/shard_map/ppermute | solution.py:39
  2.4 11.2 %collective-permute-start.3 = (bf16[128,1536]{1,0:T(8,128)(2,1)}, bf16[128,1536]{1,0:T(8,128)(2,1)S(1)}, u32[]{:S(2)}, u32[]{:S(2)}) collective-permute-start(bf16[128,1536]{1,0:T(8,128)(2,1)} %tokens.1), channel_id=1, source_target_pairs={{0,6},{1,7},{2,0},{3,1},{4,2},{5,3},{6,4},{7,5},{8,14},{9,15},{10,... | collective-permute-start | bytes 1179656 | tf_op jit(solution)/shard_map/ppermute | solution.py:39
  3.9 19.8 %collective-permute-start = (bf16[128,1536]{1,0:T(8,128)(2,1)}, bf16[128,1536]{1,0:T(8,128)(2,1)}, u32[]{:S(2)}, u32[]{:S(2)}) collective-permute-start(bf16[128,1536]{1,0:T(8,128)(2,1)} %tokens.1), channel_id=1, source_target_pairs={{0,1},{1,0},{2,3},{3,2},{4,5},{5,4},{6,7},{7,6},{8,9},{9,8},{10,11... | collective-permute-start | bytes 1179656 | tf_op jit(solution)/shard_map/ppermute | solution.py:39
  4.8 5.7 %copy-start.26 = (s32[16]{0:T(128)}, s32[16]{0:T(128)S(1)}, u32[]{:S(2)}) copy-start(s32[16]{0:T(128)S(1)} %select_reduce_fusion.1) | copy-start | bytes 196
  7.2 13.4 %copy-start.35 = (f32[6]{0:T(128)S(1)}, f32[6]{0:T(128)}, u32[]{:S(2)}) copy-start(f32[6]{0:T(128)} %param.32) | copy-start | bytes 76
  7.2 13.9 %copy-start.4 = (bf16[1536,384]{1,0:T(8,128)(2,1)S(1)}, bf16[1536,384]{1,0:T(8,128)(2,1)}, u32[]{:S(2)}) copy-start(bf16[1536,384]{1,0:T(8,128)(2,1)} %param.27) | copy-start | bytes 3538948
  13.2 10.6 %copy-start.5 = (bf16[128,1536]{1,0:T(8,128)(2,1)}, bf16[128,1536]{1,0:T(8,128)(2,1)S(1)}, u32[]{:S(2)}) copy-start(bf16[128,1536]{1,0:T(8,128)(2,1)S(1)} %collective-permute-done.1.b2) | copy-start | bytes 1179652
  13.2 7.2 %collective-permute-start.5 = (bf16[64,1536]{1,0:T(8,128)(2,1)S(1)}, bf16[64,1536]{1,0:T(8,128)(2,1)S(1)}, u32[]{:S(2)}, u32[]{:S(2)}) collective-permute-start(bf16[64,1536]{1,0:T(8,128)(2,1)S(1)} %slice.137), channel_id=1, source_target_pairs={{0,2},{1,3},{2,4},{3,5},{4,6},{5,7},{6,0},{7,1},{8,10},{9,11},{10,... | collective-permute-start | bytes 589832 | tf_op jit(solution)/shard_map/ppermute | solution.py:39
  13.5 27.6 %copy-start.28 = (s32[8]{0:T(128)}, s32[8]{0:T(128)S(1)}, u32[]{:S(2)}) copy-start(s32[8]{0:T(128)S(1)} %compare_select_fusion.3) | copy-start | bytes 100
  13.6 10.2 %copy-start.6 = (bf16[128,1536]{1,0:T(8,128)(2,1)}, bf16[128,1536]{1,0:T(8,128)(2,1)S(1)}, u32[]{:S(2)}) copy-start(bf16[128,1536]{1,0:T(8,128)(2,1)S(1)} %collective-permute-done.3.b4) | copy-start | bytes 1179652
  13.6 6.8 %collective-permute-start.6 = (bf16[64,1536]{1,0:T(8,128)(2,1)S(1)}, bf16[64,1536]{1,0:T(8,128)(2,1)S(1)}, u32[]{:S(2)}, u32[]{:S(2)}) collective-permute-start(bf16[64,1536]{1,0:T(8,128)(2,1)S(1)} %slice.138), channel_id=1, source_target_pairs={{0,6},{1,7},{2,0},{3,1},{4,2},{5,3},{6,4},{7,5},{8,14},{9,15},{10,... | collective-permute-start | bytes 589832 | tf_op jit(solution)/shard_map/ppermute | solution.py:39
  16.6 7.2 %collective-permute-start.2 = (bf16[128,1536]{1,0:T(8,128)(2,1)S(1)}, bf16[128,1536]{1,0:T(8,128)(2,1)S(1)}, u32[]{:S(2)}, u32[]{:S(2)}) collective-permute-start(bf16[128,1536]{1,0:T(8,128)(2,1)S(1)} %collective-permute-done.1.b2), channel_id=1, source_target_pairs={{0,1},{1,0},{2,3},{3,2},{4,5},{5,4},{6,7},{7,6},{8,9},{9,8},{10,11... | collective-permute-start | bytes 1179656 | tf_op jit(solution)/shard_map/ppermute | solution.py:39
  16.6 7.2 %collective-permute-start.4 = (bf16[128,1536]{1,0:T(8,128)(2,1)S(1)}, bf16[128,1536]{1,0:T(8,128)(2,1)S(1)}, u32[]{:S(2)}, u32[]{:S(2)}) collective-permute-start(bf16[128,1536]{1,0:T(8,128)(2,1)S(1)} %collective-permute-done.3.b4), channel_id=1, source_target_pairs={{0,1},{1,0},{2,3},{3,2},{4,5},{5,4},{6,7},{7,6},{8,9},{9,8},{10,11... | collective-permute-start | bytes 1179656 | tf_op jit(solution)/shard_map/ppermute | solution.py:39
  20.5 3.3 %collective-permute-start.7 = (bf16[128,1536]{1,0:T(8,128)(2,1)S(1)}, bf16[128,1536]{1,0:T(8,128)(2,1)S(1)}, u32[]{:S(2)}, u32[]{:S(2)}) collective-permute-start(bf16[128,1536]{1,0:T(8,128)(2,1)S(1)} %constant_dynamic-update-slice_fusion.b6), channel_id=1, source_target_pairs={{0,1},{1,0},{2,3},{3,2},{4,5},{5,4},{6,7},{7,6},{8,9},{9,8},{10,11... | collective-permute-start | bytes 1179656 | tf_op jit(solution)/shard_map/ppermute | solution.py:39
  24.8 16.3 %copy-start.32 = (s32[16]{0:T(128)S(1)}, s32[16]{0:T(128)}, u32[]{:S(2)}) copy-start(s32[16]{0:T(128)} %param.47) | copy-start | bytes 196
  35.8 5.9 %collective-permute-start.8 = (bf16[16,640]{1,0:T(8,128)(2,1)S(1)}, bf16[16,640]{1,0:T(8,128)(2,1)S(1)}, u32[]{:S(2)}, u32[]{:S(2)}) collective-permute-start(bf16[16,640]{1,0:T(8,128)(2,1)S(1)} %slice.108), channel_id=1, source_target_pairs={{0,8},{8,16},{16,24},{24,32},{32,40},{40,48},{48,56},{56,64},{64,7... | collective-permute-start | bytes 61448 | tf_op jit(solution)/shard_map/ppermute | solution.py:35
  42.3 22.3 %copy-start.31 = (f32[6]{0:T(128)S(1)}, f32[6]{0:T(128)}, u32[]{:S(2)}) copy-start(f32[6]{0:T(128)} %param.34) | copy-start | bytes 76
  42.3 23.0 %copy-start.30 = (f32[384]{0:T(512)S(1)}, f32[384]{0:T(512)}, u32[]{:S(2)}) copy-start(f32[384]{0:T(512)} %param.35) | copy-start | bytes 4612
  50.9 6.8 %collective-permute-start.9 = (bf16[144,384]{1,0:T(8,128)(2,1)}, bf16[144,384]{1,0:T(8,128)(2,1)S(1)}, u32[]{:S(2)}, u32[]{:S(2)}) collective-permute-start(bf16[144,384]{1,0:T(8,128)(2,1)} %get-tuple-element.27), channel_id=1, source_target_pairs={{0,8},{8,16},{16,24},{24,32},{32,40},{40,48},{48,56},{56,64},{64,7... | collective-permute-start | bytes 331784 | tf_op jit(solution)/shard_map/ppermute | solution.py:35
  59.6 24.4 %collective-permute-start.10 = (bf16[144,384]{1,0:T(8,128)(2,1)S(1)}, bf16[144,384]{1,0:T(8,128)(2,1)S(1)}, u32[]{:S(2)}, u32[]{:S(2)}) collective-permute-start(bf16[144,384]{1,0:T(8,128)(2,1)S(1)} %maximum_maximum_fusion), channel_id=1, source_target_pairs={{0,8},{8,16},{16,24},{24,32},{32,40},{40,48},{48,56},{56,64},{64,7... | collective-permute-start | bytes 331784 | tf_op jit(solution)/shard_map/ppermute | solution.py:35
  75.6 10.6 %collective-permute-start.11 = (bf16[128,384]{1,0:T(8,128)(2,1)S(1)}, bf16[128,384]{1,0:T(8,128)(2,1)S(1)}, u32[]{:S(2)}, u32[]{:S(2)}) collective-permute-start(bf16[128,384]{1,0:T(8,128)(2,1)S(1)} %add_convert_fusion), channel_id=1, source_target_pairs={{0,24},{8,32},{16,40},{24,48},{32,56},{40,64},{48,72},{56,80},{64,... | collective-permute-start | bytes 294920 | tf_op jit(solution)/shard_map/ppermute | solution.py:35
  84.0 14.7 %copy-start.13 = (bf16[144,384]{1,0:T(8,128)(2,1)}, bf16[144,384]{1,0:T(8,128)(2,1)S(1)}, u32[]{:S(2)}) copy-start(bf16[144,384]{1,0:T(8,128)(2,1)S(1)} %collective-permute-done.10) | copy-start | bytes 331780
  92.5 6.3 %collective-permute-start.12 = (bf16[4,128,1664]{2,1,0:T(8,128)(2,1)}, bf16[4,128,1664]{2,1,0:T(8,128)(2,1)}, u32[]{:S(2)}, u32[]{:S(2)}) collective-permute-start(bf16[4,128,1664]{2,1,0:T(8,128)(2,1)} %out_mate.1), channel_id=1, source_target_pairs={{0,1},{1,0},{2,3},{3,2},{4,5},{5,4},{6,7},{7,6},{8,9},{9,8},{10,11... | collective-permute-start | bytes 5111816 | tf_op jit(solution)/shard_map/ppermute | solution.py:39
  101.2 8.6 %copy-start.20 = (f32[1536]{0:T(1024)S(1)}, f32[1536]{0:T(1024)}, u32[]{:S(2)}) copy-start(f32[1536]{0:T(1024)} %param.37) | copy-start | bytes 18436
  102.0 13.2 %collective-permute-start.14 = (bf16[128,1664]{1,0:T(8,128)(2,1)}, bf16[128,1664]{1,0:T(8,128)(2,1)}, u32[]{:S(2)}, u32[]{:S(2)}) collective-permute-start(bf16[128,1664]{1,0:T(8,128)(2,1)} %pad_maximum_fusion.3), channel_id=1, source_target_pairs={{0,6},{1,7},{2,0},{3,1},{4,2},{5,3},{6,4},{7,5},{8,14},{9,15},{10,... | collective-permute-start | bytes 1277960 | tf_op jit(solution)/shard_map/ppermute | solution.py:39
  105.9 13.5 %collective-permute-start.13 = (bf16[128,1664]{1,0:T(8,128)(2,1)}, bf16[128,1664]{1,0:T(8,128)(2,1)}, u32[]{:S(2)}, u32[]{:S(2)}) collective-permute-start(bf16[128,1664]{1,0:T(8,128)(2,1)} %pad_maximum_fusion.2), channel_id=1, source_target_pairs={{0,2},{1,3},{2,4},{3,5},{4,6},{5,7},{6,0},{7,1},{8,10},{9,11},{10,... | collective-permute-start | bytes 1277960 | tf_op jit(solution)/shard_map/ppermute | solution.py:39
  107.2 17.6 %copy-start.2 = (pred[128,1024]{1,0:T(32,128)(4,1)}, pred[128,1024]{1,0:T(32,128)(4,1)S(1)}, u32[]{:S(2)}) copy-start(pred[128,1024]{1,0:T(32,128)(4,1)S(1)} %convolution_compare_fusion) | copy-start | bytes 393220
  120.5 7.8 %collective-permute-start.15 = (bf16[64,1664]{1,0:T(8,128)(2,1)S(1)}, bf16[64,1664]{1,0:T(8,128)(2,1)S(1)}, u32[]{:S(2)}, u32[]{:S(2)}) collective-permute-start(bf16[64,1664]{1,0:T(8,128)(2,1)S(1)} %get-tuple-element.48), channel_id=1, source_target_pairs={{0,2},{1,3},{2,4},{3,5},{4,6},{5,7},{6,0},{7,1},{8,10},{9,11},{10,... | collective-permute-start | bytes 638984 | tf_op jit(solution)/shard_map/ppermute | solution.py:39
  120.6 8.4 %collective-permute-start.16 = (bf16[64,1664]{1,0:T(8,128)(2,1)S(1)}, bf16[64,1664]{1,0:T(8,128)(2,1)}, u32[]{:S(2)}, u32[]{:S(2)}) collective-permute-start(bf16[64,1664]{1,0:T(8,128)(2,1)S(1)} %get-tuple-element.47), channel_id=1, source_target_pairs={{0,6},{1,7},{2,0},{3,1},{4,2},{5,3},{6,4},{7,5},{8,14},{9,15},{10,... | collective-permute-start | bytes 638984 | tf_op jit(solution)/shard_map/ppermute | solution.py:39
  133.7 6.8 %copy-start.29 = (s32[8]{0:T(128)S(1)}, s32[8]{0:T(128)}, u32[]{:S(2)}) copy-start(s32[8]{0:T(128)} %copy-done.28) | copy-start | bytes 100
  133.7 6.9 %copy-start.33 = (s32[16]{0:T(128)S(1)}, s32[16]{0:T(128)}, u32[]{:S(2)}) copy-start(s32[16]{0:T(128)} %param.47) | copy-start | bytes 196
  133.7 7.5 %copy-start.22 = (s32[64]{0:T(128)S(1)}, s32[64]{0:T(128)}, u32[]{:S(2)}) copy-start(s32[64]{0:T(128)} %concatenate.29.meta) | copy-start | bytes 772
  133.7 13.2 %copy-start.12 = (bf16[128,384]{1,0:T(8,128)(2,1)S(1)}, bf16[128,384]{1,0:T(8,128)(2,1)}, u32[]{:S(2)}) copy-start(bf16[128,384]{1,0:T(8,128)(2,1)} %copy-done.11) | copy-start | bytes 294916
  133.7 13.2 %copy-start.14 = (bf16[144,384]{1,0:T(8,128)(2,1)S(1)}, bf16[144,384]{1,0:T(8,128)(2,1)}, u32[]{:S(2)}) copy-start(bf16[144,384]{1,0:T(8,128)(2,1)} %copy-done.13) | copy-start | bytes 331780
  133.8 48.0 %all-to-all-start = ((bf16[16,4,16,1536]{3,2,1,0:T(8,128)(2,1)}), bf16[16,4,16,1536]{3,2,1,0:T(8,128)(2,1)S(1)}, u32[]{:S(2)}, u32[]{:S(2)}) async-start(bf16[16,4,16,1536]{3,2,1,0:T(8,128)(2,1)} %bitcast.62), calls=%async_computation | async-start | bytes 6291456 | tf_op jit(solution)/shard_map/all_to_all | solution.py:428
  181.7 24.7 %all-to-all-start.2 = ((bf16[16,128,384]{2,1,0:T(8,128)(2,1)}), bf16[16,128,384]{2,1,0:T(8,128)(2,1)}, u32[]{:S(2)}, u32[]{:S(2)}) async-start(bf16[16,128,384]{2,1,0:T(8,128)(2,1)} %fusion.15), calls=%async_computation.2 | async-start | bytes 3145728 | tf_op jit(solution)/shard_map/all_to_all | solution.py:396
  191.4 25.4 %collective-permute-start.18 = (bf16[384,1536]{1,0:T(8,128)(2,1)}, bf16[384,1536]{1,0:T(8,128)(2,1)}, u32[]{:S(2)}, u32[]{:S(2)}) collective-permute-start(bf16[384,1536]{1,0:T(8,128)(2,1)} %pad_maximum_fusion.1.w0), channel_id=1, source_target_pairs={{0,2},{1,3},{2,4},{3,5},{4,6},{5,7},{6,0},{7,1},{8,10},{9,11},{10,... | collective-permute-start | bytes 3538952 | tf_op jit(solution)/shard_map/ppermute | solution.py:39
  191.4 26.7 %collective-permute-start.20 = (bf16[384,1536]{1,0:T(8,128)(2,1)}, bf16[384,1536]{1,0:T(8,128)(2,1)}, u32[]{:S(2)}, u32[]{:S(2)}) collective-permute-start(bf16[384,1536]{1,0:T(8,128)(2,1)} %pad_maximum_fusion.1.w0), channel_id=1, source_target_pairs={{0,6},{1,7},{2,0},{3,1},{4,2},{5,3},{6,4},{7,5},{8,14},{9,15},{10,... | collective-permute-start | bytes 3538952 | tf_op jit(solution)/shard_map/ppermute | solution.py:39
  206.5 43.7 %all-to-all-start.1 = ((bf16[16,4,16,1536]{3,2,1,0:T(8,128)(2,1)}), bf16[16,4,16,1536]{3,2,1,0:T(8,128)(2,1)S(1)}, u32[]{:S(2)}, u32[]{:S(2)}) async-start(bf16[16,4,16,1536]{3,2,1,0:T(8,128)(2,1)} %experts.1), calls=%async_computation.1 | async-start | bytes 6291456 | tf_op jit(solution)/shard_map/all_to_all | solution.py:454
  218.0 15.9 %copy-start.27 = (s32[16]{0:T(128)S(1)}, s32[16]{0:T(128)}, u32[]{:S(2)}) copy-start(s32[16]{0:T(128)} %copy-done.26) | copy-start | bytes 196
  218.0 17.3 %copy-start.3 = (pred[128,1024]{1,0:T(32,128)(4,1)S(1)}, pred[128,1024]{1,0:T(32,128)(4,1)}, u32[]{:S(2)}) copy-start(pred[128,1024]{1,0:T(32,128)(4,1)} %copy-done.2) | copy-start | bytes 393220
  218.0 17.3 %copy-start.15 = (f32[128,64]{0,1:T(8,128)S(1)}, f32[128,64]{0,1:T(8,128)}, u32[]{:S(2)}) copy-start(f32[128,64]{0,1:T(8,128)} %get-tuple-element.36) | copy-start | bytes 98308
  218.0 11.7 %collective-permute-start.22 = (bf16[192,1536]{1,0:T(8,128)(2,1)S(1)}, bf16[192,1536]{1,0:T(8,128)(2,1)S(1)}, u32[]{:S(2)}, u32[]{:S(2)}) collective-permute-start(bf16[192,1536]{1,0:T(8,128)(2,1)S(1)} %slice.154), channel_id=1, source_target_pairs={{0,2},{1,3},{2,4},{3,5},{4,6},{5,7},{6,0},{7,1},{8,10},{9,11},{10,... | collective-permute-start | bytes 1769480 | tf_op jit(solution)/shard_map/ppermute | solution.py:39
  219.2 11.3 %collective-permute-start.23 = (bf16[192,1536]{1,0:T(8,128)(2,1)S(1)}, bf16[192,1536]{1,0:T(8,128)(2,1)S(1)}, u32[]{:S(2)}, u32[]{:S(2)}) collective-permute-start(bf16[192,1536]{1,0:T(8,128)(2,1)S(1)} %slice.155), channel_id=1, source_target_pairs={{0,6},{1,7},{2,0},{3,1},{4,2},{5,3},{6,4},{7,5},{8,14},{9,15},{10,... | collective-permute-start | bytes 1769480 | tf_op jit(solution)/shard_map/ppermute | solution.py:39
  222.5 16.4 %collective-permute-start.17 = (bf16[384,1536]{1,0:T(8,128)(2,1)}, bf16[384,1536]{1,0:T(8,128)(2,1)}, u32[]{:S(2)}, u32[]{:S(2)}) collective-permute-start(bf16[384,1536]{1,0:T(8,128)(2,1)} %pad_maximum_fusion.1.w0), channel_id=1, source_target_pairs={{0,1},{1,0},{2,3},{3,2},{4,5},{5,4},{6,7},{7,6},{8,9},{9,8},{10,11... | collective-permute-start | bytes 3538952 | tf_op jit(solution)/shard_map/ppermute | solution.py:39
  222.5 16.4 %collective-permute-start.19 = (bf16[384,1536]{1,0:T(8,128)(2,1)}, bf16[384,1536]{1,0:T(8,128)(2,1)}, u32[]{:S(2)}, u32[]{:S(2)}) collective-permute-start(bf16[384,1536]{1,0:T(8,128)(2,1)} %collective-permute-done.18.w2), channel_id=1, source_target_pairs={{0,1},{1,0},{2,3},{3,2},{4,5},{5,4},{6,7},{7,6},{8,9},{9,8},{10,11... | collective-permute-start | bytes 3538952 | tf_op jit(solution)/shard_map/ppermute | solution.py:39
  223.0 15.9 %collective-permute-start.21 = (bf16[384,1536]{1,0:T(8,128)(2,1)}, bf16[384,1536]{1,0:T(8,128)(2,1)}, u32[]{:S(2)}, u32[]{:S(2)}) collective-permute-start(bf16[384,1536]{1,0:T(8,128)(2,1)} %collective-permute-done.20.w4), channel_id=1, source_target_pairs={{0,1},{1,0},{2,3},{3,2},{4,5},{5,4},{6,7},{7,6},{8,9},{9,8},{10,11... | collective-permute-start | bytes 3538952 | tf_op jit(solution)/shard_map/ppermute | solution.py:39
  231.4 7.5 %collective-permute-start.24 = (bf16[384,1536]{1,0:T(8,128)(2,1)}, bf16[384,1536]{1,0:T(8,128)(2,1)}, u32[]{:S(2)}, u32[]{:S(2)}) collective-permute-start(bf16[384,1536]{1,0:T(8,128)(2,1)} %constant_dynamic-update-slice_fusion.2.w6), channel_id=1, source_target_pairs={{0,1},{1,0},{2,3},{3,2},{4,5},{5,4},{6,7},{7,6},{8,9},{9,8},{10,11... | collective-permute-start | bytes 3538952 | tf_op jit(solution)/shard_map/ppermute | solution.py:39
  (16 other events, 36.6 us)

commit v2 on v1

v2 whole, which is shorter than its diff:
```python
import functools

import jax
import jax.numpy as jnp
from jax import lax
from jax.experimental import pallas as pl
from jax.experimental.pallas import tpu as pltpu
from jax.sharding import PartitionSpec as P


EPS = 1e-05
HIGH = lax.Precision.HIGHEST
F32 = jnp.float32
BF16 = jnp.bfloat16
LANES = 128
ROWS = 128
CHUNK = 128
CAP = 16
HEADS = 6
HALF = 64
WIDE = 384
STATE = 128
DI = 3072
VM = pl.BlockSpec(memory_space=pltpu.VMEM)
SM = pl.BlockSpec(memory_space=pltpu.SMEM)
ANY = pl.BlockSpec(memory_space=pl.ANY)
PLUS = [(i, (i + 2) % 8) for i in range(8)]
MINUS = [(i, (i + 6) % 8) for i in range(8)]
MATE = [(i, i ^ 1) for i in range(8)]


def near_core(*arrays):
    return [pltpu.with_memory_space_constraint(a, pltpu.VMEM) for a in arrays]


def far_core(*arrays):
    return [pltpu.with_memory_space_constraint(a, pltpu.HBM) for a in arrays]


def silu(v):
    return v * (1.0 / (1.0 + jnp.exp(-v)))


def ahead(block, distance):
    return lax.ppermute(block, "seq", [(i, i + distance) for i in range(16 - distance)])


def over_exp(block, route):
    return lax.ppermute(block, "exp", route)


def spread(cols):
    rows = cols.shape[0]
    left = lax.broadcasted_iota(jnp.int32, (rows, LANES), 1) < HALF
    parts = []
    for pair in range(HEADS // 2):
        first = jnp.broadcast_to(cols[:, 2 * pair : 2 * pair + 1], (rows, LANES))
        second = jnp.broadcast_to(cols[:, 2 * pair + 1 : 2 * pair + 2], (rows, LANES))
        parts.append(jnp.where(left, first, second))
    return jnp.concatenate(parts, axis=1)


def chip_of(where):
    return where[0] // 2


def core_of(where):
    return lax.rem(where[0], 2)


def tables_kernel(
    seq, lengths, slots, dt_bias, a_log, d_skip, in_dt, conv_x, conv_bc, g_in, g_mix, g_post, x, bc, z,
    w_all, w_dt, bias, rate, skip, taps, seg_ext, seg_row, gain_in, gain_mix, gain_post, meta, sems,
):
    copies = []
    for i, (ref, at, cols) in enumerate(((x, 0, WIDE), (bc, WIDE, 2 * STATE), (z, WIDE + 2 * STATE, WIDE))):
        copies.append(pltpu.make_async_copy(ref, w_all.at[:, at : at + cols], sems.at[i]))
    for copy in copies:
        copy.start()
    base = seq[0] * (8 * CHUNK)
    total = jnp.int32(0)
    ends = []
    for req in range(16):
        total = total + lengths[req]
        ends.append(total)

    lane = lax.broadcasted_iota(jnp.int32, (1, LANES), 1)
    wide = lax.broadcasted_iota(jnp.int32, (1, WIDE), 1)
    bias_row = jnp.zeros((1, LANES), F32)
    rate_row = jnp.zeros((1, LANES), F32)
    skip_row = jnp.zeros((1, WIDE), F32)
    for head in range(HEADS):
        bias_row = jnp.where(lane == head, dt_bias[head], bias_row)
        rate_row = jnp.where(lane == head, a_log[head], rate_row)
        skip_row = jnp.where((wide >= head * HALF) & (wide < (head + 1) * HALF), d_skip[head], skip_row)
    bias[...] = bias_row
    rate[...] = jnp.where(lane < HEADS, jnp.exp(rate_row), 0.0)
    skip[...] = skip_row
    taps[:, :WIDE] = conv_x[...]
    taps[:, WIDE:] = conv_bc[...]
    gain_in[0, :] = g_in[...]
    gain_mix[0, :] = g_mix[...]
    gain_post[0, :] = g_post[...]
    w_dt[...] = jnp.zeros_like(w_dt)
    w_dt[:HEADS, :] = in_dt[...]

    def seg_at(positions):
        found = jnp.zeros_like(positions)
        for end in ends:
            found = found + jnp.where(positions >= end, 1, 0)
        return jnp.where(positions >= 0, found, -1)

    ext_i = lax.broadcasted_iota(jnp.int32, (8 * CHUNK + 16, 1), 0)
    seg_ext[...] = seg_at(base + ext_i - 16)
    row_i = lax.broadcasted_iota(jnp.int32, (8, CHUNK), 0)
    seg_row[...] = seg_at(base + row_i * CHUNK + lax.broadcasted_iota(jnp.int32, (8, CHUNK), 1))
    for c in range(8):
        before = seg_at(base + (c * CHUNK - 1))
        meta[c] = before
        meta[8 + c] = before
        meta[16 + c] = seg_at(base + (c * CHUNK + CHUNK - 1))
        meta[24 + c] = seg_at(base + c * CHUNK)
    first = seg_at(base - 1)
    open_req = jnp.maximum(first, 0)
    open_end, open_slot, source = jnp.int32(0), jnp.int32(0), jnp.int32(0)
    for req in range(16):
        meta[32 + req] = ends[req] - 1 - base
        meta[48 + req] = slots[req]
        open_end = jnp.where(open_req == req, ends[req] - 1 - base, open_end)
        open_slot = jnp.where(open_req == req, slots[req], open_slot)
        source = jnp.where(slots[req] == seq[0], (ends[req] - 1) // (8 * CHUNK), source)
    holds = (first >= 0) & (open_end >= 0) & (open_end < 8 * CHUNK)
    meta[64] = open_slot
    meta[65] = jnp.where(holds, 1, 0)
    meta[66] = jnp.clip(open_end, 0, 8 * CHUNK - 1)
    meta[67] = source
    for copy in copies:
        copy.wait()


def join_kernel(up, down, both, up_low, down_high):
    both[:ROWS, :] = up[...]
    both[ROWS:, :] = down[...]
    up_low[...] = up[:HALF, :]
    down_high[...] = down[HALF:, :]


def project_kernel(where, *refs, plan):
    count = 1 + max(piece[0] for _, pieces in plan for piece in pieces)
    blocks, rest = refs[:count], refs[count:]
    gain, w_all, w_dt, bias, rate = rest[:5]
    conv_out, step_out, cum_out, z_out, normed = rest[-5:]
    chip, core = chip_of(where), core_of(where)
    rows_i = lax.broadcasted_iota(jnp.int32, (CHUNK, CHUNK), 0)
    cols_i = lax.broadcasted_iota(jnp.int32, (CHUNK, CHUNK), 1)
    lower = (rows_i >= cols_i).astype(F32)
    for offset, pieces in plan:
        for index, source, rows, own, to in pieces:
            vals = blocks[index][source : source + rows, :].astype(F32)
            meansq = jnp.mean(vals * vals, axis=-1, keepdims=True)
            place = core if own else 1 - core
            start = pl.multiple_of(place * ROWS + to, HALF)
            normed[pl.ds(start, rows), :] = (vals * lax.rsqrt(meansq + EPS) * gain[...]).astype(BF16)
        rows = normed[...]
        at = pl.multiple_of(lax.rem(chip + offset, 4) * (2 * ROWS), 2 * ROWS)
        here = pl.ds(at, 2 * ROWS)
        raw = lax.dot_general(rows, w_dt[...], (((1,), (1,)), ((), ())), preferred_element_type=F32)
        raw = raw.astype(BF16).astype(F32) + bias[...]
        step = jnp.maximum(raw, 0.0) + jnp.log1p(jnp.exp(-jnp.abs(raw)))
        step_out[here, :] = step
        decay = -step * rate[...]
        for part in (0, 1):
            piece = decay[part * CHUNK : (part + 1) * CHUNK, :]
            cum_out[pl.ds(at + part * CHUNK, CHUNK), :] = jnp.dot(
                lower, piece, precision=HIGH, preferred_element_type=F32
            )
        mixed = jnp.dot(rows, w_all[...], preferred_element_type=F32).astype(BF16)
        conv_out[here, :] = mixed[:, :640]
        z_out[here, :] = silu(mixed[:, 640:].astype(F32))


def conv_chunk(prior, here, seg, w_conv):
    joined = jnp.concatenate([prior, here], axis=0)
    total = here * w_conv[3:4, :]
    own = seg[16:, :]
    for lag in (1, 2, 3):
        kept = (pltpu.roll(seg, lag, 0)[16:, :] == own).astype(F32)
        moved = pltpu.roll(joined, lag, 0)[16:, :]
        total = total + (kept * moved) * w_conv[3 - lag : 4 - lag, :]
    return silu(total).astype(BF16)


def fresh_state(mixed, step, cum, seg, last_seg):
    last = cum[CHUNK - 1 : CHUNK, :]
    tail = jnp.where(seg == last_seg, jnp.exp(last - cum), 0.0)
    drive = mixed[:, :WIDE].astype(F32) * spread(step * tail)
    return lax.dot_general(
        mixed[:, WIDE : WIDE + STATE], drive.astype(BF16), (((0,), (0,)), ((), ())), preferred_element_type=F32
    )


def conv_kernel(meta, conv_in, seg_ext, step, cum, w_conv, x_out, bc_out, fresh_out):
    def chunk(c, carry):
        start = pl.multiple_of(c * CHUNK, CHUNK)
        rows = pl.ds(start, CHUNK)
        seg = seg_ext[pl.ds(start, CHUNK + 16), :]
        prior = conv_in[pl.ds(pl.multiple_of(start - 16, 16), 16), :].astype(F32)
        mixed = conv_chunk(prior, conv_in[rows, :].astype(F32), seg, w_conv)
        x_out[rows, :] = mixed[:, :WIDE]
        bc_out[rows, :] = mixed[:, WIDE:]
        fresh_out[c] = fresh_state(mixed, step[rows, :], cum[rows, :], seg[16:, :], meta[16 + c])
        return carry

    lax.fori_loop(1, 8, chunk, 0)


def row_spread(row):
    return spread(jnp.broadcast_to(row, (8, LANES)))[:1, :]


def chain_kernel(meta, conv_in, edge, seg_ext, step, cum, w_conv, fresh, x_in, bc_in, x_out, bc_out, state_out, send_out, past_out):
    before_dev = meta[0]
    seg = seg_ext[: CHUNK + 16, :]
    mixed = conv_chunk(edge[...].astype(F32), conv_in[:CHUNK, :].astype(F32), seg, w_conv)
    x_out[:CHUNK, :] = mixed[:, :WIDE]
    bc_out[:CHUNK, :] = mixed[:, WIDE:]
    first = fresh_state(mixed, step[:CHUNK, :], cum[:CHUNK, :], seg[16:, :], meta[16])
    held = jnp.zeros((STATE, WIDE), F32)
    past = jnp.zeros((1, LANES), F32)
    for c in range(8):
        last = cum[(c + 1) * CHUNK - 1 : (c + 1) * CHUNK, :]
        state_out[c] = held.astype(BF16)
        past_out[c : c + 1, :] = past
        persist = row_spread(jnp.where(meta[16 + c] == meta[8 + c], jnp.exp(last), 0.0))
        held = persist * held + (first if c == 0 else fresh[c])
        past = past + last
    send_out[:STATE, :] = held.astype(BF16)
    passed = jnp.where(meta[16 + 7] == before_dev, jnp.exp(past), 0.0)
    wide = spread(jnp.broadcast_to(passed, (16, LANES)))
    high = wide.astype(BF16)
    low = (wide - high.astype(F32)).astype(BF16)
    row = lax.broadcasted_iota(jnp.int32, (16, WIDE), 0)
    send_out[STATE:, :] = jnp.where(row == 0, high, low)


def factor_of(message):
    both = message[STATE:, :].astype(F32)
    return both[0:1, :] + both[1:2, :]


def pair_kernel(sent, got, out):
    own_factor, got_factor = factor_of(sent), factor_of(got)
    out[:STATE, :] = (sent[:STATE, :].astype(F32) + own_factor * got[:STATE, :].astype(F32)).astype(BF16)
    wide = jnp.broadcast_to(own_factor * got_factor, (16, WIDE))
    high = wide.astype(BF16)
    low = (wide - high.astype(F32)).astype(BF16)
    row = lax.broadcasted_iota(jnp.int32, (16, WIDE), 0)
    out[STATE:, :] = jnp.where(row == 0, high, low)


def entering_state(near, far):
    return near[:STATE, :].astype(F32) + factor_of(near) * far[:STATE, :].astype(F32)


def open_kernel(meta, near, far, cum, past, ends_in, ends_out):
    at = meta[66]
    total = cum[pl.ds(at, 1), :] + past[pl.ds(at // CHUNK, 1), :]
    hold = row_spread(jnp.where(meta[65] > 0, jnp.exp(total), 0.0))
    value = ends_in[0].astype(F32)
    ends_out[0] = jnp.where(meta[65] > 0, value + hold * entering_state(near, far), value).astype(BF16)


def local_kernel(meta, x_in, bc_in, cum_in, step_in, seg_ext, seg_row, state_in, skip, *rest, first, last):
    y_out = rest[-1]
    rows_i = lax.broadcasted_iota(jnp.int32, (CHUNK, CHUNK), 0)
    cols_i = lax.broadcasted_iota(jnp.int32, (CHUNK, CHUNK), 1)
    causal = rows_i >= cols_i
    left = lax.broadcasted_iota(jnp.int32, (CHUNK, LANES), 1) < HALF

    def chunk(c):
        start = pl.multiple_of(c * CHUNK, CHUNK)
        rows = pl.ds(start, CHUNK)
        x = x_in[rows, :].astype(F32)
        b_rows, c_rows = bc_in[rows, :STATE], bc_in[rows, STATE:]
        cum = cum_in[rows, :]
        cum_t = cum.T
        seg = seg_ext[pl.ds(start + 16, CHUNK), :]
        mask = causal & (seg == seg_row[pl.ds(c, 1), :])
        scores = lax.dot_general(c_rows, b_rows, (((1,), (1,)), ((), ())), preferred_element_type=F32)
        scores = jnp.where(mask, scores, 0.0)
        drive_b = (x * spread(step_in[rows, :])).astype(BF16)
        entry = jnp.where(seg == meta[8 + c], jnp.exp(cum), 0.0)
        carried = jnp.dot(c_rows, state_in[c], preferred_element_type=F32)
        total = spread(entry) * carried + skip[...] * x
        for pair in range(HEADS // 2):
            block = drive_b[:, pair * LANES : (pair + 1) * LANES]
            zero = jnp.zeros_like(block)
            acc = total[:, pair * LANES : (pair + 1) * LANES]
            for side in (0, 1):
                head = 2 * pair + side
                gap = jnp.minimum(cum[:, head : head + 1] - cum_t[head : head + 1, :], 0.0)
                weights = (scores * jnp.exp(gap)).astype(BF16)
                value = jnp.where(left, block, zero) if side == 0 else jnp.where(left, zero, block)
                acc = acc + jnp.dot(weights, value, preferred_element_type=F32)
            y_out[rows, pair * LANES : (pair + 1) * LANES] = acc

    def two_chunks(i, carry):
        chunk(first + 2 * i)
        chunk(first + 2 * i + 1)
        return carry

    lax.fori_loop(0, (last - first) // 2, two_chunks, 0)


def ends_kernel(meta, x_in, bc_in, cum_in, step_in, seg_ext, state_in, ends_out):
    def close(req, carry):
        at = meta[32 + req]

        @pl.when((at >= 0) & (at < 8 * CHUNK))
        def _():
            c = at // CHUNK
            rows = pl.ds(pl.multiple_of(c * CHUNK, CHUNK), CHUNK)
            cum = cum_in[rows, :]
            cum_end = cum_in[pl.ds(at, 1), :]
            seg = seg_ext[pl.ds(c * CHUNK + 16, CHUNK), :]
            weight = jnp.where(seg == req, jnp.exp(jnp.minimum(cum_end - cum, 0.0)), 0.0)
            drive = x_in[rows, :].astype(F32) * spread(step_in[rows, :] * weight)
            fresh = lax.dot_general(
                bc_in[rows, :STATE], drive.astype(BF16), (((0,), (0,)), ((), ())), preferred_element_type=F32
            )
            hold = row_spread(jnp.where(req == meta[8 + c], jnp.exp(cum_end), 0.0))
            ends_out[meta[48 + req]] = (fresh + hold * state_in[c].astype(F32)).astype(BF16)

        return carry

    lax.fori_loop(meta[24], meta[16 + 7] + 1, close, 0)


def out_kernel(where, meta, y_in, bc_in, cum_in, seg_ext, past, z_in, near, far, norm_gain, w_out, *rest, mate):
    gated = rest[-1]
    core = core_of(where)
    if mate:
        core = 1 - core
    state = entering_state(near, far).astype(BF16)
    squares = []
    for rel in range(4):
        block = lax.rem(chip_of(where) + rel, 4) * 2 + core
        start = pl.multiple_of(block * ROWS, ROWS)
        rows = pl.ds(start, ROWS)
        carried = jnp.dot(bc_in[rows, STATE:], state, preferred_element_type=F32)
        seg = seg_ext[pl.ds(start + 16, ROWS), :]
        lead = jnp.where(seg == meta[0], jnp.exp(cum_in[rows, :] + past[pl.ds(block, 1), :]), 0.0)
        g = (y_in[rows, :] + spread(lead) * carried) * z_in[rows, :]
        squares.append(jnp.broadcast_to(jnp.sum(g * g, axis=1, keepdims=True), (ROWS, LANES)))
        gated[rel * ROWS : (rel + 1) * ROWS, :] = (g * norm_gain[...]).astype(BF16)

    if mate:
        (out,) = rest[:-1]
        for pair in (0, 1):
            mixed = jnp.dot(gated[pair * 256 : (pair + 1) * 256, :], w_out[...], preferred_element_type=F32)
            for rel in (2 * pair, 2 * pair + 1):
                at = (rel - 2 * pair) * ROWS
                out[rel, :, :1536] = mixed[at : at + ROWS, :].astype(BF16)
                out[rel, :, 1536:] = squares[rel].astype(BF16)
    else:
        other, send_a, send_b, kept_0, kept_1, kept_3 = rest[:-1]
        places = (
            ((kept_0, 0), (kept_0, HALF)),
            ((kept_1, 0), (send_a, HALF)),
            ((send_a, 0), (send_b, HALF)),
            ((send_b, 0), (kept_3, 0)),
        )
        for pair in (0, 1):
            mixed = jnp.dot(gated[pair * 256 : (pair + 1) * 256, :], w_out[...], preferred_element_type=F32)
            for rel in (2 * pair, 2 * pair + 1):
                at = (rel - 2 * pair) * ROWS
                for side, (ref, to) in enumerate(places[rel]):
                    lo = side * HALF
                    ref[to : to + HALF, :1536] = (
                        mixed[at + lo : at + lo + HALF, :] + other[rel, lo : lo + HALF, :1536].astype(F32)
                    ).astype(BF16)
                    ref[to : to + HALF, 1536:] = (
                        squares[rel][lo : lo + HALF, :] + other[rel, lo : lo + HALF, 1536:].astype(F32)
                    ).astype(BF16)


def enter_kernel(h0, p_a, p_b, q_a, q_b, tokens, gain, spots, residual_out, normed_out, outgoing, held):
    @pl.when(pl.program_id(0) == 0)
    def _():
        first = h0[:HALF, :].astype(F32) + p_b[:HALF, :].astype(F32) + q_a[...].astype(F32)
        second = h0[HALF:, :].astype(F32) + p_a[HALF:, :].astype(F32) + q_b[...].astype(F32)
        both = jnp.concatenate([first, second], axis=0)
        scale = lax.rsqrt(both[:, 1536:1537] * (1.0 / DI) + EPS)
        residual = tokens[...].astype(F32) + both[:, :1536] * scale
        residual_out[...] = residual
        meansq = jnp.mean(residual * residual, axis=-1, keepdims=True)
        normed = (residual * lax.rsqrt(meansq + EPS) * gain[...]).astype(BF16)
        normed_out[...] = normed
        held[...] = normed

    outgoing[...] = jnp.dot(spots[...], held[...], preferred_element_type=F32).astype(BF16)


def expert_kernel(rows_ref, gate, up, down, out, total):
    rows = rows_ref[:, pl.program_id(0)].reshape(256, 1536)
    g = jnp.dot(rows, gate[...], preferred_element_type=F32)
    u = jnp.dot(rows, up[...], preferred_element_type=F32)
    hidden = (silu(g) * u).astype(BF16)
    term = jnp.dot(hidden, down[...], preferred_element_type=F32)

    @pl.when(pl.program_id(1) == 0)
    def _():
        total[...] = term

    @pl.when(pl.program_id(1) == 1)
    def _():
        out[...] = (total[...] + term).astype(BF16).reshape(16, CAP, 1536)


def shared_kernel(rows_ref, w0, w1, w2, w3, w4, w5, w6, w7, residual, out):
    rows = rows_ref[...]
    total = residual[...]
    for w in (w0, w1, w2, w3, w4, w5, w6, w7):
        both = lax.dot_general(rows, w[:256, :], (((1,), (1,)), ((), ())), preferred_element_type=F32)
        hidden = (silu(both[:, :128]) * both[:, 128:]).astype(BF16)
        total = total + jnp.dot(hidden, w[256:, :], preferred_element_type=F32)
    out[...] = total


def leave_kernel(returned, mix, base, out):
    out[...] = (base[...] + jnp.dot(mix[...], returned[...], preferred_element_type=F32)).astype(BF16)


def vmem(dims, dtype):
    return pltpu.VMEM(dims, dtype)


def hbm(dims, dtype):
    return pltpu.HBM(dims, dtype)


def limit(mib):
    return pltpu.CompilerParams(vmem_limit_bytes=mib << 20)


def shape(dims, dtype):
    return jax.ShapeDtypeStruct(dims, dtype)


def body(
    tokens,
    in_gain,
    in_z,
    in_x,
    in_bc,
    in_dt,
    conv_x,
    conv_bc,
    dt_bias,
    a_log,
    d_skip,
    norm_gain,
    out_w,
    post_gain,
    sh_gate,
    sh_up,
    sh_down,
    ex_gate,
    ex_up,
    ex_down,
    routes,
    gates,
    lengths,
    cache_slot,
):
    seq_idx = lax.axis_index("seq")
    exp_idx = lax.axis_index("exp")
    where_am_i = jnp.reshape(exp_idx, (1,)).astype(jnp.int32)
    width = tokens.shape[1]
    row_count = 8 * ROWS

    up = over_exp(tokens, PLUS)
    down = over_exp(tokens, MINUS)
    mate = over_exp(tokens, MATE)

    (w_all, w_dt, bias, rate, skip, taps, seg_ext, seg_row, gain_in, gain_mix, gain_post, meta) = pl.pallas_call(
        tables_kernel,
        out_shape=(
            vmem((width, 1024), BF16),
            vmem((LANES, width), BF16),
            vmem((1, LANES), F32),
            vmem((1, LANES), F32),
            vmem((1, WIDE), F32),
            vmem((4, 640), F32),
            vmem((row_count + 16, 1), jnp.int32),
            vmem((8, CHUNK), jnp.int32),
            vmem((1, width), F32),
            vmem((1, WIDE), F32),
            vmem((1, width), F32),
            shape((80,), jnp.int32),
        ),
        in_specs=[SM] * 6 + [VM] * 6 + [ANY] * 3,
        out_specs=(VM,) * 11 + (SM,),
        scratch_shapes=[pltpu.SemaphoreType.DMA((3,))],
        compiler_params=limit(16),
        name="tables",
    )(
        seq_idx.reshape(1).astype(jnp.int32),
        lengths,
        cache_slot,
        dt_bias,
        a_log,
        d_skip,
        in_dt.T,
        conv_x,
        conv_bc,
        in_gain,
        norm_gain,
        post_gain,
        *far_core(in_x, in_bc, in_z),
    )

    picks = (routes[:, :, None] == jnp.arange(64, dtype=jnp.int32)).astype(F32)
    named = jnp.sum(picks, axis=1)
    weight = jnp.sum(picks * gates[:, :, None], axis=1)
    earlier = (jnp.arange(ROWS)[:, None] > jnp.arange(ROWS)[None, :]).astype(BF16)
    rank = jnp.dot(earlier, named.astype(BF16), preferred_element_type=F32)
    rank = jnp.where(named > 0, rank, -1.0)
    slots = jnp.arange(1024, dtype=jnp.int32)
    fan = (slots[None, :] // CAP == jnp.arange(64, dtype=jnp.int32)[:, None]).astype(BF16)
    rank_wide = jnp.dot(rank.astype(BF16), fan, preferred_element_type=F32)
    hit = rank_wide == (slots % CAP).astype(F32)[None, :]
    w_high = weight.astype(BF16)
    mix = jnp.where(hit, jnp.dot(w_high, fan, preferred_element_type=F32), 0.0).astype(BF16)
    spots = hit.astype(BF16).T

    def project(plan, blocks, *done):
        return pl.pallas_call(
            functools.partial(project_kernel, plan=plan),
            out_shape=(
                vmem((row_count, 640), BF16),
                vmem((row_count, LANES), F32),
                vmem((row_count, LANES), F32),
                vmem((row_count, WIDE), F32),
            ),
            in_specs=[SM] + [VM] * (len(blocks) + 5 + len(done)),
            out_specs=(VM,) * 4,
            scratch_shapes=[pltpu.VMEM((2 * ROWS, width), BF16)],
            input_output_aliases={len(blocks) + 6 + i: i for i in range(len(done))},
            compiler_params=limit(16),
            name="project",
        )(where_am_i, *near_core(*blocks, gain_in, w_all, w_dt, bias, rate, *done))

    done = project(((0, ((0, 0, ROWS, True, 0), (1, 0, ROWS, False, 0))),), (tokens, mate))
    up, down, done = lax.optimization_barrier((up, down, done))
    both, up_low, down_high = pl.pallas_call(
        join_kernel,
        out_shape=(
            vmem((2 * ROWS, width), BF16),
            vmem((HALF, width), BF16),
            vmem((HALF, width), BF16),
        ),
        in_specs=[VM] * 2,
        out_specs=(VM,) * 3,
        compiler_params=limit(16),
        name="join",
    )(*near_core(up, down))
    far_a = over_exp(up_low, PLUS)
    far_b = over_exp(down_high, MINUS)
    both_mate = over_exp(both, MATE)
    done = project(
        (
            (3, ((0, 0, ROWS, True, 0), (1, 0, ROWS, False, 0))),
            (1, ((0, ROWS, ROWS, True, 0), (1, ROWS, ROWS, False, 0))),
        ),
        (both, both_mate),
        *done,
    )
    far_a, far_b, done = lax.optimization_barrier((far_a, far_b, done))
    conv_in, step, cum, z = project(
        ((2, ((0, 0, HALF, True, 0), (1, 0, HALF, True, HALF), (2, 0, HALF, False, 0), (3, 0, HALF, False, HALF))),),
        (far_a, far_b, over_exp(far_a, MATE), over_exp(far_b, MATE)),
        *done,
    )

    edge = ahead(conv_in[row_count - 16 :], 1)
    x_rows, bc_rows, fresh = pl.pallas_call(
        conv_kernel,
        out_shape=(
            vmem((row_count, WIDE), BF16),
            vmem((row_count, 2 * STATE), BF16),
            vmem((8, STATE, WIDE), F32),
        ),
        in_specs=[SM] + [VM] * 5,
        out_specs=(VM,) * 3,
        compiler_params=limit(16),
        name="conv",
    )(meta, *near_core(conv_in, seg_ext, step, cum, taps))
    x_rows, bc_rows, states, sent, past = pl.pallas_call(
        chain_kernel,
        out_shape=(
            vmem((row_count, WIDE), BF16),
            vmem((row_count, 2 * STATE), BF16),
            vmem((8, STATE, WIDE), BF16),
            vmem((STATE + 16, WIDE), BF16),
            vmem((8, LANES), F32),
        ),
        in_specs=[SM] + [VM] * 9,
        out_specs=(VM,) * 5,
        input_output_aliases={8: 0, 9: 1},
        compiler_params=limit(16),
        name="chain",
    )(meta, *near_core(conv_in, edge, seg_ext, step, cum, taps, fresh, x_rows, bc_rows))

    def local_part(first, last, *done):
        return pl.pallas_call(
            functools.partial(local_kernel, first=first, last=last),
            out_shape=vmem((row_count, WIDE), F32),
            in_specs=[SM] + [VM] * (8 + len(done)),
            out_specs=VM,
            input_output_aliases={9: 0} if done else {},
            compiler_params=limit(16),
            name="local",
        )(meta, *near_core(x_rows, bc_rows, cum, step, seg_ext, seg_row, states, skip, *done))

    got = ahead(sent, 1)
    y_local = local_part(0, 4)
    got, y_local = lax.optimization_barrier((got, y_local))
    two = pl.pallas_call(
        pair_kernel,
        out_shape=vmem((STATE + 16, WIDE), BF16),
        in_specs=[VM, VM],
        out_specs=VM,
        compiler_params=limit(16),
        name="pair",
    )(*near_core(sent, got))
    two, y_local = lax.optimization_barrier((two, y_local))
    near = ahead(two, 1)
    far = ahead(two, 3)
    y_local = local_part(4, 8, y_local)
    near, far, y_local, states = lax.optimization_barrier((near, far, y_local, states))

    def project_out(mate, *other):
        wide = width + LANES
        if mate:
            outs = vmem((4, ROWS, wide), BF16)
        else:
            outs = tuple(vmem((rows, wide), BF16) for rows in (ROWS, ROWS, ROWS, HALF, HALF))
        return pl.pallas_call(
            functools.partial(out_kernel, mate=mate),
            out_shape=outs,
            in_specs=[SM, SM] + [VM] * (10 + len(other)),
            out_specs=VM if mate else (VM,) * 5,
            scratch_shapes=[pltpu.VMEM((4 * ROWS, WIDE), BF16)],
            compiler_params=limit(16),
            name="out_mate" if mate else "out_own",
        )(
            where_am_i,
            meta,
            *near_core(y_local, bc_rows, cum, seg_ext, past, z, near, far, gain_mix, out_w, *other),
        )

    mate_part = project_out(True)
    swapped = over_exp(mate_part, MATE)

    mate_part, states = lax.optimization_barrier((mate_part, states))
    ends_local = pl.pallas_call(
        ends_kernel,
        out_shape=shape((16, STATE, WIDE), BF16),
        in_specs=[SM] + [VM] * 6,
        out_specs=VM,
        compiler_params=limit(16),
        name="ends",
    )(meta, *near_core(x_rows, bc_rows, cum, step, seg_ext, states))
    slot_block = pl.BlockSpec((1, STATE, WIDE), lambda i, meta: (meta[64], 0, 0))
    ends_local = pl.pallas_call(
        open_kernel,
        out_shape=shape((16, STATE, WIDE), BF16),
        grid_spec=pltpu.PrefetchScalarGridSpec(
            num_scalar_prefetch=1,
            grid=(1,),
            in_specs=[VM] * 4 + [slot_block],
            out_specs=slot_block,
        ),
        input_output_aliases={5: 0},
        compiler_params=limit(16),
        name="open",
    )(meta, *near_core(near, far, cum, past), ends_local)
    send_a, send_b, kept_0, kept_1, kept_3 = project_out(False, swapped)
    send_a, send_b, ends_local = lax.optimization_barrier((send_a, send_b, ends_local))
    p_a = over_exp(send_a, PLUS)
    p_b = over_exp(send_b, MINUS)
    ends_all = lax.all_to_all(ends_local, "seq", split_axis=0, concat_axis=0, tiled=True)
    q_a = over_exp((kept_1.astype(F32) + p_a[:HALF].astype(F32)).astype(BF16), PLUS)
    q_b = over_exp((kept_3.astype(F32) + p_b[HALF:].astype(F32)).astype(BF16), MINUS)

    residual, normed, outgoing = pl.pallas_call(
        enter_kernel,
        out_shape=(hbm((ROWS, width), F32), hbm((ROWS, width), BF16), hbm((1024, width), BF16)),
        grid=(4,),
        in_specs=[VM] * 7 + [pl.BlockSpec((256, ROWS), lambda i: (i, 0))],
        out_specs=(VM, VM, pl.BlockSpec((256, width), lambda i: (i, 0))),
        scratch_shapes=[pltpu.VMEM((ROWS, width), BF16)],
        compiler_params=limit(16),
        name="enter",
    )(*near_core(kept_0, p_a, p_b, q_a, q_b, tokens, gain_post), spots)
    received = lax.all_to_all(
        outgoing.reshape(16, 4, CAP, width), "seq", split_axis=0, concat_axis=0, tiled=True
    )
    sh_gate, sh_up, sh_down, ends_all, outgoing = lax.optimization_barrier(
        (sh_gate, sh_up, sh_down, ends_all, outgoing)
    )
    final = lax.dynamic_index_in_dim(ends_all, meta[67], 0, False).astype(F32)
    state_cache = final.T.reshape(1, HEADS, HALF, STATE)
    packed = jnp.concatenate([sh_gate.T, sh_up.T, sh_down])
    half = packed.shape[0] // 2
    g_up = over_exp(packed, PLUS)
    g_down = over_exp(packed, MINUS)
    g_mate = over_exp(packed, MATE)
    received, g_up, g_down, g_mate, state_cache = lax.optimization_barrier(
        (received, g_up, g_down, g_mate, state_cache)
    )
    answers = pl.pallas_call(
        expert_kernel,
        out_shape=hbm((16, 4, CAP, width), BF16),
        grid=(4, 2),
        in_specs=[
            VM,
            pl.BlockSpec((None, width, 256), lambda e, f: (e, 0, f)),
            pl.BlockSpec((None, width, 256), lambda e, f: (e, 0, f)),
            pl.BlockSpec((None, 256, width), lambda e, f: (e, f, 0)),
        ],
        out_specs=pl.BlockSpec((16, None, CAP, width), lambda e, f: (0, e, 0, 0)),
        scratch_shapes=[pltpu.VMEM((256, width), F32)],
        compiler_params=limit(20),
        name="experts",
    )(*near_core(received), *far_core(ex_gate, ex_up, ex_down))
    returned = lax.all_to_all(answers, "seq", split_axis=0, concat_axis=0, tiled=True)
    g_up, g_down, answers = lax.optimization_barrier((g_up, g_down, answers))
    g_far = jnp.concatenate([over_exp(g_up[:half], PLUS), over_exp(g_down[half:], MINUS)])
    groups = (packed, g_mate, g_up, over_exp(g_up, MATE), g_down, over_exp(g_down, MATE), g_far, over_exp(g_far, MATE))
    base = pl.pallas_call(
        shared_kernel,
        out_shape=hbm((ROWS, width), F32),
        in_specs=[VM] * 10,
        out_specs=VM,
        compiler_params=limit(16),
        name="shared",
    )(normed, *groups, residual)
    layer_out = pl.pallas_call(
        leave_kernel,
        out_shape=shape((ROWS, width), BF16),
        in_specs=[VM] * 3,
        out_specs=VM,
        compiler_params=limit(16),
        name="leave",
    )(*near_core(returned.reshape(1024, width), mix), *far_core(base))
    return (layer_out, state_cache)


def solution(mesh):
    placed = (
        P(("seq", "exp"), None),
        P(),
        P(None, "exp"),
        P(None, "exp"),
        P(),
        P(None, "exp"),
        P(None, "exp"),
        P(),
        P("exp"),
        P("exp"),
        P("exp"),
        P("exp"),
        P("exp", None),
        P(),
        P(None, "exp"),
        P(None, "exp"),
        P("exp", None),
        P("seq", None, None),
        P("seq", None, None),
        P("seq", None, None),
        P(("seq", "exp"), None),
        P(("seq", "exp"), None),
        P(),
        P(),
    )
    return jax.shard_map(
        body,
        mesh=mesh,
        in_specs=placed,
        out_specs=(P(("seq", "exp"), None), P("seq", "exp", None, None)),
        check_vma=False,
    )
```

time: 258 us -> 209 us (0.81)
  other arithmetic: 20.5 us -> 3.96 us
  local copies, waits for them, and re-layouts: 27.5 us -> 14.4 us
  Pallas kernels: 66.9 us -> 58.1 us
  between operations: 7.22 us -> 3.06 us
    all_to_all x1, waiting for transfers between devices: 34.1 us -> 7.74 us  [body(): lax.all_to_all(outgoing.reshape(16, 4, CAP, width), 'seq', split_axis=0,...]
    ppermute x21, waiting for transfers between devices: 28.9 us -> 49.3 us  [over_exp(): return lax.ppermute(block, 'exp', route)]
    all_to_all x1, waiting for transfers between devices: 2.85 us -> 13.5 us  [body(): lax.all_to_all(answers, 'seq', split_axis=0, concat_axis=0, tiled=True)]
    pallas_call x8 -> x17, Pallas kernels: 63 us -> 55.7 us  [the longest x1 13.4 us: body(): pl.pallas_call(expert_kernel, out_shape=hbm((16, 4, CAP, width), BF16), g...]
    ppermute x4, waiting for transfers between devices: 5.09 us -> 0.01 us  [ahead(): lax.ppermute(block, 'seq', [(i, i + distance) for i in range(16 - distanc...]
    concatenate x5 -> x0, other arithmetic: 4.91 us -> none  [the longest x1 2.64 us: body(): w_conv_in = jnp.concatenate([in_x, in_bc], axis=1)]
    convert_element_type x8 -> x2, other arithmetic: 3.53 us -> 0.1 us  [the longest x1 0.05 us: body(): (kept_3.astype(F32) + p_b[HALF:].astype(F32)).astype(BF16)]
    dynamic_slice x5 -> x0, local copies, waits for them, and re-layouts: 3.37 us -> none  [the longest x1 0.9 us: body(): lax.dynamic_index_in_dim(ends_local, open_slot, 0, False).astype(F32)]
  transfers between devices with their start and end apart: 28 -> 28, of which waited for: 12 -> 12; matrix products, arithmetic and copies ran while one was open for 15% -> 6% of each run, Pallas kernels for 13% -> 17%
where the time goes in v2:
time: 209 us; the launch traced here: 207 us
  waiting for transfers between devices  70.5 us (34%)
  Pallas kernels  58.1 us (28%)
  starting transfers between devices  56.6 us (27%)
  local copies, waits for them, and re-layouts  14.4 us (7%)
  other arithmetic  3.96 us (2%)
  between operations  3.06 us (1%)
    ppermute x21, waiting for transfers between devices, over_exp(): return lax.ppermute(block, 'exp', route)  49.3 us
    ppermute x21, starting transfers between devices, over_exp(): return lax.ppermute(block, 'exp', route)  21.6 us
    ppermute x4, starting transfers between devices, ahead(): lax.ppermute(block, 'seq', [(i, i + distance) for i in range(16 - distanc...  17.6 us
    all_to_all x1, waiting for transfers between devices, body(): lax.all_to_all(answers, 'seq', split_axis=0, concat_axis=0, tiled=True)  13.5 us
    pallas_call x1, Pallas kernels, body(): pl.pallas_call(expert_kernel, out_shape=hbm((16, 4, CAP, width), BF16), g...  13.4 us
    all_to_all x1, waiting for transfers between devices, body(): lax.all_to_all(outgoing.reshape(16, 4, CAP, width), 'seq', split_axis=0,...  7.74 us
    pallas_call x3, Pallas kernels, project(): pl.pallas_call(functools.partial(project_kernel, plan=plan), out_shape=(v...  7.69 us
    unnamed x41, local copies, waits for them, and re-layouts  7.55 us
  transfers between devices with their start and end apart: 28, of which 12 were waited for; matrix products, arithmetic and copies ran while one was open for 6% of the time, Pallas kernels for 17%

profile of v2, /device:TPU:0, one launch (start us, length us, event | category | flops | bytes accessed | tf_op | source)
XLA Modules:
  0.0 207.3 jit_solution(3934122697934348260)
XLA Ops:
  0.7 1.8 collective-permute-start
  2.5 1.5 collective-permute-start.1
  4.0 0.7 copy-done.4
  11.5 3.1 %tables.1 = (bf16[1536,1024]{1,0:T(8,128)(2,1)S(1)}, bf16[128,1536]{1,0:T(8,128)(2,1)S(1)}, f32[1,128]{1,0:T(1,128)S(1)}, f32[1,128]{1,0:T(1,128)S(1)}, f32[1,38...) custom-call(s32[1]{0:T(128)} %bitcast.1.seq, ...), custom_call_target="tpu_custom_call" | custom-call | tf_op jit(solution)/shard_map/tables/pallas_call | solution.py:486
  14.6 2.0 project.3
  17.3 2.8 %collective-permute-start.4 = (bf16[64,1536]{1,0:T(8,128)(2,1)S(1)}, bf16[64,1536]{1,0:T(8,128)(2,1)S(1)}, u32[]{:S(2)}, u32[]{:S(2)}) collective-permute-start(bf16[64,1536]{1,0:T(8,128)(2,1)S(1)} %get-tuple-element.93), channel_id=1, source_target_pairs={{0,6},{1,7},{2,0},{3,1},{4,2},{5,3},{6,4},{7,5},{8,14},{9,15},{10,... | collective-permute-start | bytes 589832 | tf_op jit(solution)/shard_map/ppermute | solution.py:49
  20.1 3.8 %project.4 = (bf16[1024,640]{1,0:T(8,128)(2,1)S(1)}, f32[1024,128]{1,0:T(8,128)S(1)}, f32[1024,128]{1,0:T(8,128)S(1)}, f32[1024,384]{1,0:T(8,128)S(1)}) custom-call(s32[1]{0:T(128)} %bitcast.where, bf16[256,1536]{1,0:T(8,128)(2,1)S(1)} %get-tuple-element.94.refs_0_, ...), custom_call_target="tpu_custom_call", output_to_operand_aliasing={{0}: (8, {}), {1}: (9, {}), {2}: (10, {}), {3}: (11, {})} | custom-call | tf_op jit(solution)/shard_map/project/pallas_call | solution.py:538
  23.9 1.4 collective-permute-done.3.refs_0_
  25.8 0.9 collective-permute-done.6.refs_2_
  27.0 2.0 project.5
  29.0 3.9 %collective-permute-start.8 = (bf16[16,640]{1,0:T(8,128)(2,1)S(1)}, bf16[16,640]{1,0:T(8,128)(2,1)S(1)}, u32[]{:S(2)}, u32[]{:S(2)}) collective-permute-start(bf16[16,640]{1,0:T(8,128)(2,1)S(1)} %slice.18), channel_id=1, source_target_pairs={{0,8},{8,16},{16,24},{24,32},{32,40},{40,48},{48,56},{56,64},{64,7... | collective-permute-start | bytes 61448 | tf_op jit(solution)/shard_map/ppermute | solution.py:45
  33.0 4.2 %conv.1 = (bf16[1024,384]{1,0:T(8,128)(2,1)S(1)}, bf16[1024,256]{1,0:T(8,128)(2,1)S(1)}, f32[8,128,384]{2,1,0:T(8,128)S(1)}) custom-call(s32[80]{0:T(128)S(1)} %get-tuple-element.80.meta, bf16[1024,640]{1,0:T(8,128)(2,1)S(1)} %get-tuple-element.109.conv_in, s32[1040,1]{1,0:T(8,128)S(1)} %get-tuple-element.110.seg_ext, ...), custom_call_target="tpu_custom_call" | custom-call | tf_op jit(solution)/shard_map/conv/pallas_call | solution.py:587
  37.2 1.2 chain.1
  38.4 4.0 %collective-permute-start.9 = (bf16[144,384]{1,0:T(8,128)(2,1)S(1)}, bf16[144,384]{1,0:T(8,128)(2,1)S(1)}, u32[]{:S(2)}, u32[]{:S(2)}) collective-permute-start(bf16[144,384]{1,0:T(8,128)(2,1)S(1)} %get-tuple-element.117.sent), channel_id=1, source_target_pairs={{0,8},{8,16},{16,24},{24,32},{32,40},{40,48},{48,56},{56,64},{64,7... | collective-permute-start | bytes 331784 | tf_op jit(solution)/shard_map/ppermute | solution.py:45
  42.4 3.4 %local.2.rest_0_ = f32[1024,384]{1,0:T(8,128)S(1)} custom-call(s32[80]{0:T(128)S(1)} %get-tuple-element.80.meta, bf16[1024,384]{1,0:T(8,128)(2,1)S(1)} %get-tuple-element.118.x_in, bf16[1024,256]{1,0:T(8,128)(2,1)S(1)} %get-tuple-element.119.bc_in, f32[1024,128]{1,0:T(8,128)S(1)} %get-tuple-element.112.cum.cum_in, ...), custom_call_target="tpu_custom_call" | custom-call | tf_op jit(solution)/shard_map/local/pallas_call | solution.py:616
  45.9 3.7 %collective-permute-start.10 = (bf16[144,384]{1,0:T(8,128)(2,1)S(1)}, bf16[144,384]{1,0:T(8,128)(2,1)S(1)}, u32[]{:S(2)}, u32[]{:S(2)}) collective-permute-start(bf16[144,384]{1,0:T(8,128)(2,1)S(1)} %pair.1), channel_id=1, source_target_pairs={{0,8},{8,16},{16,24},{24,32},{32,40},{40,48},{48,56},{56,64},{64,7... | collective-permute-start | bytes 331784 | tf_op jit(solution)/shard_map/ppermute | solution.py:45
  49.5 5.9 %collective-permute-start.11 = (bf16[144,384]{1,0:T(8,128)(2,1)S(1)}, bf16[144,384]{1,0:T(8,128)(2,1)S(1)}, u32[]{:S(2)}, u32[]{:S(2)}) collective-permute-start(bf16[144,384]{1,0:T(8,128)(2,1)S(1)} %pair.1), channel_id=1, source_target_pairs={{0,24},{8,32},{16,40},{24,48},{32,56},{40,64},{48,72},{56,80},{64,... | collective-permute-start | bytes 331784 | tf_op jit(solution)/shard_map/ppermute | solution.py:45
  55.5 3.4 %local.3.y_in = f32[1024,384]{1,0:T(8,128)S(1)} custom-call(s32[80]{0:T(128)S(1)} %get-tuple-element.80.meta, bf16[1024,384]{1,0:T(8,128)(2,1)S(1)} %get-tuple-element.118.x_in, bf16[1024,256]{1,0:T(8,128)(2,1)S(1)} %get-tuple-element.119.bc_in, f32[1024,128]{1,0:T(8,128)S(1)} %get-tuple-element.112.cum.cum_in, ...), custom_call_target="tpu_custom_call", output_to_operand_aliasing={{}: (9, {})} | custom-call | tf_op jit(solution)/shard_map/local/pallas_call | solution.py:616
  58.9 1.9 out_mate.1
  61.6 2.2 %ends.1.ends_in = bf16[16,128,384]{2,1,0:T(8,128)(2,1)} custom-call(s32[80]{0:T(128)S(1)} %get-tuple-element.80.meta, bf16[1024,384]{1,0:T(8,128)(2,1)S(1)} %get-tuple-element.118.x_in, bf16[1024,256]{1,0:T(8,128)(2,1)S(1)} %get-tuple-element.119.bc_in, f32[1024,128]{1,0:T(8,128)S(1)} %get-tuple-element.112.cum.cum_in, ...), custom_call_target="tpu_custom_call" | custom-call | tf_op jit(solution)/shard_map/ends/pallas_call | solution.py:667
  63.8 2.2 %open.1 = bf16[16,128,384]{2,1,0:T(8,128)(2,1)} custom-call(s32[80]{0:T(128)S(1)} %get-tuple-element.80.meta, bf16[144,384]{1,0:T(8,128)(2,1)S(1)} %collective-permute-done.10.near, bf16[144,384]{1,0:T(8,128)(2,1)S(1)} %collective-permute-done.11.far, f32[1024,128]{1,0:T(8,128)S(1)} %get-tuple-element.112.cum.cum_in, ...), custom_call_target="tpu_custom_call", output_to_operand_aliasing={{}: (5, {})} | custom-call | tf_op jit(solution)/shard_map/open/pallas_call | solution.py:676
  66.0 2.7 %out_own.1 = (bf16[128,1664]{1,0:T(8,128)(2,1)S(1)}, bf16[128,1664]{1,0:T(8,128)(2,1)}, bf16[128,1664]{1,0:T(8,128)(2,1)S(1)}, bf16[64,1664]{1,0:T(8,128)(2,1)S(1)}, bf16[64,1664]{1,0:T(8,128)(2,1)S(1)}) custom-call(s32[1]{0:T(128)} %bitcast.where, s32[80]{0:T(128)S(1)} %get-tuple-element.80.meta, f32[1024,384]{1,0:T(8,128)S(1)} %local.3.y_in, ...), custom_call_target="tpu_custom_call" | custom-call | tf_op jit(solution)/shard_map/out_own/pallas_call | solution.py:649
  68.7 2.9 %collective-permute-start.14 = (bf16[128,1664]{1,0:T(8,128)(2,1)}, bf16[128,1664]{1,0:T(8,128)(2,1)S(1)}, u32[]{:S(2)}, u32[]{:S(2)}) collective-permute-start(bf16[128,1664]{1,0:T(8,128)(2,1)} %get-tuple-element.139), channel_id=1, source_target_pairs={{0,6},{1,7},{2,0},{3,1},{4,2},{5,3},{6,4},{7,5},{8,14},{9,15},{10,... | collective-permute-start | bytes 1277960 | tf_op jit(solution)/shard_map/ppermute | solution.py:49
  71.7 6.1 %all-to-all-start.1 = ((bf16[16,128,384]{2,1,0:T(8,128)(2,1)}), bf16[16,128,384]{2,1,0:T(8,128)(2,1)}, u32[]{:S(2)}, u32[]{:S(2)}) async-start(bf16[16,128,384]{2,1,0:T(8,128)(2,1)} %open.1), calls=%async_computation.1 | async-start | bytes 3145728 | tf_op jit(solution)/shard_map/all_to_all | solution.py:693
  78.3 3.4 %collective-permute-done.14.p_b = bf16[128,1664]{1,0:T(8,128)(2,1)S(1)} collective-permute-done((bf16[128,1664]{1,0:T(8,128)(2,1)}, bf16[128,1664]{1,0:T(8,128)(2,1)S(1)}, u32[]{:S(2)}, u32[]{:S(2)}) %collective-permute-start.14) | collective-permute-done | bytes 426016 | tf_op jit(solution)/shard_map/ppermute | solution.py:49
  81.8 3.7 %collective-permute-start.16 = (bf16[64,1664]{1,0:T(8,128)(2,1)S(1)}, bf16[64,1664]{1,0:T(8,128)(2,1)S(1)}, u32[]{:S(2)}, u32[]{:S(2)}) collective-permute-start(bf16[64,1664]{1,0:T(8,128)(2,1)S(1)} %add_convert_fusion), channel_id=1, source_target_pairs={{0,6},{1,7},{2,0},{3,1},{4,2},{5,3},{6,4},{7,5},{8,14},{9,15},{10,... | collective-permute-start | bytes 638984 | tf_op jit(solution)/shard_map/ppermute | solution.py:49
  85.4 5.7 %collective-permute-done.13.p_a = bf16[128,1664]{1,0:T(8,128)(2,1)S(1)} collective-permute-done((bf16[128,1664]{1,0:T(8,128)(2,1)S(1)}, bf16[128,1664]{1,0:T(8,128)(2,1)S(1)}, u32[]{:S(2)}, u32[]{:S(2)}) %collective-permute-start.13) | collective-permute-done | bytes 426016 | tf_op jit(solution)/shard_map/ppermute | solution.py:49
  91.5 7.3 %collective-permute-done.15.q_a = bf16[64,1664]{1,0:T(8,128)(2,1)S(1)} collective-permute-done((bf16[64,1664]{1,0:T(8,128)(2,1)S(1)}, bf16[64,1664]{1,0:T(8,128)(2,1)S(1)}, u32[]{:S(2)}, u32[]{:S(2)}) %collective-permute-start.15) | collective-permute-done | bytes 213024 | tf_op jit(solution)/shard_map/ppermute | solution.py:49
  98.8 3.5 %enter.1 = (f32[128,1536]{1,0:T(8,128)}, bf16[128,1536]{1,0:T(8,128)(2,1)}, bf16[1024,1536]{1,0:T(8,128)(2,1)}) custom-call(bf16[128,1664]{1,0:T(8,128)(2,1)S(1)} %get-tuple-element.133.h0, bf16[128,1664]{1,0:T(8,128)(2,1)S(1)} %collective-permute-done.13.p_a, bf16[128,1664]{1,0:T(8,128)(2,1)S(1)} %collective-permute-done.14.p_b, ...), custom_call_target="tpu_custom_call" | custom-call | tf_op jit(solution)/shard_map/enter/pallas_call | solution.py:697
  102.3 6.5 %all-to-all-start = ((bf16[16,4,16,1536]{3,2,1,0:T(8,128)(2,1)}), bf16[16,4,16,1536]{3,2,1,0:T(8,128)(2,1)S(1)}, u32[]{:S(2)}, u32[]{:S(2)}) async-start(bf16[16,4,16,1536]{3,2,1,0:T(8,128)(2,1)} %bitcast.19), calls=%async_computation | async-start | bytes 6291456 | tf_op jit(solution)/shard_map/all_to_all | solution.py:707
  108.8 1.2 copy.51
  110.0 1.9 copy.52
  111.9 2.2 %pad_maximum_fusion.w0 = bf16[384,1536]{1,0:T(8,128)(2,1)} fusion(bf16[128,1536]{1,0:T(8,128)(2,1)} %param.40, bf16[128,1536]{1,0:T(8,128)(2,1)} %bitcast.21, bf16[128,1536]{1,0:T(8,128)(2,1)S(1)} %bitcast.20), kind=kLoop, calls=%fused_computation.3 | loop fusion | flops 3538944 | bytes 2359296 | tf_op jit(solution)/shard_map/concatenate | solution.py:715
  114.2 3.2 %collective-permute-start.18 = (bf16[384,1536]{1,0:T(8,128)(2,1)}, bf16[384,1536]{1,0:T(8,128)(2,1)}, u32[]{:S(2)}, u32[]{:S(2)}) collective-permute-start(bf16[384,1536]{1,0:T(8,128)(2,1)} %pad_maximum_fusion.w0), channel_id=1, source_target_pairs={{0,6},{1,7},{2,0},{3,1},{4,2},{5,3},{6,4},{7,5},{8,14},{9,15},{10,... | collective-permute-start | bytes 3538952 | tf_op jit(solution)/shard_map/ppermute | solution.py:49
  119.9 0.9 convert_bitcast_fusion.1
  120.8 0.8 copy.53
  121.7 19.6 %collective-permute-done.17.w2 = bf16[384,1536]{1,0:T(8,128)(2,1)} collective-permute-done((bf16[384,1536]{1,0:T(8,128)(2,1)}, bf16[384,1536]{1,0:T(8,128)(2,1)}, u32[]{:S(2)}, u32[]{:S(2)}) %collective-permute-start.17) | collective-permute-done | bytes 1179680 | tf_op jit(solution)/shard_map/ppermute | solution.py:49
  141.3 7.7 %all-to-all-done.rows_ref = bf16[16,4,16,1536]{3,2,1,0:T(8,128)(2,1)S(1)} async-done(((bf16[16,4,16,1536]{3,2,1,0:T(8,128)(2,1)}), bf16[16,4,16,1536]{3,2,1,0:T(8,128)(2,1)S(1)}, u32[]{:S(2)}, u32[]{:S(2)}) %all-to-all-start) | async-done | bytes 3145760 | tf_op jit(solution)/shard_map/all_to_all | solution.py:707
  149.0 13.4 %experts.1 = bf16[16,4,16,1536]{3,2,1,0:T(8,128)(2,1)} custom-call(bf16[16,4,16,1536]{3,2,1,0:T(8,128)(2,1)S(1)} %all-to-all-done.rows_ref, bf16[4,1536,512]{2,1,0:T(8,128)(2,1)} %gate.1, bf16[4,1536,512]{2,1,0:T(8,128)(2,1)} %up.1, bf16[4,512,1536]{2,1,0:T(8,128)(2,1)} %down.1), custom_call_target="tpu_custom_call" | custom-call | tf_op jit(solution)/shard_map/experts/pallas_call | solution.py:723
  162.5 4.9 %all-to-all-start.2 = ((bf16[16,4,16,1536]{3,2,1,0:T(8,128)(2,1)}), bf16[16,4,16,1536]{3,2,1,0:T(8,128)(2,1)S(1)}, u32[]{:S(2)}, u32[]{:S(2)}) async-start(bf16[16,4,16,1536]{3,2,1,0:T(8,128)(2,1)} %experts.1), calls=%async_computation.2 | async-start | bytes 6291456 | tf_op jit(solution)/shard_map/all_to_all | solution.py:738
  167.4 1.1 slice.22
  168.6 1.1 slice.23
  169.7 3.5 %collective-permute-start.23 = (bf16[192,1536]{1,0:T(8,128)(2,1)S(1)}, bf16[192,1536]{1,0:T(8,128)(2,1)S(1)}, u32[]{:S(2)}, u32[]{:S(2)}) collective-permute-start(bf16[192,1536]{1,0:T(8,128)(2,1)S(1)} %slice.23), channel_id=1, source_target_pairs={{0,6},{1,7},{2,0},{3,1},{4,2},{5,3},{6,4},{7,5},{8,14},{9,15},{10,... | collective-permute-start | bytes 1769480 | tf_op jit(solution)/shard_map/ppermute | solution.py:49
  173.7 7.4 %collective-permute-done.22 = bf16[192,1536]{1,0:T(8,128)(2,1)S(1)} collective-permute-done((bf16[192,1536]{1,0:T(8,128)(2,1)S(1)}, bf16[192,1536]{1,0:T(8,128)(2,1)S(1)}, u32[]{:S(2)}, u32[]{:S(2)}) %collective-permute-start.22) | collective-permute-done | bytes 589856 | tf_op jit(solution)/shard_map/ppermute | solution.py:49
  182.2 2.5 %collective-permute-done.24.w7 = bf16[384,1536]{1,0:T(8,128)(2,1)S(1)} collective-permute-done((bf16[384,1536]{1,0:T(8,128)(2,1)S(1)}, bf16[384,1536]{1,0:T(8,128)(2,1)S(1)}, u32[]{:S(2)}, u32[]{:S(2)}) %collective-permute-start.24) | collective-permute-done | bytes 1179680 | tf_op jit(solution)/shard_map/ppermute | solution.py:49
  184.7 6.7 %shared.1.base = f32[128,1536]{1,0:T(8,128)} custom-call(bf16[128,1536]{1,0:T(8,128)(2,1)S(1)} %copy-done.3, bf16[384,1536]{1,0:T(8,128)(2,1)} %pad_maximum_fusion.w0, bf16[384,1536]{1,0:T(8,128)(2,1)} %collective-permute-done.19.w1, bf16[384,1536]{1,0:T(8,128)(2,1)} %collective-permute-done.17.w2, bf16[384,1536]{1,0:T(8,128)(2,1)S(1)} %collective-permute-done.20.w3, ...), custom_call_target="tpu_custom_call" | custom-call | tf_op jit(solution)/shard_map/shared/pallas_call | solution.py:742
  191.4 13.5 %all-to-all-done.2 = bf16[16,4,16,1536]{3,2,1,0:T(8,128)(2,1)S(1)} async-done(((bf16[16,4,16,1536]{3,2,1,0:T(8,128)(2,1)}), bf16[16,4,16,1536]{3,2,1,0:T(8,128)(2,1)S(1)}, u32[]{:S(2)}, u32[]{:S(2)}) %all-to-all-start.2) | async-done | bytes 3145760 | tf_op jit(solution)/shard_map/all_to_all | solution.py:738
  204.9 2.5 %leave.1 = bf16[128,1536]{1,0:T(8,128)(2,1)} custom-call(bf16[1024,1536]{1,0:T(8,128)(2,1)S(1)} %bitcast.17, bf16[128,1024]{1,0:T(8,128)(2,1)S(1)} %fusion.mix, f32[128,1536]{1,0:T(8,128)} %shared.1.base), custom_call_target="tpu_custom_call" | custom-call | tf_op jit(solution)/shard_map/leave/pallas_call | solution.py:750
  (86 shorter events, 12.3 us)
Async XLA Ops:
  0.6 14.0 %collective-permute-start.2 = (bf16[128,1536]{1,0:T(8,128)(2,1)}, bf16[128,1536]{1,0:T(8,128)(2,1)S(1)}, u32[]{:S(2)}, u32[]{:S(2)}) collective-permute-start(bf16[128,1536]{1,0:T(8,128)(2,1)} %tokens.1), channel_id=1, source_target_pairs={{0,1},{1,0},{2,3},{3,2},{4,5},{5,4},{6,7},{7,6},{8,9},{9,8},{10,11... | collective-permute-start | bytes 1179656 | tf_op jit(solution)/shard_map/ppermute | solution.py:49
  0.7 15.9 %collective-permute-start = (bf16[128,1536]{1,0:T(8,128)(2,1)}, bf16[128,1536]{1,0:T(8,128)(2,1)S(1)}, u32[]{:S(2)}, u32[]{:S(2)}) collective-permute-start(bf16[128,1536]{1,0:T(8,128)(2,1)} %tokens.1), channel_id=1, source_target_pairs={{0,2},{1,3},{2,4},{3,5},{4,6},{5,7},{6,0},{7,1},{8,10},{9,11},{10,... | collective-permute-start | bytes 1179656 | tf_op jit(solution)/shard_map/ppermute | solution.py:49
  2.5 14.1 %collective-permute-start.1 = (bf16[128,1536]{1,0:T(8,128)(2,1)}, bf16[128,1536]{1,0:T(8,128)(2,1)S(1)}, u32[]{:S(2)}, u32[]{:S(2)}) collective-permute-start(bf16[128,1536]{1,0:T(8,128)(2,1)} %tokens.1), channel_id=1, source_target_pairs={{0,6},{1,7},{2,0},{3,1},{4,2},{5,3},{6,4},{7,5},{8,14},{9,15},{10,... | collective-permute-start | bytes 1179656 | tf_op jit(solution)/shard_map/ppermute | solution.py:49
  4.0 0.7 copy-start.4
  4.8 0.7 copy-start.5
  5.5 0.7 copy-start.6
  6.2 0.7 copy-start.7
  6.9 0.7 copy-start.8
  7.5 0.7 copy-start.9
  8.2 0.7 copy-start.10
  8.9 0.7 copy-start.11
  9.5 0.7 copy-start.12
  10.2 0.7 copy-start.13
  10.8 0.7 copy-start.14
  11.5 3.1 %copy-start.1 = (bf16[128,1536]{1,0:T(8,128)(2,1)S(1)}, bf16[128,1536]{1,0:T(8,128)(2,1)}, u32[]{:S(2)}) copy-start(bf16[128,1536]{1,0:T(8,128)(2,1)} %tokens.1) | copy-start | bytes 1179652
  16.7 3.4 %collective-permute-start.5 = (bf16[256,1536]{1,0:T(8,128)(2,1)S(1)}, bf16[256,1536]{1,0:T(8,128)(2,1)S(1)}, u32[]{:S(2)}, u32[]{:S(2)}) collective-permute-start(bf16[256,1536]{1,0:T(8,128)(2,1)S(1)} %get-tuple-element.94.refs_0_), channel_id=1, source_target_pairs={{0,1},{1,0},{2,3},{3,2},{4,5},{5,4},{6,7},{7,6},{8,9},{9,8},{10,11... | collective-permute-start | bytes 2359304 | tf_op jit(solution)/shard_map/ppermute | solution.py:49
  16.8 8.5 %collective-permute-start.3 = (bf16[64,1536]{1,0:T(8,128)(2,1)S(1)}, bf16[64,1536]{1,0:T(8,128)(2,1)S(1)}, u32[]{:S(2)}, u32[]{:S(2)}) collective-permute-start(bf16[64,1536]{1,0:T(8,128)(2,1)S(1)} %get-tuple-element.92), channel_id=1, source_target_pairs={{0,2},{1,3},{2,4},{3,5},{4,6},{5,7},{6,0},{7,1},{8,10},{9,11},{10,... | collective-permute-start | bytes 589832 | tf_op jit(solution)/shard_map/ppermute | solution.py:49
  17.3 8.0 %collective-permute-start.4 = (bf16[64,1536]{1,0:T(8,128)(2,1)S(1)}, bf16[64,1536]{1,0:T(8,128)(2,1)S(1)}, u32[]{:S(2)}, u32[]{:S(2)}) collective-permute-start(bf16[64,1536]{1,0:T(8,128)(2,1)S(1)} %get-tuple-element.93), channel_id=1, source_target_pairs={{0,6},{1,7},{2,0},{3,1},{4,2},{5,3},{6,4},{7,5},{8,14},{9,15},{10,... | collective-permute-start | bytes 589832 | tf_op jit(solution)/shard_map/ppermute | solution.py:49
  25.3 1.4 collective-permute-start.6
  25.3 1.7 collective-permute-start.7
  29.0 8.2 %collective-permute-start.8 = (bf16[16,640]{1,0:T(8,128)(2,1)S(1)}, bf16[16,640]{1,0:T(8,128)(2,1)S(1)}, u32[]{:S(2)}, u32[]{:S(2)}) collective-permute-start(bf16[16,640]{1,0:T(8,128)(2,1)S(1)} %slice.18), channel_id=1, source_target_pairs={{0,8},{8,16},{16,24},{24,32},{32,40},{40,48},{48,56},{56,64},{64,7... | collective-permute-start | bytes 61448 | tf_op jit(solution)/shard_map/ppermute | solution.py:45
  38.4 7.4 %collective-permute-start.9 = (bf16[144,384]{1,0:T(8,128)(2,1)S(1)}, bf16[144,384]{1,0:T(8,128)(2,1)S(1)}, u32[]{:S(2)}, u32[]{:S(2)}) collective-permute-start(bf16[144,384]{1,0:T(8,128)(2,1)S(1)} %get-tuple-element.117.sent), channel_id=1, source_target_pairs={{0,8},{8,16},{16,24},{24,32},{32,40},{40,48},{48,56},{56,64},{64,7... | collective-permute-start | bytes 331784 | tf_op jit(solution)/shard_map/ppermute | solution.py:45
  45.9 13.1 %copy-start = (bf16[384,1536]{1,0:T(8,128)(2,1)S(1)}, bf16[384,1536]{1,0:T(8,128)(2,1)}, u32[]{:S(2)}) copy-start(bf16[384,1536]{1,0:T(8,128)(2,1)} %w_out.3) | copy-start | bytes 3538948
  45.9 13.0 %collective-permute-start.10 = (bf16[144,384]{1,0:T(8,128)(2,1)S(1)}, bf16[144,384]{1,0:T(8,128)(2,1)S(1)}, u32[]{:S(2)}, u32[]{:S(2)}) collective-permute-start(bf16[144,384]{1,0:T(8,128)(2,1)S(1)} %pair.1), channel_id=1, source_target_pairs={{0,8},{8,16},{16,24},{24,32},{32,40},{40,48},{48,56},{56,64},{64,7... | collective-permute-start | bytes 331784 | tf_op jit(solution)/shard_map/ppermute | solution.py:45
  49.5 9.4 %collective-permute-start.11 = (bf16[144,384]{1,0:T(8,128)(2,1)S(1)}, bf16[144,384]{1,0:T(8,128)(2,1)S(1)}, u32[]{:S(2)}, u32[]{:S(2)}) collective-permute-start(bf16[144,384]{1,0:T(8,128)(2,1)S(1)} %pair.1), channel_id=1, source_target_pairs={{0,24},{8,32},{16,40},{24,48},{32,56},{40,64},{48,72},{56,80},{64,... | collective-permute-start | bytes 331784 | tf_op jit(solution)/shard_map/ppermute | solution.py:45
  58.9 2.0 copy-start.18
  58.9 2.0 copy-start.19
  60.9 5.1 %collective-permute-start.12 = (bf16[4,128,1664]{2,1,0:T(8,128)(2,1)S(1)}, bf16[4,128,1664]{2,1,0:T(8,128)(2,1)S(1)}, u32[]{:S(2)}, u32[]{:S(2)}) collective-permute-start(bf16[4,128,1664]{2,1,0:T(8,128)(2,1)S(1)} %out_mate.1), channel_id=1, source_target_pairs={{0,1},{1,0},{2,3},{3,2},{4,5},{5,4},{6,7},{7,6},{8,9},{9,8},{10,11... | collective-permute-start | bytes 5111816 | tf_op jit(solution)/shard_map/ppermute | solution.py:49
  68.7 13.0 %collective-permute-start.14 = (bf16[128,1664]{1,0:T(8,128)(2,1)}, bf16[128,1664]{1,0:T(8,128)(2,1)S(1)}, u32[]{:S(2)}, u32[]{:S(2)}) collective-permute-start(bf16[128,1664]{1,0:T(8,128)(2,1)} %get-tuple-element.139), channel_id=1, source_target_pairs={{0,6},{1,7},{2,0},{3,1},{4,2},{5,3},{6,4},{7,5},{8,14},{9,15},{10,... | collective-permute-start | bytes 1277960 | tf_op jit(solution)/shard_map/ppermute | solution.py:49
  71.7 30.6 %all-to-all-start.1 = ((bf16[16,128,384]{2,1,0:T(8,128)(2,1)}), bf16[16,128,384]{2,1,0:T(8,128)(2,1)}, u32[]{:S(2)}, u32[]{:S(2)}) async-start(bf16[16,128,384]{2,1,0:T(8,128)(2,1)} %open.1), calls=%async_computation.1 | async-start | bytes 3145728 | tf_op jit(solution)/shard_map/all_to_all | solution.py:693
  78.2 24.1 %copy-start.15 = (pred[128,1024]{1,0:T(32,128)(4,1)}, pred[128,1024]{1,0:T(32,128)(4,1)S(1)}, u32[]{:S(2)}) copy-start(pred[128,1024]{1,0:T(32,128)(4,1)S(1)} %convolution_compare_fusion) | copy-start | bytes 393220
  78.2 12.9 %collective-permute-start.13 = (bf16[128,1664]{1,0:T(8,128)(2,1)S(1)}, bf16[128,1664]{1,0:T(8,128)(2,1)S(1)}, u32[]{:S(2)}, u32[]{:S(2)}) collective-permute-start(bf16[128,1664]{1,0:T(8,128)(2,1)S(1)} %get-tuple-element.138), channel_id=1, source_target_pairs={{0,2},{1,3},{2,4},{3,5},{4,6},{5,7},{6,0},{7,1},{8,10},{9,11},{10,... | collective-permute-start | bytes 1277960 | tf_op jit(solution)/shard_map/ppermute | solution.py:49
  81.8 9.8 %collective-permute-start.16 = (bf16[64,1664]{1,0:T(8,128)(2,1)S(1)}, bf16[64,1664]{1,0:T(8,128)(2,1)S(1)}, u32[]{:S(2)}, u32[]{:S(2)}) collective-permute-start(bf16[64,1664]{1,0:T(8,128)(2,1)S(1)} %add_convert_fusion), channel_id=1, source_target_pairs={{0,6},{1,7},{2,0},{3,1},{4,2},{5,3},{6,4},{7,5},{8,14},{9,15},{10,... | collective-permute-start | bytes 638984 | tf_op jit(solution)/shard_map/ppermute | solution.py:49
  91.2 7.6 %collective-permute-start.15 = (bf16[64,1664]{1,0:T(8,128)(2,1)S(1)}, bf16[64,1664]{1,0:T(8,128)(2,1)S(1)}, u32[]{:S(2)}, u32[]{:S(2)}) collective-permute-start(bf16[64,1664]{1,0:T(8,128)(2,1)S(1)} %add_convert_fusion.1), channel_id=1, source_target_pairs={{0,2},{1,3},{2,4},{3,5},{4,6},{5,7},{6,0},{7,1},{8,10},{9,11},{10,... | collective-permute-start | bytes 638984 | tf_op jit(solution)/shard_map/ppermute | solution.py:49
  102.3 46.7 %all-to-all-start = ((bf16[16,4,16,1536]{3,2,1,0:T(8,128)(2,1)}), bf16[16,4,16,1536]{3,2,1,0:T(8,128)(2,1)S(1)}, u32[]{:S(2)}, u32[]{:S(2)}) async-start(bf16[16,4,16,1536]{3,2,1,0:T(8,128)(2,1)} %bitcast.19), calls=%async_computation | async-start | bytes 6291456 | tf_op jit(solution)/shard_map/all_to_all | solution.py:707
  114.2 27.1 %collective-permute-start.17 = (bf16[384,1536]{1,0:T(8,128)(2,1)}, bf16[384,1536]{1,0:T(8,128)(2,1)}, u32[]{:S(2)}, u32[]{:S(2)}) collective-permute-start(bf16[384,1536]{1,0:T(8,128)(2,1)} %pad_maximum_fusion.w0), channel_id=1, source_target_pairs={{0,2},{1,3},{2,4},{3,5},{4,6},{5,7},{6,0},{7,1},{8,10},{9,11},{10,... | collective-permute-start | bytes 3538952 | tf_op jit(solution)/shard_map/ppermute | solution.py:49
  114.2 27.1 %collective-permute-start.18 = (bf16[384,1536]{1,0:T(8,128)(2,1)}, bf16[384,1536]{1,0:T(8,128)(2,1)}, u32[]{:S(2)}, u32[]{:S(2)}) collective-permute-start(bf16[384,1536]{1,0:T(8,128)(2,1)} %pad_maximum_fusion.w0), channel_id=1, source_target_pairs={{0,6},{1,7},{2,0},{3,1},{4,2},{5,3},{6,4},{7,5},{8,14},{9,15},{10,... | collective-permute-start | bytes 3538952 | tf_op jit(solution)/shard_map/ppermute | solution.py:49
  117.4 23.9 %collective-permute-start.19 = (bf16[384,1536]{1,0:T(8,128)(2,1)}, bf16[384,1536]{1,0:T(8,128)(2,1)}, u32[]{:S(2)}, u32[]{:S(2)}) collective-permute-start(bf16[384,1536]{1,0:T(8,128)(2,1)} %pad_maximum_fusion.w0), channel_id=1, source_target_pairs={{0,1},{1,0},{2,3},{3,2},{4,5},{5,4},{6,7},{7,6},{8,9},{9,8},{10,11... | collective-permute-start | bytes 3538952 | tf_op jit(solution)/shard_map/ppermute | solution.py:49
  162.5 42.4 %all-to-all-start.2 = ((bf16[16,4,16,1536]{3,2,1,0:T(8,128)(2,1)}), bf16[16,4,16,1536]{3,2,1,0:T(8,128)(2,1)S(1)}, u32[]{:S(2)}, u32[]{:S(2)}) async-start(bf16[16,4,16,1536]{3,2,1,0:T(8,128)(2,1)} %experts.1), calls=%async_computation.2 | async-start | bytes 6291456 | tf_op jit(solution)/shard_map/all_to_all | solution.py:738
  168.5 13.4 %copy-start.16 = (pred[128,1024]{1,0:T(32,128)(4,1)S(1)}, pred[128,1024]{1,0:T(32,128)(4,1)}, u32[]{:S(2)}) copy-start(pred[128,1024]{1,0:T(32,128)(4,1)} %copy-done.15) | copy-start | bytes 393220
  168.5 13.4 %copy-start.17 = (bf16[128,64]{0,1:T(8,128)(2,1)S(1)}, bf16[128,64]{0,1:T(8,128)(2,1)}, u32[]{:S(2)}) copy-start(bf16[128,64]{0,1:T(8,128)(2,1)} %get-tuple-element.160) | copy-start | bytes 49156
  168.5 12.6 %collective-permute-start.22 = (bf16[192,1536]{1,0:T(8,128)(2,1)S(1)}, bf16[192,1536]{1,0:T(8,128)(2,1)S(1)}, u32[]{:S(2)}, u32[]{:S(2)}) collective-permute-start(bf16[192,1536]{1,0:T(8,128)(2,1)S(1)} %slice.22), channel_id=1, source_target_pairs={{0,2},{1,3},{2,4},{3,5},{4,6},{5,7},{6,0},{7,1},{8,10},{9,11},{10,... | collective-permute-start | bytes 1769480 | tf_op jit(solution)/shard_map/ppermute | solution.py:49
  169.7 15.1 %copy-start.2 = (f32[128,1536]{1,0:T(8,128)S(1)}, f32[128,1536]{1,0:T(8,128)}, u32[]{:S(2)}) copy-start(f32[128,1536]{1,0:T(8,128)} %get-tuple-element.156.residual) | copy-start | bytes 2359300
  169.7 15.1 %copy-start.3 = (bf16[128,1536]{1,0:T(8,128)(2,1)S(1)}, bf16[128,1536]{1,0:T(8,128)(2,1)}, u32[]{:S(2)}) copy-start(bf16[128,1536]{1,0:T(8,128)(2,1)} %get-tuple-element.150.rows_ref) | copy-start | bytes 1179652
  169.7 12.1 %collective-permute-start.23 = (bf16[192,1536]{1,0:T(8,128)(2,1)S(1)}, bf16[192,1536]{1,0:T(8,128)(2,1)S(1)}, u32[]{:S(2)}, u32[]{:S(2)}) collective-permute-start(bf16[192,1536]{1,0:T(8,128)(2,1)S(1)} %slice.23), channel_id=1, source_target_pairs={{0,6},{1,7},{2,0},{3,1},{4,2},{5,3},{6,4},{7,5},{8,14},{9,15},{10,... | collective-permute-start | bytes 1769480 | tf_op jit(solution)/shard_map/ppermute | solution.py:49
  173.2 9.0 %collective-permute-start.20 = (bf16[384,1536]{1,0:T(8,128)(2,1)}, bf16[384,1536]{1,0:T(8,128)(2,1)S(1)}, u32[]{:S(2)}, u32[]{:S(2)}) collective-permute-start(bf16[384,1536]{1,0:T(8,128)(2,1)} %collective-permute-done.17.w2), channel_id=1, source_target_pairs={{0,1},{1,0},{2,3},{3,2},{4,5},{5,4},{6,7},{7,6},{8,9},{9,8},{10,11... | collective-permute-start | bytes 3538952 | tf_op jit(solution)/shard_map/ppermute | solution.py:49
  173.2 9.0 %collective-permute-start.21 = (bf16[384,1536]{1,0:T(8,128)(2,1)}, bf16[384,1536]{1,0:T(8,128)(2,1)S(1)}, u32[]{:S(2)}, u32[]{:S(2)}) collective-permute-start(bf16[384,1536]{1,0:T(8,128)(2,1)} %collective-permute-done.18.w4), channel_id=1, source_target_pairs={{0,1},{1,0},{2,3},{3,2},{4,5},{5,4},{6,7},{7,6},{8,9},{9,8},{10,11... | collective-permute-start | bytes 3538952 | tf_op jit(solution)/shard_map/ppermute | solution.py:49
  181.8 2.9 %collective-permute-start.24 = (bf16[384,1536]{1,0:T(8,128)(2,1)S(1)}, bf16[384,1536]{1,0:T(8,128)(2,1)S(1)}, u32[]{:S(2)}, u32[]{:S(2)}) collective-permute-start(bf16[384,1536]{1,0:T(8,128)(2,1)S(1)} %constant_dynamic-update-slice_fusion.w6), channel_id=1, source_target_pairs={{0,1},{1,0},{2,3},{3,2},{4,5},{5,4},{6,7},{7,6},{8,9},{9,8},{10,11... | collective-permute-start | bytes 3538952 | tf_op jit(solution)/shard_map/ppermute | solution.py:49

commit v3 on v2

--- a/solution.py
+++ b/solution.py
@@ -120,20 +120,12 @@
         meta[8 + c] = before
         meta[16 + c] = seg_at(base + (c * CHUNK + CHUNK - 1))
         meta[24 + c] = seg_at(base + c * CHUNK)
-    first = seg_at(base - 1)
-    open_req = jnp.maximum(first, 0)
-    open_end, open_slot, source = jnp.int32(0), jnp.int32(0), jnp.int32(0)
+    source = jnp.int32(0)
     for req in range(16):
         meta[32 + req] = ends[req] - 1 - base
         meta[48 + req] = slots[req]
-        open_end = jnp.where(open_req == req, ends[req] - 1 - base, open_end)
-        open_slot = jnp.where(open_req == req, slots[req], open_slot)
         source = jnp.where(slots[req] == seq[0], (ends[req] - 1) // (8 * CHUNK), source)
-    holds = (first >= 0) & (open_end >= 0) & (open_end < 8 * CHUNK)
-    meta[64] = open_slot
-    meta[65] = jnp.where(holds, 1, 0)
-    meta[66] = jnp.clip(open_end, 0, 8 * CHUNK - 1)
-    meta[67] = source
+    meta[64] = source
     for copy in copies:
         copy.wait()
 
@@ -200,18 +192,15 @@
 
 
 def conv_kernel(meta, conv_in, seg_ext, step, cum, w_conv, x_out, bc_out, fresh_out):
-    def chunk(c, carry):
-        start = pl.multiple_of(c * CHUNK, CHUNK)
+    for c in range(1, 8):
+        start = c * CHUNK
         rows = pl.ds(start, CHUNK)
         seg = seg_ext[pl.ds(start, CHUNK + 16), :]
-        prior = conv_in[pl.ds(pl.multiple_of(start - 16, 16), 16), :].astype(F32)
+        prior = conv_in[pl.ds(start - 16, 16), :].astype(F32)
         mixed = conv_chunk(prior, conv_in[rows, :].astype(F32), seg, w_conv)
         x_out[rows, :] = mixed[:, :WIDE]
         bc_out[rows, :] = mixed[:, WIDE:]
         fresh_out[c] = fresh_state(mixed, step[rows, :], cum[rows, :], seg[16:, :], meta[16 + c])
-        return carry
-
-    lax.fori_loop(1, 8, chunk, 0)
 
 
 def row_spread(row):
@@ -262,14 +251,6 @@
     return near[:STATE, :].astype(F32) + factor_of(near) * far[:STATE, :].astype(F32)
 
 
-def open_kernel(meta, near, far, cum, past, ends_in, ends_out):
-    at = meta[66]
-    total = cum[pl.ds(at, 1), :] + past[pl.ds(at // CHUNK, 1), :]
-    hold = row_spread(jnp.where(meta[65] > 0, jnp.exp(total), 0.0))
-    value = ends_in[0].astype(F32)
-    ends_out[0] = jnp.where(meta[65] > 0, value + hold * entering_state(near, far), value).astype(BF16)
-
-
 def local_kernel(meta, x_in, bc_in, cum_in, step_in, seg_ext, seg_row, state_in, skip, *rest, first, last):
     y_out = rest[-1]
     rows_i = lax.broadcasted_iota(jnp.int32, (CHUNK, CHUNK), 0)
@@ -278,7 +259,7 @@
     left = lax.broadcasted_iota(jnp.int32, (CHUNK, LANES), 1) < HALF
 
     def chunk(c):
-        start = pl.multiple_of(c * CHUNK, CHUNK)
+        start = c * CHUNK
         rows = pl.ds(start, CHUNK)
         x = x_in[rows, :].astype(F32)
         b_rows, c_rows = bc_in[rows, :STATE], bc_in[rows, STATE:]
@@ -304,15 +285,11 @@
                 acc = acc + jnp.dot(weights, value, preferred_element_type=F32)
             y_out[rows, pair * LANES : (pair + 1) * LANES] = acc
 
-    def two_chunks(i, carry):
-        chunk(first + 2 * i)
-        chunk(first + 2 * i + 1)
-        return carry
-
-    lax.fori_loop(0, (last - first) // 2, two_chunks, 0)
-
-
-def ends_kernel(meta, x_in, bc_in, cum_in, step_in, seg_ext, state_in, ends_out):
+    for c in range(first, last):
+        chunk(c)
+
+
+def ends_kernel(meta, x_in, bc_in, cum_in, step_in, seg_ext, state_in, near, far, past, ends_out):
     def close(req, carry):
         at = meta[32 + req]
 
@@ -329,7 +306,10 @@
                 bc_in[rows, :STATE], drive.astype(BF16), (((0,), (0,)), ((), ())), preferred_element_type=F32
             )
             hold = row_spread(jnp.where(req == meta[8 + c], jnp.exp(cum_end), 0.0))
-            ends_out[meta[48 + req]] = (fresh + hold * state_in[c].astype(F32)).astype(BF16)
+            since = cum_end + past[pl.ds(c, 1), :]
+            opened = row_spread(jnp.where(req == meta[0], jnp.exp(since), 0.0))
+            value = fresh + hold * state_in[c].astype(F32) + opened * entering_state(near, far)
+            ends_out[meta[48 + req]] = value.astype(BF16)
 
         return carry
 
@@ -401,20 +381,12 @@
     outgoing[...] = jnp.dot(spots[...], held[...], preferred_element_type=F32).astype(BF16)
 
 
-def expert_kernel(rows_ref, gate, up, down, out, total):
+def expert_kernel(rows_ref, gate, up, down, out):
     rows = rows_ref[:, pl.program_id(0)].reshape(256, 1536)
     g = jnp.dot(rows, gate[...], preferred_element_type=F32)
     u = jnp.dot(rows, up[...], preferred_element_type=F32)
     hidden = (silu(g) * u).astype(BF16)
-    term = jnp.dot(hidden, down[...], preferred_element_type=F32)
-
-    @pl.when(pl.program_id(1) == 0)
-    def _():
-        total[...] = term
-
-    @pl.when(pl.program_id(1) == 1)
-    def _():
-        out[...] = (total[...] + term).astype(BF16).reshape(16, CAP, 1536)
+    out[...] = jnp.dot(hidden, down[...], preferred_element_type=F32).astype(BF16).reshape(16, CAP, 1536)
 
 
 def shared_kernel(rows_ref, w0, w1, w2, w3, w4, w5, w6, w7, residual, out):
@@ -506,18 +478,22 @@
         name="tables",
     )(
         seq_idx.reshape(1).astype(jnp.int32),
-        lengths,
-        cache_slot,
-        dt_bias,
-        a_log,
-        d_skip,
-        in_dt.T,
-        conv_x,
-        conv_bc,
-        in_gain,
-        norm_gain,
-        post_gain,
-        *far_core(in_x, in_bc, in_z),
+        *far_core(
+            lengths,
+            cache_slot,
+            dt_bias,
+            a_log,
+            d_skip,
+            in_dt.T,
+            conv_x,
+            conv_bc,
+            in_gain,
+            norm_gain,
+            post_gain,
+            in_x,
+            in_bc,
+            in_z,
+        ),
     )
 
     picks = (routes[:, :, None] == jnp.arange(64, dtype=jnp.int32)).astype(F32)
@@ -666,26 +642,12 @@
     mate_part, states = lax.optimization_barrier((mate_part, states))
     ends_local = pl.pallas_call(
         ends_kernel,
-        out_shape=shape((16, STATE, WIDE), BF16),
-        in_specs=[SM] + [VM] * 6,
+        out_shape=hbm((16, STATE, WIDE), BF16),
+        in_specs=[SM] + [VM] * 9,
         out_specs=VM,
         compiler_params=limit(16),
         name="ends",
-    )(meta, *near_core(x_rows, bc_rows, cum, step, seg_ext, states))
-    slot_block = pl.BlockSpec((1, STATE, WIDE), lambda i, meta: (meta[64], 0, 0))
-    ends_local = pl.pallas_call(
-        open_kernel,
-        out_shape=shape((16, STATE, WIDE), BF16),
-        grid_spec=pltpu.PrefetchScalarGridSpec(
-            num_scalar_prefetch=1,
-            grid=(1,),
-            in_specs=[VM] * 4 + [slot_block],
-            out_specs=slot_block,
-        ),
-        input_output_aliases={5: 0},
-        compiler_params=limit(16),
-        name="open",
-    )(meta, *near_core(near, far, cum, past), ends_local)
+    )(meta, *near_core(x_rows, bc_rows, cum, step, seg_ext, states, near, far, past))
     send_a, send_b, kept_0, kept_1, kept_3 = project_out(False, swapped)
     send_a, send_b, ends_local = lax.optimization_barrier((send_a, send_b, ends_local))
     p_a = over_exp(send_a, PLUS)
@@ -710,7 +672,7 @@
     sh_gate, sh_up, sh_down, ends_all, outgoing = lax.optimization_barrier(
         (sh_gate, sh_up, sh_down, ends_all, outgoing)
     )
-    final = lax.dynamic_index_in_dim(ends_all, meta[67], 0, False).astype(F32)
+    final = lax.dynamic_index_in_dim(ends_all, meta[64], 0, False).astype(F32)
     state_cache = final.T.reshape(1, HEADS, HALF, STATE)
     packed = jnp.concatenate([sh_gate.T, sh_up.T, sh_down])
     half = packed.shape[0] // 2
@@ -723,15 +685,14 @@
     answers = pl.pallas_call(
         expert_kernel,
         out_shape=hbm((16, 4, CAP, width), BF16),
-        grid=(4, 2),
+        grid=(4,),
         in_specs=[
             VM,
-            pl.BlockSpec((None, width, 256), lambda e, f: (e, 0, f)),
-            pl.BlockSpec((None, width, 256), lambda e, f: (e, 0, f)),
-            pl.BlockSpec((None, 256, width), lambda e, f: (e, f, 0)),
+            pl.BlockSpec((None, width, 512), lambda e: (e, 0, 0)),
+            pl.BlockSpec((None, width, 512), lambda e: (e, 0, 0)),
+            pl.BlockSpec((None, 512, width), lambda e: (e, 0, 0)),
         ],
-        out_specs=pl.BlockSpec((16, None, CAP, width), lambda e, f: (0, e, 0, 0)),
-        scratch_shapes=[pltpu.VMEM((256, width), F32)],
+        out_specs=pl.BlockSpec((16, None, CAP, width), lambda e: (0, e, 0, 0)),
         compiler_params=limit(20),
         name="experts",
     )(*near_core(received), *far_core(ex_gate, ex_up, ex_down))

time: 209 us -> 201 us (0.962)
  local copies, waits for them, and re-layouts: 14.4 us -> 6.99 us
  Pallas kernels: 58.1 us -> 51.7 us
  waiting for transfers between devices: 70.5 us -> 75.2 us
    unnamed x41 -> x19, local copies, waits for them, and re-layouts: 7.55 us -> 0.08 us
    ppermute x21, waiting for transfers between devices: 49.3 us -> 53.8 us  [over_exp(): return lax.ppermute(block, 'exp', route)]
    pallas_call x1, Pallas kernels: 13.4 us -> 10.7 us  [body(): pl.pallas_call(expert_kernel, out_shape=hbm((16, 4, CAP, width), BF16), g...]
    pallas_call x2 -> x1, Pallas kernels: 4.39 us -> 2.23 us  [body(): pl.pallas_call(ends_kernel, out_shape=hbm((16, STATE, WIDE), BF16), in_sp...]
  transfers between devices with their start and end apart: 28 -> 28, of which waited for: 12 -> 15; matrix products, arithmetic and copies ran while one was open for 6% -> 6% of each run, Pallas kernels for 17% -> 15%
where the time goes in v3:
time: 201 us; the launch traced here: 200 us
  waiting for transfers between devices  75.2 us (37%)
  starting transfers between devices  58.5 us (29%)
  Pallas kernels  51.7 us (26%)
  local copies, waits for them, and re-layouts  6.99 us (3%)
  other arithmetic  3.97 us (2%)
  between operations  3.03 us (2%)
    ppermute x21, waiting for transfers between devices, over_exp(): return lax.ppermute(block, 'exp', route)  53.8 us
    ppermute x21, starting transfers between devices, over_exp(): return lax.ppermute(block, 'exp', route)  21.5 us
    ppermute x4, starting transfers between devices, ahead(): lax.ppermute(block, 'seq', [(i, i + distance) for i in range(16 - distanc...  18.3 us
    all_to_all x1, waiting for transfers between devices, body(): lax.all_to_all(answers, 'seq', split_axis=0, concat_axis=0, tiled=True)  13.8 us
    pallas_call x1, Pallas kernels, body(): pl.pallas_call(expert_kernel, out_shape=hbm((16, 4, CAP, width), BF16), g...  10.7 us
    pallas_call x3, Pallas kernels, project(): pl.pallas_call(functools.partial(project_kernel, plan=plan), out_shape=(v...  7.69 us
    all_to_all x1, waiting for transfers between devices, body(): lax.all_to_all(outgoing.reshape(16, 4, CAP, width), 'seq', split_axis=0,...  7.52 us
    all_to_all x1, starting transfers between devices, body(): lax.all_to_all(outgoing.reshape(16, 4, CAP, width), 'seq', split_axis=0,...  6.76 us
  transfers between devices with their start and end apart: 28, of which 15 were waited for; matrix products, arithmetic and copies ran while one was open for 6% of the time, Pallas kernels for 15%

profile of v3, /device:TPU:0, one launch (start us, length us, event | category | flops | bytes accessed | tf_op | source)
XLA Modules:
  0.0 200.1 jit_solution(6599896575692305678)
XLA Ops:
  0.7 1.8 collective-permute-start
  2.5 1.5 collective-permute-start.1
  4.0 3.4 %tables.1 = (bf16[1536,1024]{1,0:T(8,128)(2,1)S(1)}, bf16[128,1536]{1,0:T(8,128)(2,1)S(1)}, f32[1,128]{1,0:T(1,128)S(1)}, f32[1,128]{1,0:T(1,128)S(1)}, f32[1,38...) custom-call(s32[1]{0:T(128)} %bitcast.1.seq, ...), custom_call_target="tpu_custom_call" | custom-call | tf_op jit(solution)/shard_map/tables/pallas_call | solution.py:458
  7.4 2.0 project.3
  9.4 4.4 %collective-permute-done.up = bf16[128,1536]{1,0:T(8,128)(2,1)S(1)} collective-permute-done((bf16[128,1536]{1,0:T(8,128)(2,1)}, bf16[128,1536]{1,0:T(8,128)(2,1)S(1)}, u32[]{:S(2)}, u32[]{:S(2)}) %collective-permute-start) | collective-permute-done | bytes 393248 | tf_op jit(solution)/shard_map/ppermute | solution.py:49
  14.0 1.6 collective-permute-start.3
  15.7 1.7 collective-permute-start.4
  17.3 3.8 %project.4 = (bf16[1024,640]{1,0:T(8,128)(2,1)S(1)}, f32[1024,128]{1,0:T(8,128)S(1)}, f32[1024,128]{1,0:T(8,128)S(1)}, f32[1024,384]{1,0:T(8,128)S(1)}) custom-call(s32[1]{0:T(128)} %bitcast.where, bf16[256,1536]{1,0:T(8,128)(2,1)S(1)} %get-tuple-element.94.refs_0_, ...), custom_call_target="tpu_custom_call", output_to_operand_aliasing={{0}: (8, {}), {1}: (9, {}), {2}: (10, {}), {3}: (11, {})} | custom-call | tf_op jit(solution)/shard_map/project/pallas_call | solution.py:514
  21.1 1.4 collective-permute-done.3.refs_0_
  23.1 0.9 collective-permute-done.6.refs_2_
  24.4 2.0 project.5
  26.3 4.0 %collective-permute-start.8 = (bf16[16,640]{1,0:T(8,128)(2,1)S(1)}, bf16[16,640]{1,0:T(8,128)(2,1)S(1)}, u32[]{:S(2)}, u32[]{:S(2)}) collective-permute-start(bf16[16,640]{1,0:T(8,128)(2,1)S(1)} %slice.18), channel_id=1, source_target_pairs={{0,8},{8,16},{16,24},{24,32},{32,40},{40,48},{48,56},{56,64},{64,7... | collective-permute-start | bytes 61448 | tf_op jit(solution)/shard_map/ppermute | solution.py:45
  30.4 3.4 %conv.1 = (bf16[1024,384]{1,0:T(8,128)(2,1)S(1)}, bf16[1024,256]{1,0:T(8,128)(2,1)S(1)}, f32[8,128,384]{2,1,0:T(8,128)S(1)}) custom-call(s32[80]{0:T(128)S(1)} %get-tuple-element.80.meta, bf16[1024,640]{1,0:T(8,128)(2,1)S(1)} %get-tuple-element.109.conv_in, s32[1040,1]{1,0:T(8,128)S(1)} %get-tuple-element.110.seg_ext, ...), custom_call_target="tpu_custom_call" | custom-call | tf_op jit(solution)/shard_map/conv/pallas_call | solution.py:563
  33.8 1.2 chain.1
  34.9 3.8 %collective-permute-start.9 = (bf16[144,384]{1,0:T(8,128)(2,1)S(1)}, bf16[144,384]{1,0:T(8,128)(2,1)S(1)}, u32[]{:S(2)}, u32[]{:S(2)}) collective-permute-start(bf16[144,384]{1,0:T(8,128)(2,1)S(1)} %get-tuple-element.117.sent), channel_id=1, source_target_pairs={{0,8},{8,16},{16,24},{24,32},{32,40},{40,48},{48,56},{56,64},{64,7... | collective-permute-start | bytes 331784 | tf_op jit(solution)/shard_map/ppermute | solution.py:45
  38.8 2.9 %local.2.rest_0_ = f32[1024,384]{1,0:T(8,128)S(1)} custom-call(s32[80]{0:T(128)S(1)} %get-tuple-element.80.meta, bf16[1024,384]{1,0:T(8,128)(2,1)S(1)} %get-tuple-element.118.x_in, bf16[1024,256]{1,0:T(8,128)(2,1)S(1)} %get-tuple-element.119.bc_in, f32[1024,128]{1,0:T(8,128)S(1)} %get-tuple-element.112.cum.cum_in, ...), custom_call_target="tpu_custom_call" | custom-call | tf_op jit(solution)/shard_map/local/pallas_call | solution.py:592
  41.8 4.0 %collective-permute-start.10 = (bf16[144,384]{1,0:T(8,128)(2,1)S(1)}, bf16[144,384]{1,0:T(8,128)(2,1)S(1)}, u32[]{:S(2)}, u32[]{:S(2)}) collective-permute-start(bf16[144,384]{1,0:T(8,128)(2,1)S(1)} %pair.1), channel_id=1, source_target_pairs={{0,8},{8,16},{16,24},{24,32},{32,40},{40,48},{48,56},{56,64},{64,7... | collective-permute-start | bytes 331784 | tf_op jit(solution)/shard_map/ppermute | solution.py:45
  45.8 6.5 %collective-permute-start.11 = (bf16[144,384]{1,0:T(8,128)(2,1)S(1)}, bf16[144,384]{1,0:T(8,128)(2,1)S(1)}, u32[]{:S(2)}, u32[]{:S(2)}) collective-permute-start(bf16[144,384]{1,0:T(8,128)(2,1)S(1)} %pair.1), channel_id=1, source_target_pairs={{0,24},{8,32},{16,40},{24,48},{32,56},{40,64},{48,72},{56,80},{64,... | collective-permute-start | bytes 331784 | tf_op jit(solution)/shard_map/ppermute | solution.py:45
  52.3 2.9 %local.3.y_in = f32[1024,384]{1,0:T(8,128)S(1)} custom-call(s32[80]{0:T(128)S(1)} %get-tuple-element.80.meta, bf16[1024,384]{1,0:T(8,128)(2,1)S(1)} %get-tuple-element.118.x_in, bf16[1024,256]{1,0:T(8,128)(2,1)S(1)} %get-tuple-element.119.bc_in, f32[1024,128]{1,0:T(8,128)S(1)} %get-tuple-element.112.cum.cum_in, ...), custom_call_target="tpu_custom_call", output_to_operand_aliasing={{}: (9, {})} | custom-call | tf_op jit(solution)/shard_map/local/pallas_call | solution.py:592
  55.2 1.9 out_mate.1
  57.9 2.2 %ends.1 = bf16[16,128,384]{2,1,0:T(8,128)(2,1)} custom-call(s32[80]{0:T(128)S(1)} %get-tuple-element.80.meta, bf16[1024,384]{1,0:T(8,128)(2,1)S(1)} %get-tuple-element.118.x_in, bf16[1024,256]{1,0:T(8,128)(2,1)S(1)} %get-tuple-element.119.bc_in, f32[1024,128]{1,0:T(8,128)S(1)} %get-tuple-element.112.cum.cum_in, ...), custom_call_target="tpu_custom_call" | custom-call | tf_op jit(solution)/shard_map/ends/pallas_call | solution.py:643
  60.9 2.7 %out_own.1 = (bf16[128,1664]{1,0:T(8,128)(2,1)S(1)}, bf16[128,1664]{1,0:T(8,128)(2,1)}, bf16[128,1664]{1,0:T(8,128)(2,1)S(1)}, bf16[64,1664]{1,0:T(8,128)(2,1)S(1)}, bf16[64,1664]{1,0:T(8,128)(2,1)S(1)}) custom-call(s32[1]{0:T(128)} %bitcast.where, s32[80]{0:T(128)S(1)} %get-tuple-element.80.meta, f32[1024,384]{1,0:T(8,128)S(1)} %local.3.y_in, ...), custom_call_target="tpu_custom_call" | custom-call | tf_op jit(solution)/shard_map/out_own/pallas_call | solution.py:625
  63.5 2.9 %collective-permute-start.14 = (bf16[128,1664]{1,0:T(8,128)(2,1)}, bf16[128,1664]{1,0:T(8,128)(2,1)S(1)}, u32[]{:S(2)}, u32[]{:S(2)}) collective-permute-start(bf16[128,1664]{1,0:T(8,128)(2,1)} %get-tuple-element.139), channel_id=1, source_target_pairs={{0,6},{1,7},{2,0},{3,1},{4,2},{5,3},{6,4},{7,5},{8,14},{9,15},{10,... | collective-permute-start | bytes 1277960 | tf_op jit(solution)/shard_map/ppermute | solution.py:49
  66.4 6.7 %all-to-all-start.1 = ((bf16[16,128,384]{2,1,0:T(8,128)(2,1)}), bf16[16,128,384]{2,1,0:T(8,128)(2,1)}, u32[]{:S(2)}, u32[]{:S(2)}) async-start(bf16[16,128,384]{2,1,0:T(8,128)(2,1)} %ends.1), calls=%async_computation.1 | async-start | bytes 3145728 | tf_op jit(solution)/shard_map/all_to_all | solution.py:655
  73.9 2.2 %collective-permute-done.14.p_b = bf16[128,1664]{1,0:T(8,128)(2,1)S(1)} collective-permute-done((bf16[128,1664]{1,0:T(8,128)(2,1)}, bf16[128,1664]{1,0:T(8,128)(2,1)S(1)}, u32[]{:S(2)}, u32[]{:S(2)}) %collective-permute-start.14) | collective-permute-done | bytes 426016 | tf_op jit(solution)/shard_map/ppermute | solution.py:49
  76.2 3.7 %collective-permute-start.16 = (bf16[64,1664]{1,0:T(8,128)(2,1)S(1)}, bf16[64,1664]{1,0:T(8,128)(2,1)S(1)}, u32[]{:S(2)}, u32[]{:S(2)}) collective-permute-start(bf16[64,1664]{1,0:T(8,128)(2,1)S(1)} %add_convert_fusion), channel_id=1, source_target_pairs={{0,6},{1,7},{2,0},{3,1},{4,2},{5,3},{6,4},{7,5},{8,14},{9,15},{10,... | collective-permute-start | bytes 638984 | tf_op jit(solution)/shard_map/ppermute | solution.py:49
  79.8 6.6 %collective-permute-done.13.p_a = bf16[128,1664]{1,0:T(8,128)(2,1)S(1)} collective-permute-done((bf16[128,1664]{1,0:T(8,128)(2,1)S(1)}, bf16[128,1664]{1,0:T(8,128)(2,1)S(1)}, u32[]{:S(2)}, u32[]{:S(2)}) %collective-permute-start.13) | collective-permute-done | bytes 426016 | tf_op jit(solution)/shard_map/ppermute | solution.py:49
  86.8 6.9 %collective-permute-done.15.q_a = bf16[64,1664]{1,0:T(8,128)(2,1)S(1)} collective-permute-done((bf16[64,1664]{1,0:T(8,128)(2,1)S(1)}, bf16[64,1664]{1,0:T(8,128)(2,1)S(1)}, u32[]{:S(2)}, u32[]{:S(2)}) %collective-permute-start.15) | collective-permute-done | bytes 213024 | tf_op jit(solution)/shard_map/ppermute | solution.py:49
  93.7 3.5 %enter.1 = (f32[128,1536]{1,0:T(8,128)}, bf16[128,1536]{1,0:T(8,128)(2,1)}, bf16[1024,1536]{1,0:T(8,128)(2,1)}) custom-call(bf16[128,1664]{1,0:T(8,128)(2,1)S(1)} %get-tuple-element.133.h0, bf16[128,1664]{1,0:T(8,128)(2,1)S(1)} %collective-permute-done.13.p_a, bf16[128,1664]{1,0:T(8,128)(2,1)S(1)} %collective-permute-done.14.p_b, ...), custom_call_target="tpu_custom_call" | custom-call | tf_op jit(solution)/shard_map/enter/pallas_call | solution.py:659
  97.2 6.8 %all-to-all-start = ((bf16[16,4,16,1536]{3,2,1,0:T(8,128)(2,1)}), bf16[16,4,16,1536]{3,2,1,0:T(8,128)(2,1)S(1)}, u32[]{:S(2)}, u32[]{:S(2)}) async-start(bf16[16,4,16,1536]{3,2,1,0:T(8,128)(2,1)} %bitcast.18), calls=%async_computation | async-start | bytes 6291456 | tf_op jit(solution)/shard_map/all_to_all | solution.py:669
  104.0 1.2 copy.50
  105.2 1.9 copy.51
  107.1 2.2 %pad_maximum_fusion.w0 = bf16[384,1536]{1,0:T(8,128)(2,1)} fusion(bf16[128,1536]{1,0:T(8,128)(2,1)} %param.40, bf16[128,1536]{1,0:T(8,128)(2,1)} %bitcast.20, bf16[128,1536]{1,0:T(8,128)(2,1)S(1)} %bitcast.19), kind=kLoop, calls=%fused_computation.3 | loop fusion | flops 3538944 | bytes 2359296 | tf_op jit(solution)/shard_map/concatenate | solution.py:677
  109.4 3.2 %collective-permute-start.18 = (bf16[384,1536]{1,0:T(8,128)(2,1)}, bf16[384,1536]{1,0:T(8,128)(2,1)}, u32[]{:S(2)}, u32[]{:S(2)}) collective-permute-start(bf16[384,1536]{1,0:T(8,128)(2,1)} %pad_maximum_fusion.w0), channel_id=1, source_target_pairs={{0,6},{1,7},{2,0},{3,1},{4,2},{5,3},{6,4},{7,5},{8,14},{9,15},{10,... | collective-permute-start | bytes 3538952 | tf_op jit(solution)/shard_map/ppermute | solution.py:49
  115.1 0.9 convert_bitcast_fusion.1
  116.0 0.8 copy.52
  116.8 19.4 %collective-permute-done.17.w2 = bf16[384,1536]{1,0:T(8,128)(2,1)} collective-permute-done((bf16[384,1536]{1,0:T(8,128)(2,1)}, bf16[384,1536]{1,0:T(8,128)(2,1)}, u32[]{:S(2)}, u32[]{:S(2)}) %collective-permute-start.17) | collective-permute-done | bytes 1179680 | tf_op jit(solution)/shard_map/ppermute | solution.py:49
  136.3 7.5 %all-to-all-done.rows_ref = bf16[16,4,16,1536]{3,2,1,0:T(8,128)(2,1)S(1)} async-done(((bf16[16,4,16,1536]{3,2,1,0:T(8,128)(2,1)}), bf16[16,4,16,1536]{3,2,1,0:T(8,128)(2,1)S(1)}, u32[]{:S(2)}, u32[]{:S(2)}) %all-to-all-start) | async-done | bytes 3145760 | tf_op jit(solution)/shard_map/all_to_all | solution.py:669
  143.8 10.7 %experts.1 = bf16[16,4,16,1536]{3,2,1,0:T(8,128)(2,1)} custom-call(bf16[16,4,16,1536]{3,2,1,0:T(8,128)(2,1)S(1)} %all-to-all-done.rows_ref, bf16[4,1536,512]{2,1,0:T(8,128)(2,1)} %gate.1, bf16[4,1536,512]{2,1,0:T(8,128)(2,1)} %up.1, bf16[4,512,1536]{2,1,0:T(8,128)(2,1)} %down.1), custom_call_target="tpu_custom_call" | custom-call | tf_op jit(solution)/shard_map/experts/pallas_call | solution.py:685
  154.5 5.3 %all-to-all-start.2 = ((bf16[16,4,16,1536]{3,2,1,0:T(8,128)(2,1)}), bf16[16,4,16,1536]{3,2,1,0:T(8,128)(2,1)S(1)}, u32[]{:S(2)}, u32[]{:S(2)}) async-start(bf16[16,4,16,1536]{3,2,1,0:T(8,128)(2,1)} %experts.1), calls=%async_computation.2 | async-start | bytes 6291456 | tf_op jit(solution)/shard_map/all_to_all | solution.py:699
  159.7 1.1 slice.22
  161.0 1.1 slice.23
  162.1 3.3 %collective-permute-start.23 = (bf16[192,1536]{1,0:T(8,128)(2,1)S(1)}, bf16[192,1536]{1,0:T(8,128)(2,1)S(1)}, u32[]{:S(2)}, u32[]{:S(2)}) collective-permute-start(bf16[192,1536]{1,0:T(8,128)(2,1)S(1)} %slice.23), channel_id=1, source_target_pairs={{0,6},{1,7},{2,0},{3,1},{4,2},{5,3},{6,4},{7,5},{8,14},{9,15},{10,... | collective-permute-start | bytes 1769480 | tf_op jit(solution)/shard_map/ppermute | solution.py:49
  165.9 7.8 %collective-permute-done.22 = bf16[192,1536]{1,0:T(8,128)(2,1)S(1)} collective-permute-done((bf16[192,1536]{1,0:T(8,128)(2,1)S(1)}, bf16[192,1536]{1,0:T(8,128)(2,1)S(1)}, u32[]{:S(2)}, u32[]{:S(2)}) %collective-permute-start.22) | collective-permute-done | bytes 589856 | tf_op jit(solution)/shard_map/ppermute | solution.py:49
  174.6 2.5 %collective-permute-done.24.w7 = bf16[384,1536]{1,0:T(8,128)(2,1)S(1)} collective-permute-done((bf16[384,1536]{1,0:T(8,128)(2,1)S(1)}, bf16[384,1536]{1,0:T(8,128)(2,1)S(1)}, u32[]{:S(2)}, u32[]{:S(2)}) %collective-permute-start.24) | collective-permute-done | bytes 1179680 | tf_op jit(solution)/shard_map/ppermute | solution.py:49
  177.1 6.6 %shared.1.base = f32[128,1536]{1,0:T(8,128)} custom-call(bf16[128,1536]{1,0:T(8,128)(2,1)S(1)} %copy-done.3, bf16[384,1536]{1,0:T(8,128)(2,1)} %pad_maximum_fusion.w0, bf16[384,1536]{1,0:T(8,128)(2,1)} %collective-permute-done.19.w1, bf16[384,1536]{1,0:T(8,128)(2,1)} %collective-permute-done.17.w2, bf16[384,1536]{1,0:T(8,128)(2,1)S(1)} %collective-permute-done.20.w3, ...), custom_call_target="tpu_custom_call" | custom-call | tf_op jit(solution)/shard_map/shared/pallas_call | solution.py:703
  183.8 13.8 %all-to-all-done.2 = bf16[16,4,16,1536]{3,2,1,0:T(8,128)(2,1)S(1)} async-done(((bf16[16,4,16,1536]{3,2,1,0:T(8,128)(2,1)}), bf16[16,4,16,1536]{3,2,1,0:T(8,128)(2,1)S(1)}, u32[]{:S(2)}, u32[]{:S(2)}) %all-to-all-start.2) | async-done | bytes 3145760 | tf_op jit(solution)/shard_map/all_to_all | solution.py:699
  197.6 2.5 %leave.1 = bf16[128,1536]{1,0:T(8,128)(2,1)} custom-call(bf16[1024,1536]{1,0:T(8,128)(2,1)S(1)} %bitcast.17, bf16[128,1024]{1,0:T(8,128)(2,1)S(1)} %fusion.mix, f32[128,1536]{1,0:T(8,128)} %shared.1.base), custom_call_target="tpu_custom_call" | custom-call | tf_op jit(solution)/shard_map/leave/pallas_call | solution.py:711
  (63 shorter events, 5.8 us)
Async XLA Ops:
  0.6 6.8 %collective-permute-start.2 = (bf16[128,1536]{1,0:T(8,128)(2,1)}, bf16[128,1536]{1,0:T(8,128)(2,1)S(1)}, u32[]{:S(2)}, u32[]{:S(2)}) collective-permute-start(bf16[128,1536]{1,0:T(8,128)(2,1)} %tokens.1), channel_id=1, source_target_pairs={{0,1},{1,0},{2,3},{3,2},{4,5},{5,4},{6,7},{7,6},{8,9},{9,8},{10,11... | collective-permute-start | bytes 1179656 | tf_op jit(solution)/shard_map/ppermute | solution.py:49
  0.7 13.1 %collective-permute-start = (bf16[128,1536]{1,0:T(8,128)(2,1)}, bf16[128,1536]{1,0:T(8,128)(2,1)S(1)}, u32[]{:S(2)}, u32[]{:S(2)}) collective-permute-start(bf16[128,1536]{1,0:T(8,128)(2,1)} %tokens.1), channel_id=1, source_target_pairs={{0,2},{1,3},{2,4},{3,5},{4,6},{5,7},{6,0},{7,1},{8,10},{9,11},{10,... | collective-permute-start | bytes 1179656 | tf_op jit(solution)/shard_map/ppermute | solution.py:49
  2.5 11.4 %collective-permute-start.1 = (bf16[128,1536]{1,0:T(8,128)(2,1)}, bf16[128,1536]{1,0:T(8,128)(2,1)S(1)}, u32[]{:S(2)}, u32[]{:S(2)}) collective-permute-start(bf16[128,1536]{1,0:T(8,128)(2,1)} %tokens.1), channel_id=1, source_target_pairs={{0,6},{1,7},{2,0},{3,1},{4,2},{5,3},{6,4},{7,5},{8,14},{9,15},{10,... | collective-permute-start | bytes 1179656 | tf_op jit(solution)/shard_map/ppermute | solution.py:49
  4.0 3.4 %copy-start.1 = (bf16[128,1536]{1,0:T(8,128)(2,1)S(1)}, bf16[128,1536]{1,0:T(8,128)(2,1)}, u32[]{:S(2)}) copy-start(bf16[128,1536]{1,0:T(8,128)(2,1)} %tokens.1) | copy-start | bytes 1179652
  13.9 3.4 %collective-permute-start.5 = (bf16[256,1536]{1,0:T(8,128)(2,1)S(1)}, bf16[256,1536]{1,0:T(8,128)(2,1)S(1)}, u32[]{:S(2)}, u32[]{:S(2)}) collective-permute-start(bf16[256,1536]{1,0:T(8,128)(2,1)S(1)} %get-tuple-element.94.refs_0_), channel_id=1, source_target_pairs={{0,1},{1,0},{2,3},{3,2},{4,5},{5,4},{6,7},{7,6},{8,9},{9,8},{10,11... | collective-permute-start | bytes 2359304 | tf_op jit(solution)/shard_map/ppermute | solution.py:49
  14.0 8.5 %collective-permute-start.3 = (bf16[64,1536]{1,0:T(8,128)(2,1)S(1)}, bf16[64,1536]{1,0:T(8,128)(2,1)S(1)}, u32[]{:S(2)}, u32[]{:S(2)}) collective-permute-start(bf16[64,1536]{1,0:T(8,128)(2,1)S(1)} %get-tuple-element.92), channel_id=1, source_target_pairs={{0,2},{1,3},{2,4},{3,5},{4,6},{5,7},{6,0},{7,1},{8,10},{9,11},{10,... | collective-permute-start | bytes 589832 | tf_op jit(solution)/shard_map/ppermute | solution.py:49
  15.7 7.0 %collective-permute-start.4 = (bf16[64,1536]{1,0:T(8,128)(2,1)S(1)}, bf16[64,1536]{1,0:T(8,128)(2,1)S(1)}, u32[]{:S(2)}, u32[]{:S(2)}) collective-permute-start(bf16[64,1536]{1,0:T(8,128)(2,1)S(1)} %get-tuple-element.93), channel_id=1, source_target_pairs={{0,6},{1,7},{2,0},{3,1},{4,2},{5,3},{6,4},{7,5},{8,14},{9,15},{10,... | collective-permute-start | bytes 589832 | tf_op jit(solution)/shard_map/ppermute | solution.py:49
  22.6 1.4 collective-permute-start.6
  22.6 1.7 collective-permute-start.7
  26.3 7.4 %collective-permute-start.8 = (bf16[16,640]{1,0:T(8,128)(2,1)S(1)}, bf16[16,640]{1,0:T(8,128)(2,1)S(1)}, u32[]{:S(2)}, u32[]{:S(2)}) collective-permute-start(bf16[16,640]{1,0:T(8,128)(2,1)S(1)} %slice.18), channel_id=1, source_target_pairs={{0,8},{8,16},{16,24},{24,32},{32,40},{40,48},{48,56},{56,64},{64,7... | collective-permute-start | bytes 61448 | tf_op jit(solution)/shard_map/ppermute | solution.py:45
  34.9 6.8 %collective-permute-start.9 = (bf16[144,384]{1,0:T(8,128)(2,1)S(1)}, bf16[144,384]{1,0:T(8,128)(2,1)S(1)}, u32[]{:S(2)}, u32[]{:S(2)}) collective-permute-start(bf16[144,384]{1,0:T(8,128)(2,1)S(1)} %get-tuple-element.117.sent), channel_id=1, source_target_pairs={{0,8},{8,16},{16,24},{24,32},{32,40},{40,48},{48,56},{56,64},{64,7... | collective-permute-start | bytes 331784 | tf_op jit(solution)/shard_map/ppermute | solution.py:45
  41.8 13.4 %copy-start = (bf16[384,1536]{1,0:T(8,128)(2,1)S(1)}, bf16[384,1536]{1,0:T(8,128)(2,1)}, u32[]{:S(2)}) copy-start(bf16[384,1536]{1,0:T(8,128)(2,1)} %w_out.3) | copy-start | bytes 3538948
  41.8 13.4 %collective-permute-start.10 = (bf16[144,384]{1,0:T(8,128)(2,1)S(1)}, bf16[144,384]{1,0:T(8,128)(2,1)S(1)}, u32[]{:S(2)}, u32[]{:S(2)}) collective-permute-start(bf16[144,384]{1,0:T(8,128)(2,1)S(1)} %pair.1), channel_id=1, source_target_pairs={{0,8},{8,16},{16,24},{24,32},{32,40},{40,48},{48,56},{56,64},{64,7... | collective-permute-start | bytes 331784 | tf_op jit(solution)/shard_map/ppermute | solution.py:45
  45.8 9.4 %collective-permute-start.11 = (bf16[144,384]{1,0:T(8,128)(2,1)S(1)}, bf16[144,384]{1,0:T(8,128)(2,1)S(1)}, u32[]{:S(2)}, u32[]{:S(2)}) collective-permute-start(bf16[144,384]{1,0:T(8,128)(2,1)S(1)} %pair.1), channel_id=1, source_target_pairs={{0,24},{8,32},{16,40},{24,48},{32,56},{40,64},{48,72},{56,80},{64,... | collective-permute-start | bytes 331784 | tf_op jit(solution)/shard_map/ppermute | solution.py:45
  55.2 2.0 %copy-start.7 = (f32[128,6]{0,1:T(8,128)S(1)}, f32[128,6]{0,1:T(8,128)}, u32[]{:S(2)}) copy-start(f32[128,6]{0,1:T(8,128)} %param.45) | copy-start | bytes 9220
  55.2 2.0 %copy-start.8 = (s32[128,6]{0,1:T(8,128)S(1)}, s32[128,6]{0,1:T(8,128)}, u32[]{:S(2)}) copy-start(s32[128,6]{0,1:T(8,128)} %param.44) | copy-start | bytes 9220
  57.2 3.7 %collective-permute-start.12 = (bf16[4,128,1664]{2,1,0:T(8,128)(2,1)S(1)}, bf16[4,128,1664]{2,1,0:T(8,128)(2,1)S(1)}, u32[]{:S(2)}, u32[]{:S(2)}) collective-permute-start(bf16[4,128,1664]{2,1,0:T(8,128)(2,1)S(1)} %out_mate.1), channel_id=1, source_target_pairs={{0,1},{1,0},{2,3},{3,2},{4,5},{5,4},{6,7},{7,6},{8,9},{9,8},{10,11... | collective-permute-start | bytes 5111816 | tf_op jit(solution)/shard_map/ppermute | solution.py:49
  63.5 12.6 %collective-permute-start.14 = (bf16[128,1664]{1,0:T(8,128)(2,1)}, bf16[128,1664]{1,0:T(8,128)(2,1)S(1)}, u32[]{:S(2)}, u32[]{:S(2)}) collective-permute-start(bf16[128,1664]{1,0:T(8,128)(2,1)} %get-tuple-element.139), channel_id=1, source_target_pairs={{0,6},{1,7},{2,0},{3,1},{4,2},{5,3},{6,4},{7,5},{8,14},{9,15},{10,... | collective-permute-start | bytes 1277960 | tf_op jit(solution)/shard_map/ppermute | solution.py:49
  66.4 30.8 %all-to-all-start.1 = ((bf16[16,128,384]{2,1,0:T(8,128)(2,1)}), bf16[16,128,384]{2,1,0:T(8,128)(2,1)}, u32[]{:S(2)}, u32[]{:S(2)}) async-start(bf16[16,128,384]{2,1,0:T(8,128)(2,1)} %ends.1), calls=%async_computation.1 | async-start | bytes 3145728 | tf_op jit(solution)/shard_map/all_to_all | solution.py:655
  73.6 23.6 %copy-start.4 = (pred[128,1024]{1,0:T(32,128)(4,1)}, pred[128,1024]{1,0:T(32,128)(4,1)S(1)}, u32[]{:S(2)}) copy-start(pred[128,1024]{1,0:T(32,128)(4,1)S(1)} %convolution_compare_fusion) | copy-start | bytes 393220
  73.6 12.8 %collective-permute-start.13 = (bf16[128,1664]{1,0:T(8,128)(2,1)S(1)}, bf16[128,1664]{1,0:T(8,128)(2,1)S(1)}, u32[]{:S(2)}, u32[]{:S(2)}) collective-permute-start(bf16[128,1664]{1,0:T(8,128)(2,1)S(1)} %get-tuple-element.138), channel_id=1, source_target_pairs={{0,2},{1,3},{2,4},{3,5},{4,6},{5,7},{6,0},{7,1},{8,10},{9,11},{10,... | collective-permute-start | bytes 1277960 | tf_op jit(solution)/shard_map/ppermute | solution.py:49
  76.2 10.6 %collective-permute-start.16 = (bf16[64,1664]{1,0:T(8,128)(2,1)S(1)}, bf16[64,1664]{1,0:T(8,128)(2,1)S(1)}, u32[]{:S(2)}, u32[]{:S(2)}) collective-permute-start(bf16[64,1664]{1,0:T(8,128)(2,1)S(1)} %add_convert_fusion), channel_id=1, source_target_pairs={{0,6},{1,7},{2,0},{3,1},{4,2},{5,3},{6,4},{7,5},{8,14},{9,15},{10,... | collective-permute-start | bytes 638984 | tf_op jit(solution)/shard_map/ppermute | solution.py:49
  86.4 7.3 %collective-permute-start.15 = (bf16[64,1664]{1,0:T(8,128)(2,1)S(1)}, bf16[64,1664]{1,0:T(8,128)(2,1)S(1)}, u32[]{:S(2)}, u32[]{:S(2)}) collective-permute-start(bf16[64,1664]{1,0:T(8,128)(2,1)S(1)} %add_convert_fusion.1), channel_id=1, source_target_pairs={{0,2},{1,3},{2,4},{3,5},{4,6},{5,7},{6,0},{7,1},{8,10},{9,11},{10,... | collective-permute-start | bytes 638984 | tf_op jit(solution)/shard_map/ppermute | solution.py:49
  97.2 46.6 %all-to-all-start = ((bf16[16,4,16,1536]{3,2,1,0:T(8,128)(2,1)}), bf16[16,4,16,1536]{3,2,1,0:T(8,128)(2,1)S(1)}, u32[]{:S(2)}, u32[]{:S(2)}) async-start(bf16[16,4,16,1536]{3,2,1,0:T(8,128)(2,1)} %bitcast.18), calls=%async_computation | async-start | bytes 6291456 | tf_op jit(solution)/shard_map/all_to_all | solution.py:669
  109.4 26.9 %collective-permute-start.17 = (bf16[384,1536]{1,0:T(8,128)(2,1)}, bf16[384,1536]{1,0:T(8,128)(2,1)}, u32[]{:S(2)}, u32[]{:S(2)}) collective-permute-start(bf16[384,1536]{1,0:T(8,128)(2,1)} %pad_maximum_fusion.w0), channel_id=1, source_target_pairs={{0,2},{1,3},{2,4},{3,5},{4,6},{5,7},{6,0},{7,1},{8,10},{9,11},{10,... | collective-permute-start | bytes 3538952 | tf_op jit(solution)/shard_map/ppermute | solution.py:49
  109.4 26.9 %collective-permute-start.18 = (bf16[384,1536]{1,0:T(8,128)(2,1)}, bf16[384,1536]{1,0:T(8,128)(2,1)}, u32[]{:S(2)}, u32[]{:S(2)}) collective-permute-start(bf16[384,1536]{1,0:T(8,128)(2,1)} %pad_maximum_fusion.w0), channel_id=1, source_target_pairs={{0,6},{1,7},{2,0},{3,1},{4,2},{5,3},{6,4},{7,5},{8,14},{9,15},{10,... | collective-permute-start | bytes 3538952 | tf_op jit(solution)/shard_map/ppermute | solution.py:49
  112.6 23.7 %collective-permute-start.19 = (bf16[384,1536]{1,0:T(8,128)(2,1)}, bf16[384,1536]{1,0:T(8,128)(2,1)}, u32[]{:S(2)}, u32[]{:S(2)}) collective-permute-start(bf16[384,1536]{1,0:T(8,128)(2,1)} %pad_maximum_fusion.w0), channel_id=1, source_target_pairs={{0,1},{1,0},{2,3},{3,2},{4,5},{5,4},{6,7},{7,6},{8,9},{9,8},{10,11... | collective-permute-start | bytes 3538952 | tf_op jit(solution)/shard_map/ppermute | solution.py:49
  154.5 43.1 %all-to-all-start.2 = ((bf16[16,4,16,1536]{3,2,1,0:T(8,128)(2,1)}), bf16[16,4,16,1536]{3,2,1,0:T(8,128)(2,1)S(1)}, u32[]{:S(2)}, u32[]{:S(2)}) async-start(bf16[16,4,16,1536]{3,2,1,0:T(8,128)(2,1)} %experts.1), calls=%async_computation.2 | async-start | bytes 6291456 | tf_op jit(solution)/shard_map/all_to_all | solution.py:699
  160.8 13.4 %copy-start.5 = (pred[128,1024]{1,0:T(32,128)(4,1)S(1)}, pred[128,1024]{1,0:T(32,128)(4,1)}, u32[]{:S(2)}) copy-start(pred[128,1024]{1,0:T(32,128)(4,1)} %copy-done.4) | copy-start | bytes 393220
  160.9 13.4 %copy-start.6 = (bf16[128,64]{0,1:T(8,128)(2,1)S(1)}, bf16[128,64]{0,1:T(8,128)(2,1)}, u32[]{:S(2)}) copy-start(bf16[128,64]{0,1:T(8,128)(2,1)} %get-tuple-element.160) | copy-start | bytes 49156
  160.9 12.8 %collective-permute-start.22 = (bf16[192,1536]{1,0:T(8,128)(2,1)S(1)}, bf16[192,1536]{1,0:T(8,128)(2,1)S(1)}, u32[]{:S(2)}, u32[]{:S(2)}) collective-permute-start(bf16[192,1536]{1,0:T(8,128)(2,1)S(1)} %slice.22), channel_id=1, source_target_pairs={{0,2},{1,3},{2,4},{3,5},{4,6},{5,7},{6,0},{7,1},{8,10},{9,11},{10,... | collective-permute-start | bytes 1769480 | tf_op jit(solution)/shard_map/ppermute | solution.py:49
  162.1 15.1 %copy-start.2 = (f32[128,1536]{1,0:T(8,128)S(1)}, f32[128,1536]{1,0:T(8,128)}, u32[]{:S(2)}) copy-start(f32[128,1536]{1,0:T(8,128)} %get-tuple-element.156.residual) | copy-start | bytes 2359300
  162.1 15.0 %copy-start.3 = (bf16[128,1536]{1,0:T(8,128)(2,1)S(1)}, bf16[128,1536]{1,0:T(8,128)(2,1)}, u32[]{:S(2)}) copy-start(bf16[128,1536]{1,0:T(8,128)(2,1)} %get-tuple-element.150.rows_ref) | copy-start | bytes 1179652
  162.1 12.1 %collective-permute-start.23 = (bf16[192,1536]{1,0:T(8,128)(2,1)S(1)}, bf16[192,1536]{1,0:T(8,128)(2,1)S(1)}, u32[]{:S(2)}, u32[]{:S(2)}) collective-permute-start(bf16[192,1536]{1,0:T(8,128)(2,1)S(1)} %slice.23), channel_id=1, source_target_pairs={{0,6},{1,7},{2,0},{3,1},{4,2},{5,3},{6,4},{7,5},{8,14},{9,15},{10,... | collective-permute-start | bytes 1769480 | tf_op jit(solution)/shard_map/ppermute | solution.py:49
  165.4 9.2 %collective-permute-start.20 = (bf16[384,1536]{1,0:T(8,128)(2,1)}, bf16[384,1536]{1,0:T(8,128)(2,1)S(1)}, u32[]{:S(2)}, u32[]{:S(2)}) collective-permute-start(bf16[384,1536]{1,0:T(8,128)(2,1)} %collective-permute-done.17.w2), channel_id=1, source_target_pairs={{0,1},{1,0},{2,3},{3,2},{4,5},{5,4},{6,7},{7,6},{8,9},{9,8},{10,11... | collective-permute-start | bytes 3538952 | tf_op jit(solution)/shard_map/ppermute | solution.py:49
  165.4 9.2 %collective-permute-start.21 = (bf16[384,1536]{1,0:T(8,128)(2,1)}, bf16[384,1536]{1,0:T(8,128)(2,1)S(1)}, u32[]{:S(2)}, u32[]{:S(2)}) collective-permute-start(bf16[384,1536]{1,0:T(8,128)(2,1)} %collective-permute-done.18.w4), channel_id=1, source_target_pairs={{0,1},{1,0},{2,3},{3,2},{4,5},{5,4},{6,7},{7,6},{8,9},{9,8},{10,11... | collective-permute-start | bytes 3538952 | tf_op jit(solution)/shard_map/ppermute | solution.py:49
  174.2 2.9 %collective-permute-start.24 = (bf16[384,1536]{1,0:T(8,128)(2,1)S(1)}, bf16[384,1536]{1,0:T(8,128)(2,1)S(1)}, u32[]{:S(2)}, u32[]{:S(2)}) collective-permute-start(bf16[384,1536]{1,0:T(8,128)(2,1)S(1)} %constant_dynamic-update-slice_fusion.w6), channel_id=1, source_target_pairs={{0,1},{1,0},{2,3},{3,2},{4,5},{5,4},{6,7},{7,6},{8,9},{9,8},{10,11... | collective-permute-start | bytes 3538952 | tf_op jit(solution)/shard_map/ppermute | solution.py:49
